TPU v7x, 32 devices: a whole 2x2x4 slice. The times are simulated.
32 devices in a mesh: px: 4 (over x, core), py: 8 (over z, y).
Axes of the slice: x: 2, y: 2, z: 4, core: 2. Of those that a mesh axis runs over, the one named last changes fastest.
Arguments:
- horiz_div: float32 [128, 1024, 1024], P('py', 'px'), may hold values from -6 to 6
- w_star: float32 [128, 1024, 1024], P('py', 'px'), may hold values from -6 to 6
- air_temp: bfloat16 [128, 1024, 1024], P('py', 'px'), may hold values from -6 to 6
- roof_level: int32 [1024, 1024], P('px'), may hold values from 0 to 63
- facet_cells: int32 [32, 1024], P(('px', 'py')), may hold values from -1 to 4194303, as said below
- facet_temp: float32 [32, 1024], P(('px', 'py')), may hold values from -6 to 6
- net_radiation: float32 [32, 1024], P(('px', 'py')), may hold values from -6 to 6
- heat_capacity: float32 [32, 1024], P(('px', 'py')), may hold values from 1 to 4
- drag_coef: float32 [32, 1024], P(('px', 'py')), may hold values from 0.05 to 0.5
- heat_coef: float32 [32, 1024], P(('px', 'py')), may hold values from 0.05 to 0.5
Outputs:
- w_new: float32 [128, 1024, 1024], P('py', 'px')
- theta_new: bfloat16 [128, 1024, 1024], P('py', 'px')
- facet_temp_new: float32 [32, 1024], P(('px', 'py'))
Inputs may be any that keep to these rules, and one draw needn't show every extreme that they name: `facet_cells`: in each block of 32 rows the non-empty rows come first. For every device one owner's block is full, the same owner for all devices.
All inputs are finite; a program needn't handle non-finite values.
Results may differ from a plain program's by a relative error of at most 0.001.
Values sent between devices are 32-bit elements; how exact they have to be, the bound alone decides.
A program may use at most 320 MiB of HBM per device.

v0:
```python
import math

import jax
import jax.numpy as jnp
from jax import lax
from jax.experimental import pallas as pl
from jax.experimental.pallas import tpu as pltpu
from jax.sharding import PartitionSpec as P


def fourier_table(size):
    positions = jnp.arange(size, dtype=jnp.int32)
    half_size = size // 2
    wave_num = jnp.where(positions <= half_size, positions, positions - half_size)
    phases = positions[:, None] * wave_num[None, :] % size
    angles = 2.0 * math.pi / size * phases.astype(jnp.float32)
    norm_edge = 1.0 / math.sqrt(size)
    norm_mid = math.sqrt(2.0 / size)
    columns = positions[None, :]
    basis = jnp.where(
        columns == 0,
        norm_edge,
        jnp.where(
            columns < half_size,
            norm_mid * jnp.cos(angles),
            jnp.where(
                columns == half_size, norm_edge * jnp.cos(angles), norm_mid * jnp.sin(angles)
            ),
        ),
    )
    eigenvalue = 2.0 * jnp.cos(2.0 * math.pi / size * wave_num.astype(jnp.float32)) - 2.0
    return (basis, eigenvalue)


def edge_kernel(field_ref, diag_ref, low_ref, high_ref, out_ref):
    levels = field_ref.shape[0]
    diag = diag_ref[...]
    pivot = 1.0 / low_ref[...]
    value = field_ref[0] * pivot
    for level in range(1, levels):
        pivot = 1.0 / ((high_ref[...] if level == levels - 1 else diag) - pivot)
        value = (field_ref[level] - value) * pivot
    out_ref[0, 1] = value
    pivot = 1.0 / high_ref[...]
    value = field_ref[levels - 1] * pivot
    for level in range(levels - 2, -1, -1):
        pivot = 1.0 / ((low_ref[...] if level == 0 else diag) - pivot)
        value = (field_ref[level] - value) * pivot
    out_ref[0, 0] = value


def join_kernel(levels, edge_ref, diag_ref, out_ref):
    blocks = edge_ref.shape[0]
    diag = diag_ref[...]
    near = 1.0 / diag
    far = near
    beta = 1.0 / (diag + 1.0)
    top = 1.0 / (diag - 1.0)
    for _ in range(1, levels):
        near = 1.0 / (diag - near)
        far = -far * near
        beta = 1.0 / (diag - beta)
        top = 1.0 / (diag - top)
    alpha = edge_ref[0, 1]
    alphas, betas, heads, slopes = [alpha], [beta], [None], [None]
    for block in range(1, blocks - 1):
        scale = 1.0 / (1.0 - near * beta)
        head = (edge_ref[block, 0] - near * alpha) * scale
        slope = far * scale
        alpha = edge_ref[block, 1] - far * alpha + far * beta * head
        beta = near + far * beta * slope
        alphas.append(alpha)
        betas.append(beta)
        heads.append(head)
        slopes.append(slope)
    above = jnp.zeros_like(diag)
    first = (edge_ref[blocks - 1, 0] - top * alpha) / (1.0 - top * beta)
    for block in range(blocks - 1, 0, -1):
        if block < blocks - 1:
            first = heads[block] - slopes[block] * above
        out_ref[block, 0] = alphas[block - 1] - betas[block - 1] * first
        out_ref[block, 1] = above
        above = first
    out_ref[0, 0] = jnp.zeros_like(diag)
    out_ref[0, 1] = above


def solve_kernel(field_ref, diag_ref, low_ref, high_ref, ends_ref, out_ref, pivots):
    levels = field_ref.shape[0]
    diag = diag_ref[...]
    below = ends_ref[0, 0]
    pivot = 1.0 / low_ref[...]
    value = (field_ref[0] - below) * pivot
    pivots[0] = pivot
    out_ref[0] = value
    for level in range(1, levels):
        pivot = 1.0 / ((high_ref[...] if level == levels - 1 else diag) - pivot)
        source = field_ref[level]
        if level == levels - 1:
            source = source - ends_ref[0, 1]
        value = (source - value) * pivot
        pivots[level] = pivot
        out_ref[level] = value
    for level in range(levels - 2, -1, -1):
        lower = out_ref[level] - pivots[level] * value
        out_ref[level + 1] = value - lower
        value = lower
    out_ref[0] = jnp.where(low_ref[...] == diag, value - below, 0.0)


def solve_columns(field, diag, py_count):
    levels, ky_count, kx_width = field.shape
    ky_width = ky_count // py_count
    rows = math.gcd(32, ky_width)
    per_owner = ky_width // rows
    mine = lax.axis_index("py")
    low = diag + jnp.where(mine == 0, 1.0, 0.0)
    high = diag - jnp.where(mine == py_count - 1, 1.0, 0.0)
    tall = pl.BlockSpec((levels, rows, kx_width), lambda i: (0, i, 0))
    flat = pl.BlockSpec((rows, kx_width), lambda i: (i, 0))
    ends = pl.BlockSpec(
        (1, 2, rows, kx_width), lambda i: (i // per_owner, 0, i % per_owner, 0)
    )
    edge_shape = jax.ShapeDtypeStruct((py_count, 2, ky_width, kx_width), jnp.float32)
    edges = pl.pallas_call(
        edge_kernel,
        out_shape=edge_shape,
        grid=(ky_count // rows,),
        in_specs=[tall, flat, flat, flat],
        out_specs=ends,
    )(field, diag, low, high)
    edges = lax.all_to_all(edges, "py", split_axis=0, concat_axis=0, tiled=True)
    join = pl.BlockSpec((py_count, 2, 8, kx_width), lambda i: (0, 0, i, 0))
    own_diag = lax.dynamic_slice_in_dim(diag, mine * ky_width, ky_width)
    joined = pl.pallas_call(
        lambda *refs: join_kernel(levels, *refs),
        out_shape=edge_shape,
        grid=(ky_width // 8,),
        in_specs=[join, pl.BlockSpec((8, kx_width), lambda i: (i, 0))],
        out_specs=join,
    )(edges, own_diag)
    joined = lax.all_to_all(joined, "py", split_axis=0, concat_axis=0, tiled=True)
    return pl.pallas_call(
        solve_kernel,
        out_shape=jax.ShapeDtypeStruct(field.shape, jnp.float32),
        grid=(ky_count // rows,),
        in_specs=[tall, flat, flat, flat, ends],
        out_specs=tall,
        scratch_shapes=[pltpu.VMEM((levels, rows, kx_width), jnp.float32)],
    )(field, diag, low, high, joined)


def body(
    horiz_div,
    w_star,
    air_temp,
    roof_level,
    facet_cells,
    facet_temp,
    net_radiation,
    heat_capacity,
    drag_coef,
    heat_coef,
):
    level_count, row_count, x_cells = w_star.shape
    px_count = lax.axis_size("px")
    py_count = lax.axis_size("py")
    cell_ids = facet_cells[0]
    is_live = cell_ids >= 0
    safe_ids = jnp.maximum(cell_ids, 0)
    w_flat = w_star.reshape(-1)
    temp_flat = air_temp.reshape(-1).astype(jnp.float32)
    sampled = jnp.stack(
        [jnp.where(is_live, w_flat[safe_ids], 0.0), jnp.where(is_live, temp_flat[safe_ids], 0.0)]
    )
    arrived = lax.all_to_all(sampled, ("px", "py"), split_axis=1, concat_axis=1, tiled=True)
    w_cell = arrived[0]
    temp_cell = arrived[1]
    speeds = jnp.sqrt(w_cell * w_cell + 0.25)
    stress = drag_coef[0] * speeds * w_cell
    heat_flux = heat_coef[0] * speeds * (facet_temp[0] - temp_cell)
    new_temp = (
        facet_temp[0] + (net_radiation[0] - heat_flux - 0.5 * facet_temp[0]) / heat_capacity[0]
    )
    outgoing_flux = jnp.stack([stress, heat_flux])
    returned = lax.all_to_all(outgoing_flux, ("px", "py"), split_axis=1, concat_axis=1, tiled=True)
    momentum_sink = jnp.where(is_live, returned[0], 0.0)
    warmed = jnp.where(is_live, returned[1], 0.0)
    w_corr = w_flat.at[safe_ids].add(-momentum_sink).reshape(w_star.shape)
    theta_new = temp_flat.at[safe_ids].add(warmed).astype(jnp.bfloat16).reshape(air_temp.shape)
    basis_x, eigen_x = fourier_table(x_cells)
    y_cells = row_count * px_count
    basis_y, eigen_y = fourier_table(y_cells)
    high = lax.Precision.HIGH
    from_above = lax.ppermute(w_corr[:1], "py", [(j, j - 1) for j in range(1, py_count)])
    w_shifted = jnp.concatenate([w_corr[1:], from_above], axis=0)
    source = horiz_div + w_shifted - w_corr
    modes_x = jnp.einsum("zyx,xk->zyk", source, basis_x, precision=high)
    modes_x = lax.all_to_all(modes_x, "px", split_axis=2, concat_axis=1, tiled=True)
    modes_xy = jnp.einsum("zyk,ym->zmk", modes_x, basis_y, precision=high)
    kx_width = x_cells // px_count
    eigen_xl = lax.dynamic_slice_in_dim(eigen_x, lax.axis_index("px") * kx_width, kx_width)
    diag = eigen_y[:, None] + eigen_xl[None, :] - 2.0
    outgoing = solve_columns(modes_xy, diag, py_count)
    spectral_y = jnp.einsum("zmk,ym->zyk", outgoing, basis_y, precision=high)
    spectral_y = lax.all_to_all(spectral_y, "px", split_axis=1, concat_axis=2, tiled=True)
    physical = jnp.einsum("zyk,xk->zyx", spectral_y, basis_x, precision=high)
    level_ids = lax.axis_index("py") * level_count + jnp.arange(level_count, dtype=jnp.int32)
    inside_solid = level_ids[:, None, None] < roof_level[None, :, :]
    w_new = jnp.where(inside_solid, 0.0, w_corr - physical)
    return (w_new, theta_new, new_temp[None])


def solution(mesh):
    placed = (
        P("py", "px", None),
        P("py", "px", None),
        P("py", "px", None),
        P("px", None),
        P(("px", "py"), None),
        P(("px", "py"), None),
        P(("px", "py"), None),
        P(("px", "py"), None),
        P(("px", "py"), None),
        P(("px", "py"), None),
    )
    return jax.shard_map(
        body,
        mesh=mesh,
        in_specs=placed,
        out_specs=(P("py", "px", None), P("py", "px", None), P(("px", "py"), None)),
        check_vma=False,
    )
```

profile of v0, /device:TPU:0, one launch (start us, length us, event | category | flops | bytes accessed | tf_op | source)
XLA Modules:
  0.0 1021.6 jit_solution(11158688381479883112)
XLA Ops:
  0.6 0.7 broadcast_maximum_fusion
  1.3 14.2 %copy.26 = f32[512,8,8,128]{3,1,2,0:T(8,128)} copy(f32[512,8,8,128]{3,2,1,0:T(8,128)} %bitcast.57) | data formatting | bytes 33554432
  15.5 11.3 %convert_element_type.34 = f32[16,256,1024]{2,1,0:T(8,128)} convert(bf16[16,256,1024]{2,1,0:T(8,128)(2,1)} %param.12) | non-fusion elementwise | flops 4194304 | bytes 25165824 | tf_op jit(solution)/shard_map/convert_element_type | solution.py:172
  26.8 14.1 %copy.27 = f32[512,8,8,128]{3,1,2,0:T(8,128)} copy(f32[512,8,8,128]{3,2,1,0:T(8,128)} %bitcast.56) | data formatting | bytes 33554432
  40.9 22.3 %gather_fusion = f32[1024]{0:T(1024)S(1)} fusion(f32[4194304]{0:T(1024)} %bitcast.51, s32[1024]{0:T(1024)S(1)} %broadcast_clamp_fusion), kind=kCustom, calls=%fused_computation | custom fusion | bytes 12288 | tf_op jit(solution)/shard_map/gather | solution.py:174
  63.3 22.1 %gather_fusion.1 = f32[1024]{0:T(1024)S(1)} fusion(f32[4194304]{0:T(1024)} %bitcast.53, s32[1024]{0:T(1024)S(1)} %broadcast_clamp_fusion), kind=kCustom, calls=%fused_computation.1 | custom fusion | bytes 12288 | tf_op jit(solution)/shard_map/gather | solution.py:174
  85.7 18.5 %all_to_all.58 = f32[2,32,32]{2,0,1:T(2,128)S(1)} all-to-all(f32[2,32,32]{2,0,1:T(2,128)S(1)} %pad_maximum_fusion), channel_id=1, replica_groups=mesh['px'=4,'py'=8] {'px','py'}, dimensions={1} | all-to-all | bytes 16384 | tf_op jit(solution)/shard_map/all_to_all | solution.py:176
  104.4 0.6 divide_add_fusion
  105.0 0.5 broadcast.219
  105.6 0.7 reduce.33
  106.4 0.7 pad_maximum_fusion.1
  107.1 2.6 all-to-all-start.1
  109.7 7.2 all-to-all-done.1
  117.1 0.6 broadcast_select_fusion
  117.7 17.8 %scatter_fusion = f32[4194304]{0:T(1024)} fusion(f32[4194304]{0:T(1024)} %bitcast.52, s32[1024]{0:T(1024)S(1)} %bitcast.60, f32[1024]{0:T(1024)S(1)} %get-tuple-element.16), kind=kCustom, calls=%fused_computation.2 | custom fusion | flops 1024 | bytes 16384 | tf_op jit(solution)/shard_map/scatter-add | solution.py:189
  135.4 1.3 slice.66
  136.9 1.3 collective-permute-start
  138.2 10.9 %slice.65 = f32[3932160]{0:T(1024)} slice(f32[4194304]{0:T(1024)} %scatter_fusion), slice={[262144:4194304]} | slice | bytes 31457280 | tf_op jit(solution)/shard_map/slice | solution.py:196
  149.1 18.0 %reshape.124 = f32[16,256,1024]{2,1,0:T(8,128)} reshape(f32[4194304]{0:T(1024)} %scatter_fusion) | data formatting | bytes 33554432 | tf_op jit(solution)/shard_map/reshape | solution.py:189
  167.1 17.7 %slice.54 = f32[15,256,1024]{2,1,0:T(8,128)} reshape(f32[3932160]{0:T(1024)} %slice.65) | data formatting | bytes 31457280 | tf_op jit(solution)/shard_map/slice | solution.py:196
  184.8 23.4 %fusion.61 = f32[16,256,1024]{2,1,0:T(8,128)} fusion(f32[16,256,1024]{2,1,0:T(8,128)} %reshape.124, f32[16,256,1024]{2,1,0:T(8,128)} %param.10, f32[1,256,1024]{2,1,0:T(8,128)S(1)} %collective-permute-done, f32[15,256,1024]{2,1,0:T(8,128)} %slice.54), kind=kLoop, calls=%fused_computation.5.clone.clone.2 | loop fusion | flops 12582912 | bytes 67108864 | tf_op jit(solution)/shard_map/zyx,xk->zyk/dot_general | solution.py:198
  208.2 51.3 %fusion.1 = f32[16,256,1024]{2,1,0:T(8,128)} fusion(s32[1024]{0:T(1024)S(1)} %compare_select_fusion, pred[1024]{0:T(1024)(128)(4,1)S(1)} %get-tuple-element.17, pred[1024]{0:T(1024)(128)(4,1)S(1)} %get-tuple-element.18, pred[1024]{0:T(1024)(128)(4,1)S(1)} %iota_compare_fusion.2, f32[16,256,1024]{2,1,0:T(8,128)} %fusion.61), kind=kOutput, calls=%fused_computation.6 | convolution fusion | flops 25790775296 | bytes 33561600 | tf_op jit(solution)/shard_map/zyx,xk->zyk/dot_general | solution.py:198
  259.5 17.5 %copy.19 = f32[16,256,1024]{1,0,2:T(8,128)} copy(f32[16,256,1024]{2,1,0:T(8,128)} %fusion.1) | data formatting | bytes 33554432 | tf_op jit(solution)/shard_map/zyx,xk->zyk/dot_general | solution.py:198
  277.0 7.5 all-to-all-start.2
  284.6 2.0 fusion.15
  286.6 18.3 %fusion.65 = f32[1024,1024,1]{1,0,2:T(8,128)} fusion(pred[1024]{0:T(1024)(128)(4,1)S(1)} %get-tuple-element.17, s32[1024]{0:T(1024)S(1)} %compare_select_fusion, pred[1024]{0:T(1024)(128)(4,1)S(1)} %get-tuple-element.18, pred[1024]{0:T(1024)(128)(4,1)S(1)} %iota_compare_fusion.2), kind=kLoop, calls=%fused_computation.19.clone.1 | loop fusion | flops 20971520 | bytes 4201472 | tf_op jit(solution)/shard_map/zyk,ym->zmk/dot_general | solution.py:200
  304.9 162.6 %all-to-all-done.2 = f32[16,256,1024]{1,0,2:T(8,128)} async-done(((f32[16,256,1024]{1,0,2:T(8,128)}), f32[16,256,1024]{1,0,2:T(8,128)}, u32[]{:S(2)}, u32[]{:S(2)}) %all-to-all-start.2) | async-done | bytes 16777248 | tf_op jit(solution)/shard_map/all_to_all | solution.py:199
  467.5 19.2 %copy.20 = f32[16,256,4,256]{3,1,2,0:T(8,128)} copy(f32[16,256,4,256]{1,0,3,2:T(8,128)} %bitcast.5) | data formatting | bytes 33554432 | tf_op jit(solution)/shard_map/all_to_all | solution.py:199
  486.8 33.1 %convolution_bitcast_fusion.1.field_ref = f32[16,1024,256]{2,1,0:T(8,128)} fusion(f32[16,1024,256]{2,1,0:T(8,128)} %bitcast.58, f32[1024,1024,1]{1,0,2:T(8,128)} %fusion.65), kind=kOutput, calls=%fused_computation.12 | convolution fusion | flops 25769803776 | bytes 37748736 | tf_op jit(solution)/shard_map/zyk,ym->zmk/dot_general | solution.py:200
  519.9 22.8 %shard_map.121 = f32[8,2,128,256]{3,2,1,0:T(8,128)} custom-call(f32[16,1024,256]{2,1,0:T(8,128)} %convolution_bitcast_fusion.1.field_ref, f32[1024,256]{1,0:T(8,128)} %get-tuple-element.13.diag_ref, f32[1024,256]{1,0:T(8,128)} %get-tuple-element.12.low_ref, f32[1024,256]{1,0:T(8,128)} %get-tuple-element.11.high_ref), custom_call_target="tpu_custom_call" | custom-call | tf_op jit(solution)/shard_map/pallas_call | solution.py:125
  542.7 4.1 all-to-all-start.3
  546.8 1.6 constant_dynamic-slice_fusion.refs_1_
  548.4 46.5 %all-to-all-done.3.refs_0_ = f32[8,2,128,256]{3,2,1,0:T(8,128)S(1)} async-done(((f32[8,2,128,256]{3,2,1,0:T(8,128)}), f32[8,2,128,256]{3,2,1,0:T(8,128)S(1)}, u32[]{:S(2)}, u32[]{:S(2)}) %all-to-all-start.3) | async-done | bytes 2097184 | tf_op jit(solution)/shard_map/all_to_all | solution.py:132
  594.9 1.3 copy-done
  596.2 10.7 %shard_map.122 = f32[8,2,128,256]{3,2,1,0:T(8,128)} custom-call(f32[8,2,128,256]{3,2,1,0:T(8,128)} %copy-done, f32[128,256]{1,0:T(8,128)} %constant_dynamic-slice_fusion.refs_1_), custom_call_target="tpu_custom_call" | custom-call | tf_op jit(solution)/shard_map/pallas_call | solution.py:135
  606.9 52.2 %all_to_all.59.ends_ref = f32[8,2,128,256]{3,2,1,0:T(8,128)} all-to-all(f32[8,2,128,256]{3,2,1,0:T(8,128)} %shard_map.122), channel_id=1, replica_groups=mesh['px'=4,'py'=8] {'py'}, dimensions={0} | all-to-all | bytes 4194304 | tf_op jit(solution)/shard_map/all_to_all | solution.py:142
  659.1 24.9 %shard_map.123 = f32[16,1024,256]{2,1,0:T(8,128)} custom-call(f32[16,1024,256]{2,1,0:T(8,128)} %convolution_bitcast_fusion.1.field_ref, f32[1024,256]{1,0:T(8,128)} %get-tuple-element.13.diag_ref, f32[1024,256]{1,0:T(8,128)} %get-tuple-element.12.low_ref, f32[1024,256]{1,0:T(8,128)} %get-tuple-element.11.high_ref, f32[8,2,128,256]{3,2,1,0:T(8,128)} %all_to_all.59.ends_ref), custom_call_target="tpu_custom_call" | custom-call | tf_op jit(solution)/shard_map/pallas_call | solution.py:143
  684.0 53.8 %convolution_bitcast_fusion = f32[16,1024,256]{2,1,0:T(8,128)} fusion(f32[16,1024,256]{2,1,0:T(8,128)} %shard_map.123, s32[1024]{0:T(1024)S(1)} %compare_select_fusion, pred[1024]{0:T(1024)(128)(4,1)S(1)} %get-tuple-element.17, pred[1024]{0:T(1024)(128)(4,1)S(1)} %get-tuple-element.18, pred[1024]{0:T(1024)(128)(4,1)S(1)} %iota_compare_fusion.2), kind=kOutput, calls=%fused_computation.11 | convolution fusion | flops 25790775296 | bytes 33561600 | tf_op jit(solution)/shard_map/zmk,ym->zyk/dot_general | solution.py:205
  737.8 17.8 %copy.22 = f32[16,1024,256]{2,0,1:T(8,128)} copy(f32[16,1024,256]{2,1,0:T(8,128)} %convolution_bitcast_fusion) | data formatting | bytes 33554432 | tf_op jit(solution)/shard_map/zmk,ym->zyk/transpose | solution.py:205
  755.5 7.1 all-to-all-start.5
  762.7 18.4 %fusion.63 = f32[1024,1024,1]{1,0,2:T(8,128)} fusion(pred[1024]{0:T(1024)(128)(4,1)S(1)} %get-tuple-element.17, s32[1024]{0:T(1024)S(1)} %compare_select_fusion, pred[1024]{0:T(1024)(128)(4,1)S(1)} %get-tuple-element.18, pred[1024]{0:T(1024)(128)(4,1)S(1)} %iota_compare_fusion.2), kind=kLoop, calls=%fused_computation.20.clone.1 | loop fusion | flops 20971520 | bytes 4201472 | tf_op jit(solution)/shard_map/zyk,xk->zyx/dot_general | solution.py:207
  781.0 17.3 %scatter_fusion.1 = f32[4194304]{0:T(1024)} fusion(f32[4194304]{0:T(1024)} %bitcast.54, s32[1024]{0:T(1024)S(1)} %bitcast.61, f32[1024]{0:T(1024)S(1)} %copy-done.4), kind=kCustom, calls=%fused_computation.3 | custom fusion | flops 1024 | bytes 16384 | tf_op jit(solution)/shard_map/scatter-add | solution.py:190
  798.4 9.0 convert_element_type.33
  807.4 13.3 %reshape.125 = bf16[16,256,1024]{2,1,0:T(8,128)(2,1)} reshape(bf16[4194304]{0:T(1024)(128)(2,1)} %convert_element_type.33) | data formatting | bytes 16777216 | tf_op jit(solution)/shard_map/reshape | solution.py:190
  820.6 125.1 %all-to-all-done.5 = f32[16,1024,256]{2,0,1:T(8,128)} async-done(((f32[16,1024,256]{2,0,1:T(8,128)}), f32[16,1024,256]{2,0,1:T(8,128)}, u32[]{:S(2)}, u32[]{:S(2)}) %all-to-all-start.5) | async-done | bytes 16777248 | tf_op jit(solution)/shard_map/all_to_all | solution.py:206
  945.7 21.1 %copy.29 = f32[16,4,256,256]{3,1,2,0:T(4,128)} copy(f32[16,4,256,256]{3,0,2,1:T(8,128)} %bitcast.10) | data formatting | bytes 33554432 | tf_op jit(solution)/shard_map/all_to_all | solution.py:206
  966.8 20.8 %all_to_all.51 = f32[16,256,1024]{2,1,0:T(8,128)} reshape(f32[16,256,4,256]{3,2,1,0:T(4,128)} %bitcast.55) | data formatting | bytes 33554432 | tf_op jit(solution)/shard_map/all_to_all | solution.py:206
  987.5 33.9 %subtract_select_fusion = f32[16,256,1024]{2,1,0:T(8,128)} fusion(f32[16,256,1024]{2,1,0:T(8,128)} %reshape.124, f32[16,256,1024]{2,1,0:T(8,128)} %all_to_all.51, s32[256,1024]{1,0:T(8,128)S(1)} %copy-done.10, s32[16]{0:T(128)S(1)} %iota_add_fusion, f32[1024,1024,1]{1,0,2:T(8,128)} %fusion.63), kind=kOutput, calls=%fused_computation.10 | convolution fusion | flops 25782386688 | bytes 55574592 | tf_op jit(solution)/shard_map/zyk,xk->zyx/dot_general | solution.py:207
  (43 shorter events, 1.3 us)
Async XLA Ops:
  1.3 116.3 %copy-start.1 = (s32[1,1024]{1,0:T(1,128)}, s32[1,1024]{1,0:T(1,128)S(1)}, u32[]{:S(2)}) copy-start(s32[1,1024]{1,0:T(1,128)S(1)} %broadcast_maximum_fusion) | copy-start | bytes 12292
  40.9 44.5 %copy-start.3 = (s32[1,1024]{1,0:T(1,128)S(1)}, s32[1,1024]{1,0:T(1,128)}, u32[]{:S(2)}) copy-start(s32[1,1024]{1,0:T(1,128)} %param.14) | copy-start | bytes 12292
  40.9 63.5 %copy-start.5 = (f32[1,1024]{1,0:T(1,128)S(1)}, f32[1,1024]{1,0:T(1,128)}, u32[]{:S(2)}) copy-start(f32[1,1024]{1,0:T(1,128)} %param.15) | copy-start | bytes 12292
  40.9 63.5 %copy-start.6 = (f32[1,1024]{1,0:T(1,128)S(1)}, f32[1,1024]{1,0:T(1,128)}, u32[]{:S(2)}) copy-start(f32[1,1024]{1,0:T(1,128)} %param.17) | copy-start | bytes 12292
  40.9 63.5 %copy-start.7 = (f32[1,1024]{1,0:T(1,128)S(1)}, f32[1,1024]{1,0:T(1,128)}, u32[]{:S(2)}) copy-start(f32[1,1024]{1,0:T(1,128)} %param.16) | copy-start | bytes 12292
  40.9 63.5 %copy-start.8 = (f32[1,1024]{1,0:T(1,128)S(1)}, f32[1,1024]{1,0:T(1,128)}, u32[]{:S(2)}) copy-start(f32[1,1024]{1,0:T(1,128)} %param.19) | copy-start | bytes 12292
  40.9 63.5 %copy-start.9 = (f32[1,1024]{1,0:T(1,128)S(1)}, f32[1,1024]{1,0:T(1,128)}, u32[]{:S(2)}) copy-start(f32[1,1024]{1,0:T(1,128)} %param.18) | copy-start | bytes 12292
  107.1 9.8 all-to-all-start.1
  136.9 47.9 %collective-permute-start = (f32[1,256,1024]{2,1,0:T(8,128)S(1)}, f32[1,256,1024]{2,1,0:T(8,128)S(1)}, u32[]{:S(2)}, u32[]{:S(2)}) collective-permute-start(f32[1,256,1024]{2,1,0:T(8,128)S(1)} %slice.56), channel_id=1, source_target_pairs={{1,0},{2,1},{3,2},{4,3},{5,4},{6,5},{7,6},{9,8},{10,9},{11,10},{12... | collective-permute-start | bytes 3145736 | tf_op jit(solution)/shard_map/ppermute | solution.py:195
  277.0 190.5 %all-to-all-start.2 = ((f32[16,256,1024]{1,0,2:T(8,128)}), f32[16,256,1024]{1,0,2:T(8,128)}, u32[]{:S(2)}, u32[]{:S(2)}) async-start(f32[16,256,1024]{1,0,2:T(8,128)} %copy.19), calls=%async_computation.2 | async-start | bytes 33554432 | tf_op jit(solution)/shard_map/all_to_all | solution.py:199
  542.7 52.2 %all-to-all-start.3 = ((f32[8,2,128,256]{3,2,1,0:T(8,128)}), f32[8,2,128,256]{3,2,1,0:T(8,128)S(1)}, u32[]{:S(2)}, u32[]{:S(2)}) async-start(f32[8,2,128,256]{3,2,1,0:T(8,128)} %shard_map.121), calls=%async_computation.3 | async-start | bytes 4194304 | tf_op jit(solution)/shard_map/all_to_all | solution.py:132
  594.9 1.3 copy-start
  755.5 190.1 %all-to-all-start.5 = ((f32[16,1024,256]{2,0,1:T(8,128)}), f32[16,1024,256]{2,0,1:T(8,128)}, u32[]{:S(2)}, u32[]{:S(2)}) async-start(f32[16,1024,256]{2,0,1:T(8,128)} %copy.22), calls=%async_computation.5 | async-start | bytes 33554432 | tf_op jit(solution)/shard_map/all_to_all | solution.py:206
  762.6 18.4 %copy-start.2 = (s32[1,1024]{1,0:T(1,128)S(1)}, s32[1,1024]{1,0:T(1,128)}, u32[]{:S(2)}) copy-start(s32[1,1024]{1,0:T(1,128)} %copy-done.1) | copy-start | bytes 12292
  762.6 18.4 %copy-start.4 = (f32[1024]{0:T(1024)S(1)}, f32[1024]{0:T(1024)}, u32[]{:S(2)}) copy-start(f32[1024]{0:T(1024)} %get-tuple-element.15) | copy-start | bytes 12292
  966.8 20.8 %copy-start.10 = (s32[256,1024]{1,0:T(8,128)S(1)}, s32[256,1024]{1,0:T(8,128)}, u32[]{:S(2)}) copy-start(s32[256,1024]{1,0:T(8,128)} %param.13) | copy-start | bytes 3145732
where the time goes:
time: 1040 us; the launch traced here: 1020 us
  waiting for transfers between devices  341 us (33%)
  local copies, waits for them, and re-layouts  235 us (23%)
  matrix products  172 us (17%)
  other arithmetic  121 us (12%)
  blocking collectives  70.7 us (7%)
  Pallas kernels  58.4 us (6%)
  starting transfers between devices  22.6 us (2%)
    all_to_all x1, waiting for transfers between devices, body(): lax.all_to_all(modes_x, 'px', split_axis=2, concat_axis=1, tiled=True)  163 us
    all_to_all x1, waiting for transfers between devices, body(): lax.all_to_all(spectral_y, 'px', split_axis=1, concat_axis=2, tiled=True)  125 us
    dot_general x1, matrix products, body(): spectral_y = jnp.einsum('zmk,ym->zyk', outgoing, basis_y, precision=high)  53.8 us
    all_to_all x1, blocking collectives, solve_columns(): lax.all_to_all(joined, 'py', split_axis=0, concat_axis=0, tiled=True)  52.2 us
    dot_general x1, matrix products, body(): modes_x = jnp.einsum('zyx,xk->zyk', source, basis_x, precision=high)  51.3 us
    all_to_all x1, waiting for transfers between devices, solve_columns(): edges = lax.all_to_all(edges, 'py', split_axis=0, concat_axis=0, tiled=True)  46.5 us
    all_to_all x2, local copies, waits for them, and re-layouts, body(): lax.all_to_all(spectral_y, 'px', split_axis=1, concat_axis=2, tiled=True)  41.8 us
    dot_general x1, matrix products, body(): physical = jnp.einsum('zyk,xk->zyx', spectral_y, basis_x, precision=high)  33.9 us
  transfers between devices with their start and end apart: 5, of which 4 were waited for; matrix products, arithmetic and copies ran while one was open for 12% of the time, Pallas kernels for 0%

commit v1 on v0

v1 whole, which is shorter than its diff:
```python
import math

import jax
import jax.numpy as jnp
import ml_dtypes
import numpy as np
from jax import lax
from jax.experimental import pallas as pl
from jax.experimental.pallas import tpu as pltpu
from jax.sharding import PartitionSpec as P

F32 = jnp.float32
BF16 = jnp.bfloat16
HBM = pl.BlockSpec(memory_space=pl.ANY)
VMEM = pl.BlockSpec(memory_space=pltpu.VMEM)
SMEM = pl.BlockSpec(memory_space=pltpu.SMEM)
PARAMS = pltpu.CompilerParams(vmem_limit_bytes=58 * 2**20)


def two_halves(table):
    high = table.astype(ml_dtypes.bfloat16)
    low = (table - high.astype(np.float64)).astype(ml_dtypes.bfloat16)
    return (jnp.asarray(high), jnp.asarray(low))


def periodic_tables(size):
    half, quarter = size // 2, size // 4
    groups = (
        (np.arange(0, half + 1, 4), np.arange(4, half, 4), quarter),
        (np.arange(2, half, 4), np.arange(2, half, 4), quarter),
        (np.arange(1, half, 2), np.arange(1, half, 2), half),
    )
    tables, waves = [], []
    for cosines, sines, rows in groups:
        x = np.arange(rows)[:, None]
        norms = np.where((cosines == 0) | (cosines == half), np.sqrt(1.0 / size), np.sqrt(2.0 / size))
        tables.append(
            np.concatenate(
                [
                    norms * np.cos(2.0 * np.pi / size * (x * cosines % size)),
                    np.sqrt(2.0 / size) * np.sin(2.0 * np.pi / size * (x * sines % size)),
                ],
                axis=1,
            )
        )
        waves += [cosines, sines]
    waves = np.concatenate(waves)
    return (tables, 4.0 * np.sin(np.pi * waves / size) ** 2)


def cosine_table(size):
    modes = np.arange(size)[:, None]
    table = np.sqrt(2.0 / size) * np.cos(np.pi * modes * (2 * np.arange(size)[None, :] + 1) / (2 * size))
    table[0] = np.sqrt(1.0 / size)
    return (table, 4.0 * np.sin(np.pi * modes[:, 0] / (2 * size)) ** 2)


def level_tables(size):
    modes, levels = np.arange(size)[None, :], np.arange(size)[:, None]
    omegas = (
        np.pi * (2 * modes + 1) / (2 * size + 1),
        np.pi * (modes + 1) / (size + 1),
        np.pi * (modes + 1) / (size + 0.5),
    )
    vectors = (
        np.cos(omegas[0] * (levels + 0.5)),
        np.sin(omegas[1] * (levels + 1)),
        np.sin(omegas[2] * (levels + 1)),
    )
    vectors = [v / np.sqrt(np.sum(v * v, axis=0, keepdims=True)) for v in vectors]
    return (vectors, [4.0 * np.sin(o[0] / 2) ** 2 for o in omegas])


def split(value):
    high = value.astype(BF16)
    return (high, (value - high.astype(F32)).astype(BF16))


def dot3(left, right, dims=((1,), (0,))):
    one = lambda a, b: lax.dot_general(a, b, (dims, ((), ())), preferred_element_type=F32)
    return one(left[0], right[0]) + (one(left[1], right[0]) + one(left[0], right[1]))


def read_pair(refs):
    return (refs[0][...], refs[1][...])


def periodic_forward(value, tables):
    half, quarter = value.shape[1] // 2, value.shape[1] // 4
    even, odd = value[:, :half] + value[:, half:], value[:, :half] - value[:, half:]
    parts = (even[:, :quarter] + even[:, quarter:], even[:, :quarter] - even[:, quarter:], odd)
    return jnp.concatenate([dot3(split(p), read_pair(t)) for p, t in zip(parts, tables)], axis=1)


def periodic_inverse(value, tables):
    half, quarter = value.shape[1] // 2, value.shape[1] // 4
    parts = (value[:, :quarter], value[:, quarter:half], value[:, half:])
    four, two, odd = [dot3(split(p), read_pair(t), ((1,), (1,))) for p, t in zip(parts, tables)]
    even = jnp.concatenate([four + two, four - two], axis=1)
    return jnp.concatenate([even + odd, even - odd], axis=1)


def power(base, exponent):
    result = None
    while exponent:
        if exponent & 1:
            result = base if result is None else result * base
        base = base * base
        exponent >>= 1
    return result


def first_sweeps(load, root, top, above, store, levels):
    value = None
    for level in range(levels):
        value = load(level) if value is None else load(level) + root * value
        store[level] = value
    last = value
    value = top * value if above is None else top * value + above
    for level in range(levels - 1, -1, -1):
        value = root * (value - store[level])
    return (value, last)


def second_sweeps(load, start, root, top, above, store, levels, emit):
    value = start
    for level in range(levels):
        value = root * value if load is None else load(level) + root * value
        store[level] = value
    value = top * value if above is None else top * value + above
    for level in range(levels - 1, -1, -1):
        value = root * (value - store[level])
        emit(level, value)


def block_fluxes(ends, weights_ref, vectors_ref, levels, out_ref):
    blocks = len(ends)
    one = lambda dims, b: lax.dot_general(
        vectors_ref[...], b, (dims, ((), ())), precision=lax.Precision.HIGHEST, preferred_element_type=F32
    )
    upper = lower = None
    for block in range(blocks):
        even_next, odd_next = ends[(block + 1) % blocks]
        even, odd = ends[block]
        jump = one(((0,), (0,)), (even_next + odd_next) - (even - odd))
        up, low = weights_ref[0, block] * jump, weights_ref[1, block] * jump
        upper = up if upper is None else upper + up
        lower = low if lower is None else lower + low
    upper, lower = one(((1,), (0,)), upper), one(((1,), (0,)), lower)
    width = upper.shape[1]
    is_even = lax.broadcasted_iota(jnp.int32, (8, width), 0) % 2 == 0
    for level in range(levels):
        up, low = upper[level : level + 1], lower[level : level + 1]
        out_ref[level] = jnp.where(is_even, up - low, -up - low)


def fold_ends(total, out_ref, levels):
    is_even = lax.broadcasted_iota(jnp.int32, total.shape[1:], 0) % 2 == 0
    for level in range(levels):
        value = total[level]
        out_ref[0, level : level + 1] = jnp.sum(jnp.where(is_even, value, 0.0), axis=0, keepdims=True)
        out_ref[1, level : level + 1] = jnp.sum(jnp.where(is_even, 0.0, value), axis=0, keepdims=True)


def forward_kernel(
    levels, tile, div_ref, w_ref, t0h, t0l, t1h, t1l, t2h, t2l, ch, cl, root_ref, inv_ref, start_ref, top_ref,
    end_ref, field_ref, edge_ref, ends_ref, field, above, lowest, store, total,
):
    step = pl.program_id(0)
    tables = ((t0h, t0l), (t1h, t1l), (t2h, t2l))

    def transform(value):
        return dot3(read_pair((ch, cl)), split(periodic_forward(value, tables)))

    @pl.when(step == 0)
    def _():
        above[...] = jnp.zeros_like(above)
        total[...] = jnp.zeros_like(total)

    @pl.when(step < levels)
    def _():
        value = w_ref[0]
        field[levels - 1 - step] = transform(div_ref[0] + above[...] - value)
        above[...] = value

    @pl.when(step == levels - 1)
    def _():
        lowest[...] = transform(w_ref[0])

    @pl.when(step >= levels)
    def _():
        def rows_of(sub, _):
            here = pl.multiple_of(sub * 8, 8)
            rows = pl.ds(here, 8)
            full = pl.ds(pl.multiple_of((step - levels) * tile + here, 8), 8)
            root, top = root_ref[rows], top_ref[rows]
            load = lambda level: field[level, full]
            first, _ = first_sweeps(load, root, top, None, store, levels)
            edge_ref[0, rows] = first * inv_ref[rows] - lowest[full]
            weight = end_ref[rows, :1]

            def emit(level, value):
                total[level] += weight * value
                if level == levels - 1:
                    edge_ref[1, rows] = value

            second_sweeps(load, first * start_ref[rows], root, top, None, store, levels, emit)
            for level in range(levels):
                field_ref[level, rows] = load(level)
            return 0

        lax.fori_loop(0, tile // 8, rows_of, 0)

    @pl.when(step == pl.num_programs(0) - 1)
    def _():
        fold_ends(total, ends_ref, levels)


def edge_kernel(
    levels, edge_ref, ends_ref, weights_ref, vectors_ref, root_ref, inv_ref, start_ref, top_ref, end_ref, ch, cl,
    out_ref, pattern, store, fixed,
):
    block_fluxes(
        [(ends_ref[b, 0], ends_ref[b, 1]) for b in range(ends_ref.shape[0])], weights_ref, vectors_ref, levels, pattern
    )

    def rows_of(sub, _):
        rows = pl.ds(pl.multiple_of(sub * 8, 8), 8)
        root, top = root_ref[rows], top_ref[rows]
        first, last = first_sweeps(lambda level: pattern[level], root, top, None, store, levels)
        weight = end_ref[rows, :1]
        fixed[0, rows] = edge_ref[0, rows] - weight * (first * inv_ref[rows])
        last = last + power(root, levels) * (first * start_ref[rows])
        fixed[1, rows] = edge_ref[1, rows] - weight * (root * (top - 1.0) * last)
        return 0

    lax.fori_loop(0, edge_ref.shape[1] // 8, rows_of, 0)
    for side in range(2):
        value = dot3(split(fixed[side].T), read_pair((ch, cl)))
        out_ref[:, side] = value.reshape(out_ref.shape[0], out_ref.shape[2], out_ref.shape[3])


def join_kernel(
    levels, px_count, py_count, edge_ref, t0h, t0l, t1h, t1l, t2h, t2l, diag_ref, out_ref, modes
):
    tables = ((t0h, t0l), (t1h, t1l), (t2h, t2l))
    rows, width = edge_ref.shape[2:]
    for block in range(py_count):
        for side in range(2):
            whole = jnp.concatenate([edge_ref[i * py_count + block, side] for i in range(px_count)], axis=1)
            modes[block, side] = whole
    count = 2 * py_count * rows
    modes[...] = periodic_forward(modes[...].reshape(count, -1), tables).reshape(modes.shape)

    def rows_of(sub, _):
        here = pl.ds(pl.multiple_of(sub * 8, 8), 8)
        diag = diag_ref[here]
        near = 1.0 / diag
        far = near
        beta = 1.0 / (diag + 1.0)
        top = 1.0 / (diag - 1.0)
        for _ in range(1, levels):
            near = 1.0 / (diag - near)
            far = -far * near
            beta = 1.0 / (diag - beta)
            top = 1.0 / (diag - top)
        alpha = modes[0, 1, here]
        alphas, betas, heads, slopes = [alpha], [beta], [None], [None]
        for block in range(1, py_count - 1):
            scale = 1.0 / (1.0 - near * beta)
            head = (modes[block, 0, here] - near * alpha) * scale
            slope = far * scale
            alpha = modes[block, 1, here] - far * alpha + far * beta * head
            beta = near + far * beta * slope
            alphas.append(alpha)
            betas.append(beta)
            heads.append(head)
            slopes.append(slope)
        above = jnp.zeros_like(diag)
        first = (modes[py_count - 1, 0, here] - top * alpha) / (1.0 - top * beta)
        for block in range(py_count - 1, 0, -1):
            if block < py_count - 1:
                first = heads[block] - slopes[block] * above
            modes[block, 0, here] = alphas[block - 1] - betas[block - 1] * first
            modes[block, 1, here] = above
            above = first
        modes[0, 0, here] = jnp.zeros_like(diag)
        modes[0, 1, here] = above
        return 0

    lax.fori_loop(0, rows // 8, rows_of, 0)
    modes[...] = periodic_inverse(modes[...].reshape(count, -1), tables).reshape(modes.shape)
    for block in range(py_count):
        for side in range(2):
            for i in range(px_count):
                out_ref[i * py_count + block, side] = modes[block, side, :, i * width : (i + 1) * width]


def spread_kernel(levels, joined_ref, ch, cl, root_ref, start_ref, below_ref, top_ref, end_ref, out_ref, ends_ref, store, total):
    kx_width = joined_ref.shape[0] * joined_ref.shape[2]
    for side in range(2):
        value = joined_ref[:, side].reshape(kx_width, joined_ref.shape[3])
        out_ref[side] = dot3(read_pair((ch, cl)), split(value), ((1,), (1,)))
    total[...] = jnp.zeros_like(total)

    def rows_of(sub, _):
        rows = pl.ds(pl.multiple_of(sub * 8, 8), 8)
        root, top = root_ref[rows], top_ref[rows]
        below, above = out_ref[0, rows], out_ref[1, rows]
        start = start_ref[rows] * (power(root, levels) * above) - below_ref[rows] * below
        weight = end_ref[rows, :1]

        def emit(level, value):
            total[level] += weight * value

        second_sweeps(None, start, root, top, above, store, levels, emit)
        return 0

    lax.fori_loop(0, out_ref.shape[1] // 8, rows_of, 0)
    fold_ends(total, ends_ref, levels)


def inverse_kernel(
    levels, tile, place_ref, field_ref, sides_ref, ends_ref, more_ref, weights_ref, vectors_ref, root_ref, start_ref,
    below_ref, top_ref, end_ref, t0h, t0l, t1h, t1l, t2h, t2l, ch, cl, w_ref, roof_ref, out_ref, field, pattern, store,
):
    step = pl.program_id(0)
    tiles = pl.num_programs(0) - levels
    tables = ((t0h, t0l), (t1h, t1l), (t2h, t2l))

    @pl.when(step == 0)
    def _():
        ends = [
            (ends_ref[b, 0] + more_ref[b, 0], ends_ref[b, 1] + more_ref[b, 1]) for b in range(ends_ref.shape[0])
        ]
        block_fluxes(ends, weights_ref, vectors_ref, levels, pattern)

    @pl.when(step < tiles)
    def _():
        def rows_of(sub, _):
            here = pl.multiple_of(sub * 8, 8)
            rows = pl.ds(here, 8)
            full = pl.ds(pl.multiple_of(step * tile + here, 8), 8)
            root, top = root_ref[rows], top_ref[rows]
            below, above = sides_ref[0, rows], sides_ref[1, rows]
            weight = end_ref[rows, :1]
            load = lambda level: field_ref[level, rows] - weight * pattern[level]
            first, _ = first_sweeps(load, root, top, above, store, levels)
            start = start_ref[rows] * first - below_ref[rows] * below
            held = []

            def emit(level, value):
                if held:
                    field[level + 1, full] = held.pop() - value
                held.append(value)

            second_sweeps(load, start, root, top, above, store, levels, emit)
            field[0, full] = jnp.where(place_ref[0] == 0, 0.0, held[0] - below)
            return 0

        lax.fori_loop(0, tile // 8, rows_of, 0)

    @pl.when(step >= tiles)
    def _():
        level = step - tiles
        rows_y = dot3(read_pair((ch, cl)), split(field[level]))
        slope = periodic_inverse(rows_y, tables)
        solid = place_ref[0] * levels + level < roof_ref[...]
        out_ref[0] = jnp.where(solid, 0.0, w_ref[0] - slope)


def tile_at(cell, width, tall):
    row, column = cell // width, cell % width
    return (pl.ds(pl.multiple_of(row // tall * tall, tall), tall), pl.ds(pl.multiple_of(column // 128 * 128, 128), 128))


def gather_kernel(ids_ref, w_ref, temp_ref, w_out, temp_out):
    width = w_ref.shape[1]
    group = 8

    def pick(i, _):
        for lane in range(group):
            facet = i * group + lane
            cell = jnp.maximum(ids_ref[facet], 0)
            w_out[facet] = w_ref[tile_at(cell, width, 8)]
            temp_out[facet] = temp_ref[tile_at(cell, width, 16)]
        return 0

    lax.fori_loop(0, ids_ref.shape[0] // group, pick, 0)


def scatter_kernel(ids_ref, w_new_ref, temp_new_ref, w_hbm, temp_hbm, w_out, temp_out, sems):
    copies = [
        pltpu.make_async_copy(w_hbm, w_out, sems.at[0]),
        pltpu.make_async_copy(temp_hbm, temp_out, sems.at[1]),
    ]
    for copy in copies:
        copy.start()
    width = w_out.shape[1]

    def put(facet, new_ref, out, tall):
        cell = ids_ref[facet]
        safe = jnp.maximum(cell, 0)
        here = tile_at(safe, width, tall)
        row = jnp.where(cell < 0, -1, safe // width % tall)
        hit = lax.broadcasted_iota(jnp.int32, (tall, 128), 0) == row
        hit = hit & (lax.broadcasted_iota(jnp.int32, (tall, 128), 1) == safe % 128)
        out[here] = jnp.where(hit, new_ref[facet], out[here].astype(F32)).astype(out.dtype)
        return 0

    copies[0].wait()
    lax.fori_loop(0, ids_ref.shape[0], lambda facet, _: put(facet, w_new_ref, w_out, 8), 0)
    copies[1].wait()
    lax.fori_loop(0, ids_ref.shape[0], lambda facet, _: put(facet, temp_new_ref, temp_out, 16), 0)


def near_walls(w_rows, temp_rows, ids, facet_temp, net_radiation, heat_capacity, drag_coef, heat_coef):
    count = ids.shape[0]
    near = pl.pallas_call(
        gather_kernel,
        out_shape=(jax.ShapeDtypeStruct((count, 8, 128), F32), jax.ShapeDtypeStruct((count, 16, 128), BF16)),
        in_specs=[SMEM, VMEM, VMEM],
        out_specs=(VMEM, VMEM),
        compiler_params=PARAMS,
        name="facet_gather",
    )(ids, w_rows, temp_rows)

    def own_cell(tiles):
        hit = lax.broadcasted_iota(jnp.int32, tiles.shape, 1) == (ids // w_rows.shape[1] % tiles.shape[1])[:, None, None]
        hit = hit & (lax.broadcasted_iota(jnp.int32, tiles.shape, 2) == (ids % 128)[:, None, None])
        hit = hit & (ids >= 0)[:, None, None]
        return jnp.sum(jnp.where(hit, tiles.astype(F32), 0.0), axis=(1, 2))

    own = jnp.stack([own_cell(tiles) for tiles in near])
    arrived = lax.all_to_all(own, ("px", "py"), split_axis=1, concat_axis=1, tiled=True)
    w_cell, temp_cell = arrived[0], arrived[1]
    speeds = jnp.sqrt(w_cell * w_cell + 0.25)
    stress = drag_coef * speeds * w_cell
    heat_flux = heat_coef * speeds * (facet_temp - temp_cell)
    new_temp = facet_temp + (net_radiation - heat_flux - 0.5 * facet_temp) / heat_capacity
    returned = lax.all_to_all(
        jnp.stack([stress, heat_flux]), ("px", "py"), split_axis=1, concat_axis=1, tiled=True
    )
    same = ids[:, None] == ids[None, :]
    sums = [jnp.sum(jnp.where(same, returned[i][None, :], 0.0), axis=1) for i in range(2)]
    w_corr, theta = pl.pallas_call(
        scatter_kernel,
        out_shape=(jax.ShapeDtypeStruct(w_rows.shape, F32), jax.ShapeDtypeStruct(temp_rows.shape, BF16)),
        in_specs=[SMEM, SMEM, SMEM, HBM, HBM],
        out_specs=(VMEM, VMEM),
        scratch_shapes=[pltpu.SemaphoreType.DMA((2,))],
        compiler_params=PARAMS,
        name="facet_scatter",
    )(ids, own[0] - sums[0], own[1] + sums[1], w_rows, temp_rows)
    return (w_corr, theta, new_temp)


def body(
    horiz_div,
    w_star,
    air_temp,
    roof_level,
    facet_cells,
    facet_temp,
    net_radiation,
    heat_capacity,
    drag_coef,
    heat_coef,
):
    levels, rows, width = w_star.shape
    px_count, py_count = lax.axis_size("px"), lax.axis_size("py")
    devices = px_count * py_count
    place_x, place_y = lax.axis_index("px"), lax.axis_index("py")
    own_kx = width // devices
    y_cells = rows * px_count

    w_corr, theta_new, new_temp = near_walls(
        w_star.reshape(levels * rows, width),
        air_temp.reshape(levels * rows, width),
        facet_cells[0],
        facet_temp[0],
        net_radiation[0],
        heat_capacity[0],
        drag_coef[0],
        heat_coef[0],
    )
    w_corr = w_corr.reshape(w_star.shape)
    theta_new = theta_new.reshape(air_temp.shape)

    x_parts, sin_x = periodic_tables(width)
    y_parts, sin_y = periodic_tables(y_cells)
    cosines, sin_block = cosine_table(rows)
    x_tables = [t for part in x_parts for t in two_halves(part)]
    y_tables = [t for part in y_parts for t in two_halves(part)]
    to_modes, to_rows = two_halves(cosines), two_halves(np.ascontiguousarray(cosines.T))
    sin_x = jnp.asarray(sin_x, F32)

    sine = jnp.asarray(sin_block, F32)[:, None] + sin_x[None, :]
    half_root = 0.5 * jnp.sqrt(sine)
    root = jnp.sqrt(1.0 + half_root * half_root) - half_root
    root = root * root
    is_first, is_last = place_y == 0, place_y == py_count - 1
    top = jnp.where(is_last, root / (1.0 + root), 0.0)
    kappa = jnp.zeros_like(root)
    for _ in range(levels):
        kappa = root * root * (1.0 + kappa)
    decay = power(root, levels)
    bottom = jnp.where(is_first, 1.0 - 1.0 / root, 1.0)
    inv = 1.0 / (1.0 + bottom * (kappa - top * decay * decay))
    start = bottom * inv
    from_below = inv / root
    end = np.where(np.arange(rows) == 0, np.sqrt(1.0 / rows), cosines[:, 0])
    end = jnp.asarray(np.repeat(end[:, None], 128, axis=1), F32)

    vectors, sin_z = level_tables(levels)
    pick = lambda three: jnp.where(is_first, three[0], jnp.where(is_last, three[2], three[1])).astype(F32)
    vectors, sin_z = pick(vectors), pick(sin_z)
    sine_z = sin_z[:, None] + sin_x[None, :]
    size_z = jnp.sqrt(sine_z)
    half_z = 0.5 * size_z
    cosh_z = jnp.sqrt(1.0 + half_z * half_z)
    half_step = cosh_z - half_z
    across = jnp.exp(2.0 * rows * jnp.log(half_step))
    scale = 1.0 / ((1.0 - across * across) * size_z)
    same_end = -half_step * (1.0 + across * across / (half_step * half_step)) * scale
    far_end = -2.0 * across * cosh_z * scale
    turns = np.arange(px_count)
    circulant = jnp.stack(
        [1.0 / (1.0 - 2.0 * same_end + 2.0 * math.cos(2.0 * math.pi * s / px_count) * far_end) for s in turns]
    )
    phase_of = jnp.asarray(np.cos(2.0 * np.pi * turns[:, None] * turns[None, :] / px_count) / px_count, F32)
    offsets = jnp.stack([(place_x - turns) % px_count, (place_x - 1 - turns) % px_count])
    phases = phase_of[offsets]
    weights = jnp.sum(phases[:, :, :, None, None] * circulant[None, None], axis=2)

    mine = place_x * py_count + place_y
    own_sin = lax.dynamic_slice_in_dim(sin_x, mine * own_kx, own_kx)
    diag = -2.0 - own_sin[:, None] - jnp.asarray(sin_y, F32)[None, :]

    tile = math.gcd(rows, 32)
    tiles = rows // tile
    flat = lambda i: pl.BlockSpec((tile, width), i)
    fixed = lambda a: pl.BlockSpec(a.shape, lambda i: (0,) * a.ndim)
    late = lambda i: (jnp.maximum(i - levels, 0), 0)
    down = lambda i: (jnp.maximum(levels - 1 - i, 0), 0, 0)
    slab = pl.BlockSpec((1, rows, width), down)
    end_late = pl.BlockSpec((tile, 128), late)
    ends_shape = jax.ShapeDtypeStruct((2, levels, width), F32)
    field, edges, ends = pl.pallas_call(
        lambda *refs: forward_kernel(levels, tile, *refs),
        out_shape=(
            jax.ShapeDtypeStruct(w_star.shape, F32),
            jax.ShapeDtypeStruct((2, rows, width), F32),
            ends_shape,
        ),
        grid=(levels + tiles,),
        in_specs=[slab, slab] + [fixed(t) for t in (*x_tables, *to_modes)] + [flat(late)] * 4 + [end_late],
        out_specs=(
            pl.BlockSpec((levels, tile, width), lambda i: (0, *late(i))),
            pl.BlockSpec((2, tile, width), lambda i: (0, *late(i))),
            fixed(ends_shape),
        ),
        scratch_shapes=[
            pltpu.VMEM(w_star.shape, F32),
            pltpu.VMEM((rows, width), F32),
            pltpu.VMEM((rows, width), F32),
            pltpu.VMEM((levels, 8, width), F32),
            pltpu.VMEM((levels, 8, width), F32),
        ],
        compiler_params=PARAMS,
        name="forward",
    )(horiz_div, w_corr, *x_tables, *to_modes, root, inv, start, top, end)

    all_ends = lax.all_gather(ends, "px")
    packed = jax.ShapeDtypeStruct((devices, 2, own_kx, rows), F32)
    working = [pltpu.VMEM((levels, 8, width), F32)] * 2
    edges = pl.pallas_call(
        lambda *refs: edge_kernel(levels, *refs),
        out_shape=packed,
        in_specs=[VMEM] * 11,
        out_specs=VMEM,
        scratch_shapes=working + [pltpu.VMEM((2, rows, width), F32)],
        compiler_params=PARAMS,
        name="edges",
    )(edges, all_ends, weights, vectors, root, inv, start, top, end, *to_modes)
    edges = lax.all_to_all(edges, ("px", "py"), split_axis=0, concat_axis=0, tiled=True)
    joined = pl.pallas_call(
        lambda *refs: join_kernel(levels, px_count, py_count, *refs),
        out_shape=packed,
        in_specs=[VMEM] * 8,
        out_specs=VMEM,
        scratch_shapes=[pltpu.VMEM((py_count, 2, own_kx, y_cells), F32)],
        compiler_params=PARAMS,
        name="join",
    )(edges, *y_tables, diag)
    joined = lax.all_to_all(joined, ("px", "py"), split_axis=0, concat_axis=0, tiled=True)
    sides, more = pl.pallas_call(
        lambda *refs: spread_kernel(levels, *refs),
        out_shape=(jax.ShapeDtypeStruct((2, rows, width), F32), ends_shape),
        in_specs=[VMEM] * 8,
        out_specs=(VMEM, VMEM),
        scratch_shapes=working,
        compiler_params=PARAMS,
        name="spread",
    )(joined, *to_modes, root, start, from_below, top, end)
    more = lax.all_gather(more, "px")

    early = lambda i: (jnp.minimum(i, tiles - 1), 0)
    up = lambda i: (jnp.maximum(i - tiles, 0), 0, 0)
    slab = pl.BlockSpec((1, rows, width), up)
    w_new = pl.pallas_call(
        lambda *refs: inverse_kernel(levels, tile, *refs),
        out_shape=jax.ShapeDtypeStruct(w_star.shape, F32),
        grid=(tiles + levels,),
        in_specs=[
            SMEM,
            pl.BlockSpec((levels, tile, width), lambda i: (0, *early(i))),
            pl.BlockSpec((2, tile, width), lambda i: (0, *early(i))),
        ]
        + [fixed(a) for a in (all_ends, more, weights, vectors)]
        + [flat(early)] * 4
        + [pl.BlockSpec((tile, 128), early)]
        + [fixed(t) for t in (*x_tables, *to_rows)]
        + [slab, fixed(roof_level)],
        out_specs=slab,
        scratch_shapes=[pltpu.VMEM(w_star.shape, F32)] + working,
        compiler_params=PARAMS,
        name="inverse",
    )(
        place_y.astype(jnp.int32).reshape(1),
        field,
        sides,
        all_ends,
        more,
        weights,
        vectors,
        root,
        start,
        from_below,
        top,
        end,
        *x_tables,
        *to_rows,
        w_corr,
        roof_level,
    )
    return (w_new, theta_new, new_temp[None])


def solution(mesh):
    placed = (
        P("py", "px", None),
        P("py", "px", None),
        P("py", "px", None),
        P("px", None),
        P(("px", "py"), None),
        P(("px", "py"), None),
        P(("px", "py"), None),
        P(("px", "py"), None),
        P(("px", "py"), None),
        P(("px", "py"), None),
    )
    return jax.shard_map(
        body,
        mesh=mesh,
        in_specs=placed,
        out_specs=(P("py", "px", None), P("py", "px", None), P(("px", "py"), None)),
        check_vma=False,
    )
```

time: 1040 us -> 391 us (0.38); the launches traced: 1020 us -> 389 us
  waiting for transfers between devices: 341 us -> 56.7 us
  local copies, waits for them, and re-layouts: 235 us -> 3.38 us
  matrix products: 172 us -> 0 us
  Pallas kernels: 58.4 us -> 194 us
  other arithmetic: 121 us -> 49.9 us
    all_to_all x4 -> x3, waiting for transfers between devices: 341 us -> 56.7 us  [the longest x1 49.1 us: body(): lax.all_to_all(edges, ('px', 'py'), split_axis=0, concat_axis=0, tiled=True)]
    dot_general x4 -> x0, matrix products: 172 us -> none  [the longest x1 53.8 us: body(): spectral_y = jnp.einsum('zmk,ym->zyk', outgoing, basis_y, precision=high)]
    pallas_call x3 -> x7, Pallas kernels: 58.4 us -> 194 us  [the longest x1 58.1 us: near_walls(): pl.pallas_call(scatter_kernel, out_shape=(jax.ShapeDtypeStruct(w_rows.sha...]
    all_to_all x3 -> x0, local copies, waits for them, and re-layouts: 61.1 us -> none  [the longest x2 41.8 us: body(): lax.all_to_all(spectral_y, 'px', split_axis=1, concat_axis=2, tiled=True)]
    dot_general x3 -> x0, other arithmetic: 60 us -> none  [the longest x1 23.4 us: body(): modes_x = jnp.einsum('zyx,xk->zyk', source, basis_x, precision=high)]
    gather x2 -> x1, local copies, waits for them, and re-layouts: 44.5 us -> 0.56 us  [body(): phases = phase_of[offsets]]
    reduce_sum x0 -> x4, other arithmetic: none -> 39 us  [the longest x2 36.9 us: own_cell(): return jnp.sum(jnp.where(hit, tiles.astype(F32), 0.0), axis=(1, 2))]
    scatter-add x2 -> x0, other arithmetic: 35.1 us -> none  [the longest x1 17.8 us: body(): w_corr = w_flat.at[safe_ids].add(-momentum_sink).reshape(w_star.shape)]
  transfers between devices with their start and end apart: 5 -> 3, of which waited for: 4 -> 3; matrix products, arithmetic and copies ran while one was open for 12% -> 2% of each run, Pallas kernels for 0% -> 0%
where the time goes in v1:
time: 391 us; the launch traced here: 389 us
  Pallas kernels  194 us (50%)
  blocking collectives  69.7 us (18%)
  waiting for transfers between devices  56.7 us (15%)
  other arithmetic  49.9 us (13%)
  starting transfers between devices  14.7 us (4%)
    pallas_call x1, Pallas kernels, near_walls(): pl.pallas_call(scatter_kernel, out_shape=(jax.ShapeDtypeStruct(w_rows.sha...  58.1 us
    all_to_all x1, blocking collectives, body(): lax.all_to_all(joined, ('px', 'py'), split_axis=0, concat_axis=0, tiled=T...  53.5 us
    all_to_all x1, waiting for transfers between devices, body(): lax.all_to_all(edges, ('px', 'py'), split_axis=0, concat_axis=0, tiled=True)  49.1 us
    pallas_call x1, Pallas kernels, body(): pl.pallas_call(lambda *refs: inverse_kernel(levels, tile, *refs), out_sha...  40.8 us
    pallas_call x1, Pallas kernels, body(): pl.pallas_call(lambda *refs: forward_kernel(levels, tile, *refs), out_sha...  39.9 us
    reduce_sum x2, other arithmetic, own_cell(): return jnp.sum(jnp.where(hit, tiles.astype(F32), 0.0), axis=(1, 2))  36.9 us
    pallas_call x1, Pallas kernels, near_walls(): pl.pallas_call(gather_kernel, out_shape=(jax.ShapeDtypeStruct((count, 8,...  27.8 us
    pallas_call x1, Pallas kernels, body(): pl.pallas_call(lambda *refs: edge_kernel(levels, *refs), out_shape=packed...  9.79 us
  transfers between devices with their start and end apart: 3, of which 3 were waited for; matrix products, arithmetic and copies ran while one was open for 2% of the time, Pallas kernels for 0%

profile of v1, /device:TPU:0, one launch (start us, length us, event | category | flops | bytes accessed | tf_op | source)
XLA Modules:
  0.0 389.0 jit_solution(10028413530214208549)
XLA Ops:
  0.6 0.7 broadcast_compare_fusion
  1.3 0.7 add_select_fusion
  2.0 27.8 %facet_gather.1 = (f32[1024,8,128]{2,1,0:T(8,128)}, bf16[1024,16,128]{2,1,0:T(8,128)(2,1)}) custom-call(s32[1024]{0:T(1024)} %bitcast.24, f32[4096,1024]{1,0:T(8,128)} %bitcast.15, bf16[4096,1024]{1,0:T(8,128)(2,1)} %bitcast.17), custom_call_target="tpu_custom_call" | custom-call | tf_op jit(solution)/shard_map/facet_gather/pallas_call | solution.py:419
  29.8 0.0 copy-start.3
  29.9 18.5 %select_reduce_fusion = f32[1024]{0:T(1024)S(1)} fusion(bf16[1024,16,128]{2,1,0:T(8,128)(2,1)} %get-tuple-element.13, s32[1024]{0:T(1024)S(1)} %get-tuple-element.41, s32[1024]{0:T(1024)S(1)} %get-tuple-element.39, pred[1024]{0:T(1024)(128)(4,1)S(1)} %broadcast_compare_fusion), kind=kLoop, calls=%fused_computation.1 | loop fusion | flops 14679040 | bytes 4207616 | tf_op jit(solution)/shard_map/reduce_sum | solution.py:432
  48.4 0.1 stack.35
  48.5 18.4 %select_reduce_fusion.1 = f32[1024]{0:T(1024)S(1)} fusion(f32[1024,8,128]{2,1,0:T(8,128)} %get-tuple-element.12, s32[1024]{0:T(1024)S(1)} %get-tuple-element.41, s32[1024]{0:T(1024)S(1)} %get-tuple-element.40, pred[1024]{0:T(1024)(128)(4,1)S(1)} %broadcast_compare_fusion), kind=kLoop, calls=%fused_computation.10 | loop fusion | flops 6290432 | bytes 4207616 | tf_op jit(solution)/shard_map/reduce_sum | solution.py:432
  67.0 0.1 stack.34
  67.1 0.7 pad_maximum_fusion.1
  67.7 7.3 %all-to-all-start = ((f32[2,32,32]{2,0,1:T(2,128)}), f32[2,32,32]{2,0,1:T(2,128)S(1)}, u32[]{:S(2)}, u32[]{:S(2)}) async-start(f32[2,32,32]{2,0,1:T(2,128)} %pad_maximum_fusion.1), calls=%async_computation | async-start | bytes 65536 | tf_op jit(solution)/shard_map/all_to_all | solution.py:435
  75.1 0.1 reshape.494
  75.2 0.2 add_divide_fusion.4
  75.4 4.1 %multiply_divide_fusion = (f32[256,1024]{1,0:T(8,128)}, f32[256,1024]{1,0:T(8,128)}, f32[256,1024]{1,0:T(8,128)}, f32[256,1024]{1,0:T(8,128)}, f32[256,1024]{1,0:T(8,128)}) fusion(f32[1024]{0:T(1024)S(1)} %copy-done.3, f32[256]{0:T(256)S(1)} %copy-done.13, pred[]{:T(512)S(6)} %eq.71, pred[]{:T(512)S(6)} %eq.70), kind=kLoop, calls=%fused_computation.49 | loop fusion | flops 14417920 | bytes 5248002 | tf_op jit(solution)/shard_map/div | solution.py:511
  79.5 0.6 select_select_fusion.refs_3_.refs_6_
  80.2 0.6 gather_fusion
  80.7 1.5 all-to-all-done
  82.2 0.1 slice_reduce_fusion.3
  82.3 0.1 slice.21
  82.4 0.1 slice.23
  82.5 0.6 divide_add_fusion
  83.2 0.5 broadcast.665
  83.7 0.7 reduce.27
  84.3 0.1 stack.38
  84.4 0.1 stack.37
  84.5 0.7 pad_maximum_fusion.2
  85.2 4.4 %all-to-all-start.1 = ((f32[2,32,32]{2,0,1:T(2,128)}), f32[2,32,32]{2,0,1:T(2,128)S(1)}, u32[]{:S(2)}, u32[]{:S(2)}) async-start(f32[2,32,32]{2,0,1:T(2,128)} %pad_maximum_fusion.2), calls=%async_computation.1 | async-start | bytes 65536 | tf_op jit(solution)/shard_map/all_to_all | solution.py:441
  89.5 1.1 multiply_reduce_fusion.refs_2_.refs_5_
  90.6 6.1 %all-to-all-done.1 = f32[2,32,32]{2,0,1:T(2,128)S(1)} async-done(((f32[2,32,32]{2,0,1:T(2,128)}), f32[2,32,32]{2,0,1:T(2,128)S(1)}, u32[]{:S(2)}, u32[]{:S(2)}) %all-to-all-start.1) | async-done | bytes 8224 | tf_op jit(solution)/shard_map/all_to_all | solution.py:441
  96.7 0.1 slice_reduce_fusion
  96.8 0.1 broadcast_in_dim.56
  96.9 0.1 broadcast_in_dim.53
  97.0 1.0 fusion.3
  97.9 0.6 add.273.temp_new_ref
  98.5 0.6 sub.139.w_new_ref
  99.1 58.1 %facet_scatter.1 = (f32[4096,1024]{1,0:T(8,128)}, bf16[4096,1024]{1,0:T(8,128)(2,1)}) custom-call(s32[1024]{0:T(1024)} %bitcast.25, f32[1024]{0:T(1024)} %sub.139.w_new_ref, f32[1024]{0:T(1024)} %add.273.temp_new_ref, f32[4096,1024]{1,0:T(8,128)} %bitcast.16, bf16[4096,1024]{1,0:T(8,128)(2,1)} %bitcast.18), custom_call_target="tpu_custom_call" | custom-call | tf_op jit(solution)/shard_map/facet_scatter/pallas_call | solution.py:446
  157.2 39.9 %forward.1 = (f32[16,256,1024]{2,1,0:T(8,128)}, f32[2,256,1024]{2,1,0:T(8,128)}, f32[2,16,1024]{2,1,0:T(8,128)}) custom-call(f32[16,256,1024]{2,1,0:T(8,128)} %refs_0_.1, f32[16,256,1024]{2,1,0:T(8,128)} %bitcast.13, bf16[256,256]{1,0:T(8,128)(2,1)} %constant.159.clone.refs_2_.refs_1_.refs_12_, bf16[256,256]{1,0:T(8,128)(2,1)} %constant.160.clone.refs_3_.refs_2_.refs_13_, ...), custom_call_target="tpu_custom_call" | custom-call | tf_op jit(solution)/shard_map/forward/pallas_call | solution.py:549
  197.1 8.0 %all-gather = f32[8,16,1024]{2,1,0:T(8,128)} all-gather(f32[2,16,1024]{2,1,0:T(8,128)} %get-tuple-element.17), channel_id=2, replica_groups=mesh['px'=4,'py'=8] {'px'}, dimensions={0}, use_global_device_ids=true | all-gather | bytes 655360 | tf_op jit(solution)/shard_map/all_gather | solution.py:574
  205.1 9.8 %edges.1 = f32[32,2,32,256]{3,2,1,0:T(8,128)} custom-call(f32[2,256,1024]{2,1,0:T(8,128)} %get-tuple-element.16.refs_0_, f32[4,2,16,1024]{3,2,1,0:T(8,128)} %bitcast.19, f32[2,4,16,1024]{3,2,1,0:T(8,128)} %multiply_reduce_fusion.refs_2_.refs_5_, f32[16,16]{1,0:T(8,128)} %select_select_fusion.refs_3_.refs_6_, ...), custom_call_target="tpu_custom_call" | custom-call | tf_op jit(solution)/shard_map/edges/pallas_call | solution.py:577
  214.9 3.0 all-to-all-start.2
  218.0 0.1 dynamic-slice_subtract_fusion
  218.0 0.7 broadcast_add_fusion.refs_7_
  218.7 49.1 %all-to-all-done.2.refs_0_ = f32[32,2,32,256]{3,2,1,0:T(8,128)S(1)} async-done(((f32[32,2,32,256]{3,2,1,0:T(8,128)}), f32[32,2,32,256]{3,2,1,0:T(8,128)S(1)}, u32[]{:S(2)}, u32[]{:S(2)}) %all-to-all-start.2) | async-done | bytes 2097184 | tf_op jit(solution)/shard_map/all_to_all | solution.py:586
  267.9 1.3 copy-done
  269.2 7.9 %join.1 = f32[32,2,32,256]{3,2,1,0:T(8,128)} custom-call(f32[32,2,32,256]{3,2,1,0:T(8,128)} %copy-done, bf16[256,256]{1,0:T(8,128)(2,1)} %constant.159.clone.refs_2_.refs_1_.refs_12_, bf16[256,256]{1,0:T(8,128)(2,1)} %constant.160.clone.refs_3_.refs_2_.refs_13_, bf16[256,256]{1,0:T(8,128)(2,1)} %constant.161.clone.refs_4_.refs_3_.refs_14_, ...), custom_call_target="tpu_custom_call" | custom-call | tf_op jit(solution)/shard_map/join/pallas_call | solution.py:587
  277.1 53.5 %all_to_all.22.refs_0_ = f32[32,2,32,256]{3,2,1,0:T(8,128)} all-to-all(f32[32,2,32,256]{3,2,1,0:T(8,128)} %join.1), channel_id=1, replica_groups=mesh['px'=4,'py'=8] {'px','py'}, dimensions={0} | all-to-all | bytes 4194304 | tf_op jit(solution)/shard_map/all_to_all | solution.py:596
  330.6 9.3 %spread.1 = (f32[2,256,1024]{2,1,0:T(8,128)}, f32[2,16,1024]{2,1,0:T(8,128)}) custom-call(f32[32,2,32,256]{3,2,1,0:T(8,128)} %all_to_all.22.refs_0_, bf16[256,256]{1,0:T(8,128)(2,1)} %constant.165.clone.refs_8_.refs_9_.refs_1_, bf16[256,256]{1,0:T(8,128)(2,1)} %constant.166.clone.refs_9_.refs_10_.refs_2_, ...), custom_call_target="tpu_custom_call" | custom-call | tf_op jit(solution)/shard_map/spread/pallas_call | solution.py:597
  339.9 8.2 %all-gather.1 = f32[8,16,1024]{2,1,0:T(8,128)} all-gather(f32[2,16,1024]{2,1,0:T(8,128)} %get-tuple-element.19), channel_id=3, replica_groups=mesh['px'=4,'py'=8] {'px'}, dimensions={0}, use_global_device_ids=true | all-gather | bytes 655360 | tf_op jit(solution)/shard_map/all_gather | solution.py:606
  348.1 40.8 %inverse.1 = f32[16,256,1024]{2,1,0:T(8,128)} custom-call(s32[1]{0:T(128)} %bitcast.refs_0_, f32[16,256,1024]{2,1,0:T(8,128)} %get-tuple-element.15.refs_1_, f32[2,256,1024]{2,1,0:T(8,128)} %get-tuple-element.18.refs_2_, f32[4,2,16,1024]{3,2,1,0:T(8,128)} %bitcast.20, f32[4,2,16,1024]{3,2,1,0:T(8,128)} %bitcast.21, ...), custom_call_target="tpu_custom_call" | custom-call | tf_op jit(solution)/shard_map/inverse/pallas_call | solution.py:611
  (37 shorter events, 0.2 us)
Async XLA Ops:
  29.8 45.4 %copy-start.14 = (f32[16]{0:T(128)S(1)}, f32[16]{0:T(128)}, u32[]{:S(2)}) copy-start(f32[16]{0:T(128)} %constant.177.clone) | copy-start | bytes 196
  29.8 45.4 %copy-start.15 = (f32[16]{0:T(128)S(1)}, f32[16]{0:T(128)}, u32[]{:S(2)}) copy-start(f32[16]{0:T(128)} %constant.176.clone) | copy-start | bytes 196
  29.8 45.4 %copy-start.16 = (f32[16]{0:T(128)S(1)}, f32[16]{0:T(128)}, u32[]{:S(2)}) copy-start(f32[16]{0:T(128)} %constant.175.clone) | copy-start | bytes 196
  29.8 45.4 %copy-start.3 = (f32[1024]{0:T(1024)S(1)}, f32[1024]{0:T(1024)}, u32[]{:S(2)}) copy-start(f32[1024]{0:T(1024)} %constant.169.clone) | copy-start | bytes 12292
  29.8 45.6 %copy-start.13 = (f32[256]{0:T(256)S(1)}, f32[256]{0:T(256)}, u32[]{:S(2)}) copy-start(f32[256]{0:T(256)} %constant.170.clone) | copy-start | bytes 3076
  48.4 31.1 %copy-start.4 = (f32[16,16]{1,0:T(8,128)S(1)}, f32[16,16]{1,0:T(8,128)}, u32[]{:S(2)}) copy-start(f32[16,16]{1,0:T(8,128)} %constant.174.clone) | copy-start | bytes 3076
  48.5 31.1 %copy-start.5 = (f32[16,16]{1,0:T(8,128)S(1)}, f32[16,16]{1,0:T(8,128)}, u32[]{:S(2)}) copy-start(f32[16,16]{1,0:T(8,128)} %constant.173.clone) | copy-start | bytes 3076
  48.5 31.1 %copy-start.6 = (f32[16,16]{1,0:T(8,128)S(1)}, f32[16,16]{1,0:T(8,128)}, u32[]{:S(2)}) copy-start(f32[16,16]{1,0:T(8,128)} %constant.172.clone) | copy-start | bytes 3076
  48.5 31.7 %copy-start.1 = (f32[4,4]{1,0:T(4,128)S(1)}, f32[4,4]{1,0:T(4,128)}, u32[]{:S(2)}) copy-start(f32[4,4]{1,0:T(4,128)} %constant.178.clone) | copy-start | bytes 196
  66.9 15.6 %copy-start.7 = (f32[1,1024]{1,0:T(1,128)S(1)}, f32[1,1024]{1,0:T(1,128)}, u32[]{:S(2)}) copy-start(f32[1,1024]{1,0:T(1,128)} %param.43) | copy-start | bytes 12292
  66.9 15.6 %copy-start.8 = (f32[1,1024]{1,0:T(1,128)S(1)}, f32[1,1024]{1,0:T(1,128)}, u32[]{:S(2)}) copy-start(f32[1,1024]{1,0:T(1,128)} %param.45) | copy-start | bytes 12292
  67.0 15.5 %copy-start.9 = (f32[1,1024]{1,0:T(1,128)S(1)}, f32[1,1024]{1,0:T(1,128)}, u32[]{:S(2)}) copy-start(f32[1,1024]{1,0:T(1,128)} %param.44) | copy-start | bytes 12292
  67.0 15.5 %copy-start.10 = (f32[1,1024]{1,0:T(1,128)S(1)}, f32[1,1024]{1,0:T(1,128)}, u32[]{:S(2)}) copy-start(f32[1,1024]{1,0:T(1,128)} %param.47) | copy-start | bytes 12292
  67.0 15.5 %copy-start.11 = (f32[1,1024]{1,0:T(1,128)S(1)}, f32[1,1024]{1,0:T(1,128)}, u32[]{:S(2)}) copy-start(f32[1,1024]{1,0:T(1,128)} %param.46) | copy-start | bytes 12292
  67.0 30.0 %copy-start.2 = (s32[1,1024]{1,0:T(1,128)S(1)}, s32[1,1024]{1,0:T(1,128)}, u32[]{:S(2)}) copy-start(s32[1,1024]{1,0:T(1,128)} %param.42) | copy-start | bytes 12292
  67.7 14.5 %all-to-all-start = ((f32[2,32,32]{2,0,1:T(2,128)}), f32[2,32,32]{2,0,1:T(2,128)S(1)}, u32[]{:S(2)}, u32[]{:S(2)}) async-start(f32[2,32,32]{2,0,1:T(2,128)} %pad_maximum_fusion.1), calls=%async_computation | async-start | bytes 65536 | tf_op jit(solution)/shard_map/all_to_all | solution.py:435
  85.2 11.6 %all-to-all-start.1 = ((f32[2,32,32]{2,0,1:T(2,128)}), f32[2,32,32]{2,0,1:T(2,128)S(1)}, u32[]{:S(2)}, u32[]{:S(2)}) async-start(f32[2,32,32]{2,0,1:T(2,128)} %pad_maximum_fusion.2), calls=%async_computation.1 | async-start | bytes 65536 | tf_op jit(solution)/shard_map/all_to_all | solution.py:441
  214.9 3.1 copy-start.12
  214.9 53.0 %all-to-all-start.2 = ((f32[32,2,32,256]{3,2,1,0:T(8,128)}), f32[32,2,32,256]{3,2,1,0:T(8,128)S(1)}, u32[]{:S(2)}, u32[]{:S(2)}) async-start(f32[32,2,32,256]{3,2,1,0:T(8,128)} %edges.1), calls=%async_computation.2 | async-start | bytes 4194304 | tf_op jit(solution)/shard_map/all_to_all | solution.py:586
  267.9 1.3 copy-start

commit v2 on v1

--- a/solution.py
+++ b/solution.py
@@ -163,8 +163,9 @@
 
 
 def forward_kernel(
-    levels, tile, div_ref, w_ref, t0h, t0l, t1h, t1l, t2h, t2l, ch, cl, root_ref, inv_ref, start_ref, top_ref,
-    end_ref, field_ref, edge_ref, ends_ref, field, above, lowest, store, total,
+    levels, tile, ids_ref, w_new_ref, w_hbm, div_ref, t0h, t0l, t1h, t1l, t2h, t2l, ch, cl, root_ref, inv_ref,
+    start_ref, top_ref, end_ref, field_ref, edge_ref, ends_ref, corr_hbm, field, w_rows, above, lowest, store, total,
+    sems,
 ):
     step = pl.program_id(0)
     tables = ((t0h, t0l), (t1h, t1l), (t2h, t2l))
@@ -174,18 +175,25 @@
 
     @pl.when(step == 0)
     def _():
+        load = pltpu.make_async_copy(w_hbm, w_rows, sems.at[0])
+        load.start()
         above[...] = jnp.zeros_like(above)
         total[...] = jnp.zeros_like(total)
+        load.wait()
+        put_cells(ids_ref, w_new_ref, w_rows)
+        pltpu.make_async_copy(w_rows, corr_hbm, sems.at[1]).start()
+
+    row_count = above.shape[0]
 
     @pl.when(step < levels)
     def _():
-        value = w_ref[0]
+        value = w_rows[pl.ds(pl.multiple_of((levels - 1 - step) * row_count, row_count), row_count)]
         field[levels - 1 - step] = transform(div_ref[0] + above[...] - value)
         above[...] = value
 
     @pl.when(step == levels - 1)
     def _():
-        lowest[...] = transform(w_ref[0])
+        lowest[...] = transform(w_rows[:row_count])
 
     @pl.when(step >= levels)
     def _():
@@ -214,6 +222,7 @@
     @pl.when(step == pl.num_programs(0) - 1)
     def _():
         fold_ends(total, ends_ref, levels)
+        pltpu.make_async_copy(w_rows, corr_hbm, sems.at[1]).wait()
 
 
 def edge_kernel(
@@ -369,69 +378,113 @@
         out_ref[0] = jnp.where(solid, 0.0, w_ref[0] - slope)
 
 
+def divide(value, size):
+    if size & (size - 1):
+        return lax.div(value, size)
+    return lax.shift_right_logical(value, size.bit_length() - 1)
+
+
+def remainder(value, size):
+    return lax.rem(value, size) if size & (size - 1) else value & (size - 1)
+
+
 def tile_at(cell, width, tall):
-    row, column = cell // width, cell % width
-    return (pl.ds(pl.multiple_of(row // tall * tall, tall), tall), pl.ds(pl.multiple_of(column // 128 * 128, 128), 128))
-
-
-def gather_kernel(ids_ref, w_ref, temp_ref, w_out, temp_out):
-    width = w_ref.shape[1]
-    group = 8
-
-    def pick(i, _):
-        for lane in range(group):
-            facet = i * group + lane
-            cell = jnp.maximum(ids_ref[facet], 0)
-            w_out[facet] = w_ref[tile_at(cell, width, 8)]
-            temp_out[facet] = temp_ref[tile_at(cell, width, 16)]
-        return 0
-
-    lax.fori_loop(0, ids_ref.shape[0] // group, pick, 0)
-
-
-def scatter_kernel(ids_ref, w_new_ref, temp_new_ref, w_hbm, temp_hbm, w_out, temp_out, sems):
+    row, column = divide(cell, width), remainder(cell, width)
+    return (
+        pl.ds(pl.multiple_of(divide(row, tall) * tall, tall), tall),
+        pl.ds(pl.multiple_of(divide(column, 128) * 128, 128), 128),
+    )
+
+
+def gather_kernel(ids_ref, w_hbm, temp_hbm, w_out, temp_out, w_ref, temp_ref, sems):
     copies = [
-        pltpu.make_async_copy(w_hbm, w_out, sems.at[0]),
-        pltpu.make_async_copy(temp_hbm, temp_out, sems.at[1]),
+        pltpu.make_async_copy(w_hbm, w_ref, sems.at[0]),
+        pltpu.make_async_copy(temp_hbm, temp_ref, sems.at[1]),
     ]
     for copy in copies:
         copy.start()
-    width = w_out.shape[1]
-
-    def put(facet, new_ref, out, tall):
-        cell = ids_ref[facet]
-        safe = jnp.maximum(cell, 0)
-        here = tile_at(safe, width, tall)
-        row = jnp.where(cell < 0, -1, safe // width % tall)
-        hit = lax.broadcasted_iota(jnp.int32, (tall, 128), 0) == row
-        hit = hit & (lax.broadcasted_iota(jnp.int32, (tall, 128), 1) == safe % 128)
-        out[here] = jnp.where(hit, new_ref[facet], out[here].astype(F32)).astype(out.dtype)
+    width = w_ref.shape[1]
+    sublane = lax.broadcasted_iota(jnp.int32, (8, 128), 0)
+
+    def pick(i, ref, out):
+        rows = None
+        for lane in range(8):
+            cell = jnp.maximum(ids_ref[i * 8 + lane], 0)
+            row = divide(cell, width)
+            if ref.dtype == F32:
+                tile = ref[tile_at(cell, width, 8)]
+            else:
+                both = ref[tile_at(cell, width, 16)].astype(F32)
+                tile = jnp.where(remainder(row, 16) < 8, both[:8], both[8:])
+            tile = pltpu.roll(tile, remainder(lane + 8 - remainder(row, 8), 8), 0)
+            rows = tile if rows is None else jnp.where(sublane == lane, tile, rows)
+        out[pl.ds(pl.multiple_of(i * 8, 8), 8)] = rows
         return 0
 
+    groups = ids_ref.shape[0] // 8
     copies[0].wait()
-    lax.fori_loop(0, ids_ref.shape[0], lambda facet, _: put(facet, w_new_ref, w_out, 8), 0)
+    lax.fori_loop(0, groups, lambda i, _: pick(i, w_ref, w_out), 0)
     copies[1].wait()
-    lax.fori_loop(0, ids_ref.shape[0], lambda facet, _: put(facet, temp_new_ref, temp_out, 16), 0)
+    lax.fori_loop(0, groups, lambda i, _: pick(i, temp_ref, temp_out), 0)
+
+
+def put_cells(ids_ref, new_ref, out):
+    width = out.shape[1]
+    sublane = lax.broadcasted_iota(jnp.int32, (8, 128), 0)
+    lane = lax.broadcasted_iota(jnp.int32, (8, 128), 1)
+    position = sublane * 128 + lane
+
+    def put(i, _):
+        for k in range(8):
+            facet = i * 8 + k
+            cell = ids_ref[facet]
+            safe = jnp.maximum(cell, 0)
+            at = remainder(divide(safe, width), 8) * 128 + remainder(safe, 128)
+            hit = position == jnp.where(cell < 0, -1, at)
+            pltpu.store(out.at[tile_at(safe, width, 8)], jnp.full((8, 128), new_ref[facet]), mask=hit)
+        return 0
+
+    lax.fori_loop(0, ids_ref.shape[0] // 8, put, 0)
+
+
+def theta_kernel(ids_ref, new_ref, temp_ref, out_ref, wide):
+    rows = temp_ref.shape[0]
+    chunk = math.gcd(rows, 64)
+
+    def widen(i, _):
+        here = pl.ds(pl.multiple_of(i * chunk, chunk), chunk)
+        wide[here] = temp_ref[here].astype(F32)
+        return 0
+
+    def narrow(i, _):
+        here = pl.ds(pl.multiple_of(i * chunk, chunk), chunk)
+        out_ref[here] = wide[here].astype(BF16)
+        return 0
+
+    lax.fori_loop(0, rows // chunk, widen, 0)
+    put_cells(ids_ref, new_ref, wide)
+    lax.fori_loop(0, rows // chunk, narrow, 0)
 
 
 def near_walls(w_rows, temp_rows, ids, facet_temp, net_radiation, heat_capacity, drag_coef, heat_coef):
     count = ids.shape[0]
+    shape = jax.ShapeDtypeStruct((count, 128), F32)
     near = pl.pallas_call(
         gather_kernel,
-        out_shape=(jax.ShapeDtypeStruct((count, 8, 128), F32), jax.ShapeDtypeStruct((count, 16, 128), BF16)),
-        in_specs=[SMEM, VMEM, VMEM],
+        out_shape=(shape, shape),
+        in_specs=[SMEM, HBM, HBM],
         out_specs=(VMEM, VMEM),
+        scratch_shapes=[
+            pltpu.VMEM(w_rows.shape, F32),
+            pltpu.VMEM(temp_rows.shape, BF16),
+            pltpu.SemaphoreType.DMA((2,)),
+        ],
         compiler_params=PARAMS,
         name="facet_gather",
     )(ids, w_rows, temp_rows)
-
-    def own_cell(tiles):
-        hit = lax.broadcasted_iota(jnp.int32, tiles.shape, 1) == (ids // w_rows.shape[1] % tiles.shape[1])[:, None, None]
-        hit = hit & (lax.broadcasted_iota(jnp.int32, tiles.shape, 2) == (ids % 128)[:, None, None])
-        hit = hit & (ids >= 0)[:, None, None]
-        return jnp.sum(jnp.where(hit, tiles.astype(F32), 0.0), axis=(1, 2))
-
-    own = jnp.stack([own_cell(tiles) for tiles in near])
+    lane = jnp.where(ids < 0, -1, ids % 128)
+    hit = lax.broadcasted_iota(jnp.int32, (count, 128), 1) == lane[:, None]
+    own = jnp.stack([jnp.sum(jnp.where(hit, rows, 0.0), axis=1) for rows in near])
     arrived = lax.all_to_all(own, ("px", "py"), split_axis=1, concat_axis=1, tiled=True)
     w_cell, temp_cell = arrived[0], arrived[1]
     speeds = jnp.sqrt(w_cell * w_cell + 0.25)
@@ -443,16 +496,7 @@
     )
     same = ids[:, None] == ids[None, :]
     sums = [jnp.sum(jnp.where(same, returned[i][None, :], 0.0), axis=1) for i in range(2)]
-    w_corr, theta = pl.pallas_call(
-        scatter_kernel,
-        out_shape=(jax.ShapeDtypeStruct(w_rows.shape, F32), jax.ShapeDtypeStruct(temp_rows.shape, BF16)),
-        in_specs=[SMEM, SMEM, SMEM, HBM, HBM],
-        out_specs=(VMEM, VMEM),
-        scratch_shapes=[pltpu.SemaphoreType.DMA((2,))],
-        compiler_params=PARAMS,
-        name="facet_scatter",
-    )(ids, own[0] - sums[0], own[1] + sums[1], w_rows, temp_rows)
-    return (w_corr, theta, new_temp)
+    return (own[0] - sums[0], own[1] + sums[1], new_temp)
 
 
 def body(
@@ -474,18 +518,19 @@
     own_kx = width // devices
     y_cells = rows * px_count
 
-    w_corr, theta_new, new_temp = near_walls(
-        w_star.reshape(levels * rows, width),
-        air_temp.reshape(levels * rows, width),
-        facet_cells[0],
+    w_rows = w_star.reshape(levels * rows, width)
+    temp_rows = air_temp.reshape(levels * rows, width)
+    ids = facet_cells[0]
+    w_near, temp_near, new_temp = near_walls(
+        w_rows,
+        temp_rows,
+        ids,
         facet_temp[0],
         net_radiation[0],
         heat_capacity[0],
         drag_coef[0],
         heat_coef[0],
     )
-    w_corr = w_corr.reshape(w_star.shape)
-    theta_new = theta_new.reshape(air_temp.shape)
 
     x_parts, sin_x = periodic_tables(width)
     y_parts, sin_y = periodic_tables(y_cells)
@@ -546,30 +591,34 @@
     slab = pl.BlockSpec((1, rows, width), down)
     end_late = pl.BlockSpec((tile, 128), late)
     ends_shape = jax.ShapeDtypeStruct((2, levels, width), F32)
-    field, edges, ends = pl.pallas_call(
+    field, edges, ends, w_corr = pl.pallas_call(
         lambda *refs: forward_kernel(levels, tile, *refs),
         out_shape=(
             jax.ShapeDtypeStruct(w_star.shape, F32),
             jax.ShapeDtypeStruct((2, rows, width), F32),
             ends_shape,
+            jax.ShapeDtypeStruct(w_rows.shape, F32),
         ),
         grid=(levels + tiles,),
-        in_specs=[slab, slab] + [fixed(t) for t in (*x_tables, *to_modes)] + [flat(late)] * 4 + [end_late],
+        in_specs=[SMEM, SMEM, HBM, slab] + [fixed(t) for t in (*x_tables, *to_modes)] + [flat(late)] * 4 + [end_late],
         out_specs=(
             pl.BlockSpec((levels, tile, width), lambda i: (0, *late(i))),
             pl.BlockSpec((2, tile, width), lambda i: (0, *late(i))),
             fixed(ends_shape),
+            HBM,
         ),
         scratch_shapes=[
             pltpu.VMEM(w_star.shape, F32),
+            pltpu.VMEM(w_rows.shape, F32),
             pltpu.VMEM((rows, width), F32),
             pltpu.VMEM((rows, width), F32),
             pltpu.VMEM((levels, 8, width), F32),
             pltpu.VMEM((levels, 8, width), F32),
+            pltpu.SemaphoreType.DMA((2,)),
         ],
         compiler_params=PARAMS,
         name="forward",
-    )(horiz_div, w_corr, *x_tables, *to_modes, root, inv, start, top, end)
+    )(ids, w_near, w_rows, horiz_div, *x_tables, *to_modes, root, inv, start, top, end)
 
     all_ends = lax.all_gather(ends, "px")
     packed = jax.ShapeDtypeStruct((devices, 2, own_kx, rows), F32)
@@ -583,6 +632,17 @@
         compiler_params=PARAMS,
         name="edges",
     )(edges, all_ends, weights, vectors, root, inv, start, top, end, *to_modes)
+    temp_near, edges = lax.optimization_barrier((temp_near, edges))
+    theta_new = pl.pallas_call(
+        theta_kernel,
+        out_shape=jax.ShapeDtypeStruct(temp_rows.shape, BF16),
+        in_specs=[SMEM, SMEM, VMEM],
+        out_specs=VMEM,
+        scratch_shapes=[pltpu.VMEM(temp_rows.shape, F32)],
+        compiler_params=PARAMS,
+        cost_estimate=pl.CostEstimate(flops=temp_rows.size, bytes_accessed=8 * temp_rows.size, transcendentals=0),
+        name="theta",
+    )(ids, temp_near, temp_rows).reshape(air_temp.shape)
     edges = lax.all_to_all(edges, ("px", "py"), split_axis=0, concat_axis=0, tiled=True)
     joined = pl.pallas_call(
         lambda *refs: join_kernel(levels, px_count, py_count, *refs),
@@ -641,7 +701,7 @@
         end,
         *x_tables,
         *to_rows,
-        w_corr,
+        w_corr.reshape(w_star.shape),
         roof_level,
     )
     return (w_new, theta_new, new_temp[None])

time: 391 us -> 302 us (0.77)
  blocking collectives: 69.7 us -> 16.2 us
  Pallas kernels: 194 us -> 156 us
  other arithmetic: 49.9 us -> 14 us
  waiting for transfers between devices: 56.7 us -> 91.1 us
    all_to_all x1 -> x0, blocking collectives: 53.5 us -> none  [body(): lax.all_to_all(joined, ('px', 'py'), split_axis=0, concat_axis=0, tiled=T...]
    pallas_call x2, Pallas kernels: 85.9 us -> 35.9 us  [the longest x1 20.2 us: near_walls(): pl.pallas_call(gather_kernel, out_shape=(shape, shape), in_specs=[SMEM, H...]
    reduce_sum x2 -> x1, other arithmetic: 36.9 us -> 1.73 us  [near_walls(): jnp.sum(jnp.where(hit, rows, 0.0), axis=1)]
    all_to_all x0 -> x1, waiting for transfers between devices: none -> 34.4 us  [body(): lax.all_to_all(joined, ('px', 'py'), split_axis=0, concat_axis=0, tiled=T...]
    pallas_call x1, Pallas kernels: 39.9 us -> 52.5 us  [body(): pl.pallas_call(lambda *refs: forward_kernel(levels, tile, *refs), out_sha...]
  transfers between devices with their start and end apart: 3 -> 4, of which waited for: 3 -> 4; matrix products, arithmetic and copies ran while one was open for 2% -> 2% of each run, Pallas kernels for 0% -> 5%
where the time goes in v2:
time: 302 us; the launch traced here: 301 us
  Pallas kernels  156 us (52%)
  waiting for transfers between devices  91.1 us (30%)
  starting transfers between devices  17.5 us (6%)
  blocking collectives  16.2 us (5%)
  other arithmetic  14 us (5%)
  local copies, waits for them, and re-layouts  4.71 us (2%)
    pallas_call x1, Pallas kernels, body(): pl.pallas_call(lambda *refs: forward_kernel(levels, tile, *refs), out_sha...  52.5 us
    all_to_all x1, waiting for transfers between devices, body(): lax.all_to_all(edges, ('px', 'py'), split_axis=0, concat_axis=0, tiled=True)  49.1 us
    pallas_call x1, Pallas kernels, body(): pl.pallas_call(lambda *refs: inverse_kernel(levels, tile, *refs), out_sha...  40.8 us
    all_to_all x1, waiting for transfers between devices, body(): lax.all_to_all(joined, ('px', 'py'), split_axis=0, concat_axis=0, tiled=T...  34.4 us
    pallas_call x1, Pallas kernels, near_walls(): pl.pallas_call(gather_kernel, out_shape=(shape, shape), in_specs=[SMEM, H...  20.2 us
    pallas_call x1, Pallas kernels, body(): pl.pallas_call(theta_kernel, out_shape=jax.ShapeDtypeStruct(temp_rows.sha...  15.7 us
    pallas_call x1, Pallas kernels, body(): pl.pallas_call(lambda *refs: edge_kernel(levels, *refs), out_shape=packed...  9.79 us
    pallas_call x1, Pallas kernels, body(): pl.pallas_call(lambda *refs: spread_kernel(levels, *refs), out_shape=(jax...  9.3 us
  transfers between devices with their start and end apart: 4, of which 4 were waited for; matrix products, arithmetic and copies ran while one was open for 2% of the time, Pallas kernels for 5%

profile of v2, /device:TPU:0, one launch (start us, length us, event | category | flops | bytes accessed | tf_op | source)
XLA Modules:
  0.0 300.7 jit_solution(749725745907174463)
XLA Ops:
  0.6 0.7 compare_select_fusion.3
  1.3 0.0 copy-start.17
  1.4 20.2 %facet_gather.1 = (f32[1024,128]{1,0:T(8,128)}, f32[1024,128]{1,0:T(8,128)}) custom-call(s32[1024]{0:T(1024)} %bitcast.23, f32[4096,1024]{1,0:T(8,128)} %bitcast.13, bf16[4096,1024]{1,0:T(8,128)(2,1)} %bitcast.15), custom_call_target="tpu_custom_call" | custom-call | tf_op jit(solution)/shard_map/facet_gather/pallas_call | solution.py:472
  21.7 1.7 select_reduce_fusion
  23.5 0.1 stack.35
  23.6 0.1 stack.34
  23.7 0.7 pad_maximum_fusion.1
  24.3 7.3 %all-to-all-start = ((f32[2,32,32]{2,0,1:T(2,128)}), f32[2,32,32]{2,0,1:T(2,128)S(1)}, u32[]{:S(2)}, u32[]{:S(2)}) async-start(f32[2,32,32]{2,0,1:T(2,128)} %pad_maximum_fusion.1), calls=%async_computation | async-start | bytes 65536 | tf_op jit(solution)/shard_map/all_to_all | solution.py:488
  31.7 0.1 reshape.435
  31.8 0.2 add_divide_fusion.4
  32.0 4.1 %multiply_divide_fusion = (f32[256,1024]{1,0:T(8,128)}, f32[256,1024]{1,0:T(8,128)}, f32[256,1024]{1,0:T(8,128)}, f32[256,1024]{1,0:T(8,128)}, f32[256,1024]{1,0:T(8,128)}) fusion(f32[1024]{0:T(1024)S(1)} %copy-done.4, f32[256]{0:T(256)S(1)} %copy-done.14, pred[]{:T(512)S(6)} %eq.38, pred[]{:T(512)S(6)} %eq.37), kind=kLoop, calls=%fused_computation.39 | loop fusion | flops 14417920 | bytes 5248002 | tf_op jit(solution)/shard_map/div | solution.py:556
  36.1 0.6 select_select_fusion.refs_3_.refs_6_
  36.8 0.6 gather_fusion
  37.3 1.5 all-to-all-done
  38.8 0.1 slice_reduce_fusion.3
  38.9 0.1 slice.21
  39.0 0.1 slice.23
  39.1 0.6 divide_add_fusion
  39.7 0.5 broadcast.554
  40.2 0.7 reduce.27
  40.9 0.1 stack.38
  41.0 0.1 stack.37
  41.1 0.7 pad_maximum_fusion.2
  41.7 4.4 %all-to-all-start.1 = ((f32[2,32,32]{2,0,1:T(2,128)}), f32[2,32,32]{2,0,1:T(2,128)S(1)}, u32[]{:S(2)}, u32[]{:S(2)}) async-start(f32[2,32,32]{2,0,1:T(2,128)} %pad_maximum_fusion.2), calls=%async_computation.1 | async-start | bytes 65536 | tf_op jit(solution)/shard_map/all_to_all | solution.py:494
  46.1 1.1 multiply_reduce_fusion.refs_2_.refs_5_
  47.2 6.1 %all-to-all-done.1 = f32[2,32,32]{2,0,1:T(2,128)S(1)} async-done(((f32[2,32,32]{2,0,1:T(2,128)}), f32[2,32,32]{2,0,1:T(2,128)S(1)}, u32[]{:S(2)}, u32[]{:S(2)}) %all-to-all-start.1) | async-done | bytes 8224 | tf_op jit(solution)/shard_map/all_to_all | solution.py:494
  53.3 0.1 slice_reduce_fusion
  53.4 0.1 broadcast_in_dim.53
  53.5 0.1 broadcast_in_dim.49
  53.6 1.0 fusion.1
  54.5 0.6 add.266.new_ref
  55.1 0.6 sub.130.refs_1_
  55.7 52.5 %forward.1 = (f32[16,256,1024]{2,1,0:T(8,128)}, f32[2,256,1024]{2,1,0:T(8,128)}, f32[2,16,1024]{2,1,0:T(8,128)}, f32[4096,1024]{1,0:T(8,128)}) custom-call(s32[1024]{0:T(1024)} %bitcast.24, f32[1024]{0:T(1024)} %sub.130.refs_1_, f32[4096,1024]{1,0:T(8,128)} %bitcast.14, f32[16,256,1024]{2,1,0:T(8,128)} %refs_3_.2, ...), custom_call_target="tpu_custom_call" | custom-call | tf_op jit(solution)/shard_map/forward/pallas_call | solution.py:594
  108.2 8.0 %all-gather = f32[8,16,1024]{2,1,0:T(8,128)} all-gather(f32[2,16,1024]{2,1,0:T(8,128)} %get-tuple-element.17), channel_id=2, replica_groups=mesh['px'=4,'py'=8] {'px'}, dimensions={0}, use_global_device_ids=true | all-gather | bytes 655360 | tf_op jit(solution)/shard_map/all_gather | solution.py:623
  116.2 9.8 %edges.1 = f32[32,2,32,256]{3,2,1,0:T(8,128)} custom-call(f32[2,256,1024]{2,1,0:T(8,128)} %get-tuple-element.16.refs_0_, f32[4,2,16,1024]{3,2,1,0:T(8,128)} %bitcast.19, f32[2,4,16,1024]{3,2,1,0:T(8,128)} %multiply_reduce_fusion.refs_2_.refs_5_, f32[16,16]{1,0:T(8,128)} %select_select_fusion.refs_3_.refs_6_, ...), custom_call_target="tpu_custom_call" | custom-call | tf_op jit(solution)/shard_map/edges/pallas_call | solution.py:626
  126.0 3.0 %all-to-all-start.2 = ((f32[32,2,32,256]{3,2,1,0:T(8,128)}), f32[32,2,32,256]{3,2,1,0:T(8,128)S(1)}, u32[]{:S(2)}, u32[]{:S(2)}) async-start(f32[32,2,32,256]{3,2,1,0:T(8,128)} %edges.1), calls=%async_computation.2 | async-start | bytes 4194304 | tf_op jit(solution)/shard_map/all_to_all | solution.py:646
  129.1 0.1 dynamic-slice_subtract_fusion
  129.1 0.7 broadcast_add_fusion.refs_7_
  129.9 49.1 %all-to-all-done.2.refs_0_ = f32[32,2,32,256]{3,2,1,0:T(8,128)S(1)} async-done(((f32[32,2,32,256]{3,2,1,0:T(8,128)}), f32[32,2,32,256]{3,2,1,0:T(8,128)S(1)}, u32[]{:S(2)}, u32[]{:S(2)}) %all-to-all-start.2) | async-done | bytes 2097184 | tf_op jit(solution)/shard_map/all_to_all | solution.py:646
  179.0 1.3 copy-done
  180.3 7.9 %join.1 = f32[32,2,32,256]{3,2,1,0:T(8,128)} custom-call(f32[32,2,32,256]{3,2,1,0:T(8,128)} %copy-done, bf16[256,256]{1,0:T(8,128)(2,1)} %constant.123.clone.refs_4_.refs_1_.refs_12_, bf16[256,256]{1,0:T(8,128)(2,1)} %constant.124.clone.refs_5_.refs_2_.refs_13_, bf16[256,256]{1,0:T(8,128)(2,1)} %constant.125.clone.refs_6_.refs_3_.refs_14_, ...), custom_call_target="tpu_custom_call" | custom-call | tf_op jit(solution)/shard_map/join/pallas_call | solution.py:647
  188.2 2.7 all-to-all-start.3
  190.9 15.7 %theta.1 = bf16[4096,1024]{1,0:T(8,128)(2,1)} custom-call(s32[1024]{0:T(1024)} %bitcast.25, f32[1024]{0:T(1024)} %add.266.new_ref, bf16[4096,1024]{1,0:T(8,128)(2,1)} %bitcast.16), custom_call_target="tpu_custom_call" | custom-call | flops 4194304 | bytes 33554432 | tf_op jit(solution)/shard_map/theta/pallas_call | solution.py:636
  206.6 34.4 %all-to-all-done.3.refs_0_ = f32[32,2,32,256]{3,2,1,0:T(8,128)S(1)} async-done(((f32[32,2,32,256]{3,2,1,0:T(8,128)}), f32[32,2,32,256]{3,2,1,0:T(8,128)S(1)}, u32[]{:S(2)}, u32[]{:S(2)}) %all-to-all-start.3) | async-done | bytes 2097184 | tf_op jit(solution)/shard_map/all_to_all | solution.py:656
  241.0 1.3 copy-done.1
  242.3 9.3 %spread.1 = (f32[2,256,1024]{2,1,0:T(8,128)}, f32[2,16,1024]{2,1,0:T(8,128)}) custom-call(f32[32,2,32,256]{3,2,1,0:T(8,128)} %copy-done.1, bf16[256,256]{1,0:T(8,128)(2,1)} %constant.129.clone.refs_10_.refs_9_.refs_1_, bf16[256,256]{1,0:T(8,128)(2,1)} %constant.130.clone.refs_11_.refs_10_.refs_2_, ...), custom_call_target="tpu_custom_call" | custom-call | tf_op jit(solution)/shard_map/spread/pallas_call | solution.py:657
  251.7 8.2 %all-gather.1 = f32[8,16,1024]{2,1,0:T(8,128)} all-gather(f32[2,16,1024]{2,1,0:T(8,128)} %get-tuple-element.20), channel_id=3, replica_groups=mesh['px'=4,'py'=8] {'px'}, dimensions={0}, use_global_device_ids=true | all-gather | bytes 655360 | tf_op jit(solution)/shard_map/all_gather | solution.py:666
  259.8 40.8 %inverse.1 = f32[16,256,1024]{2,1,0:T(8,128)} custom-call(s32[1]{0:T(128)} %bitcast.refs_0_, f32[16,256,1024]{2,1,0:T(8,128)} %get-tuple-element.15.refs_1_, f32[2,256,1024]{2,1,0:T(8,128)} %get-tuple-element.19.refs_2_, f32[4,2,16,1024]{3,2,1,0:T(8,128)} %bitcast.20, f32[4,2,16,1024]{3,2,1,0:T(8,128)} %bitcast.21, ...), custom_call_target="tpu_custom_call" | custom-call | tf_op jit(solution)/shard_map/inverse/pallas_call | solution.py:671
  (38 shorter events, 0.2 us)
Async XLA Ops:
  1.3 30.4 %copy-start.15 = (f32[16]{0:T(128)S(1)}, f32[16]{0:T(128)}, u32[]{:S(2)}) copy-start(f32[16]{0:T(128)} %constant.141.clone) | copy-start | bytes 196
  1.3 30.4 %copy-start.16 = (f32[16]{0:T(128)S(1)}, f32[16]{0:T(128)}, u32[]{:S(2)}) copy-start(f32[16]{0:T(128)} %constant.140.clone) | copy-start | bytes 196
  1.3 30.4 %copy-start.17 = (f32[16]{0:T(128)S(1)}, f32[16]{0:T(128)}, u32[]{:S(2)}) copy-start(f32[16]{0:T(128)} %constant.139.clone) | copy-start | bytes 196
  1.3 30.4 %copy-start.4 = (f32[1024]{0:T(1024)S(1)}, f32[1024]{0:T(1024)}, u32[]{:S(2)}) copy-start(f32[1024]{0:T(1024)} %constant.133.clone) | copy-start | bytes 12292
  1.4 30.6 %copy-start.14 = (f32[256]{0:T(256)S(1)}, f32[256]{0:T(256)}, u32[]{:S(2)}) copy-start(f32[256]{0:T(256)} %constant.134.clone) | copy-start | bytes 3076
  21.6 14.5 %copy-start.5 = (f32[16,16]{1,0:T(8,128)S(1)}, f32[16,16]{1,0:T(8,128)}, u32[]{:S(2)}) copy-start(f32[16,16]{1,0:T(8,128)} %constant.138.clone) | copy-start | bytes 3076
  21.6 14.5 %copy-start.6 = (f32[16,16]{1,0:T(8,128)S(1)}, f32[16,16]{1,0:T(8,128)}, u32[]{:S(2)}) copy-start(f32[16,16]{1,0:T(8,128)} %constant.137.clone) | copy-start | bytes 3076
  21.6 14.5 %copy-start.7 = (f32[16,16]{1,0:T(8,128)S(1)}, f32[16,16]{1,0:T(8,128)}, u32[]{:S(2)}) copy-start(f32[16,16]{1,0:T(8,128)} %constant.136.clone) | copy-start | bytes 3076
  21.7 15.1 %copy-start.2 = (f32[4,4]{1,0:T(4,128)S(1)}, f32[4,4]{1,0:T(4,128)}, u32[]{:S(2)}) copy-start(f32[4,4]{1,0:T(4,128)} %constant.142.clone) | copy-start | bytes 196
  21.7 17.4 %copy-start.8 = (f32[1,1024]{1,0:T(1,128)S(1)}, f32[1,1024]{1,0:T(1,128)}, u32[]{:S(2)}) copy-start(f32[1,1024]{1,0:T(1,128)} %param.43) | copy-start | bytes 12292
  21.7 17.4 %copy-start.9 = (f32[1,1024]{1,0:T(1,128)S(1)}, f32[1,1024]{1,0:T(1,128)}, u32[]{:S(2)}) copy-start(f32[1,1024]{1,0:T(1,128)} %param.45) | copy-start | bytes 12292
  21.7 17.4 %copy-start.10 = (f32[1,1024]{1,0:T(1,128)S(1)}, f32[1,1024]{1,0:T(1,128)}, u32[]{:S(2)}) copy-start(f32[1,1024]{1,0:T(1,128)} %param.44) | copy-start | bytes 12292
  21.7 17.4 %copy-start.11 = (f32[1,1024]{1,0:T(1,128)S(1)}, f32[1,1024]{1,0:T(1,128)}, u32[]{:S(2)}) copy-start(f32[1,1024]{1,0:T(1,128)} %param.47) | copy-start | bytes 12292
  21.7 17.4 %copy-start.12 = (f32[1,1024]{1,0:T(1,128)S(1)}, f32[1,1024]{1,0:T(1,128)}, u32[]{:S(2)}) copy-start(f32[1,1024]{1,0:T(1,128)} %param.46) | copy-start | bytes 12292
  21.7 31.8 %copy-start.3 = (s32[1,1024]{1,0:T(1,128)S(1)}, s32[1,1024]{1,0:T(1,128)}, u32[]{:S(2)}) copy-start(s32[1,1024]{1,0:T(1,128)} %param.42) | copy-start | bytes 12292
  24.3 14.5 %all-to-all-start = ((f32[2,32,32]{2,0,1:T(2,128)}), f32[2,32,32]{2,0,1:T(2,128)S(1)}, u32[]{:S(2)}, u32[]{:S(2)}) async-start(f32[2,32,32]{2,0,1:T(2,128)} %pad_maximum_fusion.1), calls=%async_computation | async-start | bytes 65536 | tf_op jit(solution)/shard_map/all_to_all | solution.py:488
  41.7 11.6 %all-to-all-start.1 = ((f32[2,32,32]{2,0,1:T(2,128)}), f32[2,32,32]{2,0,1:T(2,128)S(1)}, u32[]{:S(2)}, u32[]{:S(2)}) async-start(f32[2,32,32]{2,0,1:T(2,128)} %pad_maximum_fusion.2), calls=%async_computation.1 | async-start | bytes 65536 | tf_op jit(solution)/shard_map/all_to_all | solution.py:494
  126.0 3.1 %copy-start.13 = (f32[1024]{0:T(1024)S(1)}, f32[1024]{0:T(1024)}, u32[]{:S(2)}) copy-start(f32[1024]{0:T(1024)} %constant.149) | copy-start | bytes 12292
  126.0 53.0 %all-to-all-start.2 = ((f32[32,2,32,256]{3,2,1,0:T(8,128)}), f32[32,2,32,256]{3,2,1,0:T(8,128)S(1)}, u32[]{:S(2)}, u32[]{:S(2)}) async-start(f32[32,2,32,256]{3,2,1,0:T(8,128)} %edges.1), calls=%async_computation.2 | async-start | bytes 4194304 | tf_op jit(solution)/shard_map/all_to_all | solution.py:646
  179.0 1.3 copy-start
  188.2 52.8 %all-to-all-start.3 = ((f32[32,2,32,256]{3,2,1,0:T(8,128)}), f32[32,2,32,256]{3,2,1,0:T(8,128)S(1)}, u32[]{:S(2)}, u32[]{:S(2)}) async-start(f32[32,2,32,256]{3,2,1,0:T(8,128)} %join.1), calls=%async_computation.3 | async-start | bytes 4194304 | tf_op jit(solution)/shard_map/all_to_all | solution.py:656
  241.0 1.3 copy-start.1

commit v3 on v2

--- a/solution.py
+++ b/solution.py
@@ -249,60 +249,89 @@
         out_ref[:, side] = value.reshape(out_ref.shape[0], out_ref.shape[2], out_ref.shape[3])
 
 
-def join_kernel(
-    levels, px_count, py_count, edge_ref, t0h, t0l, t1h, t1l, t2h, t2l, diag_ref, out_ref, modes
-):
-    tables = ((t0h, t0l), (t1h, t1l), (t2h, t2l))
-    rows, width = edge_ref.shape[2:]
-    for block in range(py_count):
+def join_start(levels, near_top, diag):
+    near = 1.0 / diag
+    far = near
+    ends = [1.0 / (diag + 1.0), 1.0 / (diag - 1.0)]
+    for _ in range(1, levels):
+        near = 1.0 / (diag - near)
+        far = -far * near
+        ends = [1.0 / (diag - e) for e in ends]
+    own = jnp.where(near_top, ends[1], ends[0])
+    other = jnp.where(near_top, ends[0], ends[1])
+    return (near, far, own, other)
+
+
+def join_chain(load, blocks, near, far, beta):
+    alpha = load(0, 1)
+    alphas, betas, heads, slopes = [alpha], [beta], [None], [None]
+    for block in range(1, blocks):
+        scale = 1.0 / (1.0 - near * beta)
+        head = (load(block, 0) - near * alpha) * scale
+        slope = far * scale
+        alpha = load(block, 1) - far * alpha + far * beta * head
+        beta = near + far * beta * slope
+        alphas.append(alpha)
+        betas.append(beta)
+        heads.append(head)
+        slopes.append(slope)
+    return (alphas, betas, heads, slopes)
+
+
+def chain_place(block, blocks, half):
+    return block + half * (blocks - 1 - 2 * block)
+
+
+def gather_modes_kernel(levels, px_count, half_ref, edge_ref, t0h, t0l, t1h, t1l, t2h, t2l, diag_ref, out_ref, alpha_ref):
+    blocks, _, rows, _ = out_ref.shape
+    half = half_ref[0]
+    for block in range(blocks):
         for side in range(2):
-            whole = jnp.concatenate([edge_ref[i * py_count + block, side] for i in range(px_count)], axis=1)
-            modes[block, side] = whole
-    count = 2 * py_count * rows
-    modes[...] = periodic_forward(modes[...].reshape(count, -1), tables).reshape(modes.shape)
+            whole = jnp.concatenate([edge_ref[i * blocks + block, side] for i in range(px_count)], axis=1)
+            out_ref[block, side] = periodic_forward(whole, ((t0h, t0l), (t1h, t1l), (t2h, t2l)))
 
     def rows_of(sub, _):
         here = pl.ds(pl.multiple_of(sub * 8, 8), 8)
-        diag = diag_ref[here]
-        near = 1.0 / diag
-        far = near
-        beta = 1.0 / (diag + 1.0)
-        top = 1.0 / (diag - 1.0)
-        for _ in range(1, levels):
-            near = 1.0 / (diag - near)
-            far = -far * near
-            beta = 1.0 / (diag - beta)
-            top = 1.0 / (diag - top)
-        alpha = modes[0, 1, here]
-        alphas, betas, heads, slopes = [alpha], [beta], [None], [None]
-        for block in range(1, py_count - 1):
-            scale = 1.0 / (1.0 - near * beta)
-            head = (modes[block, 0, here] - near * alpha) * scale
-            slope = far * scale
-            alpha = modes[block, 1, here] - far * alpha + far * beta * head
-            beta = near + far * beta * slope
-            alphas.append(alpha)
-            betas.append(beta)
-            heads.append(head)
-            slopes.append(slope)
-        above = jnp.zeros_like(diag)
-        first = (modes[py_count - 1, 0, here] - top * alpha) / (1.0 - top * beta)
-        for block in range(py_count - 1, 0, -1):
-            if block < py_count - 1:
-                first = heads[block] - slopes[block] * above
-            modes[block, 0, here] = alphas[block - 1] - betas[block - 1] * first
-            modes[block, 1, here] = above
-            above = first
-        modes[0, 0, here] = jnp.zeros_like(diag)
-        modes[0, 1, here] = above
+        near, far, own, _ = join_start(levels, half == 1, diag_ref[here])
+        load = lambda block, outer: out_ref[chain_place(block, blocks, half), jnp.abs(outer - half), here]
+        alpha_ref[here] = join_chain(load, blocks, near, far, own)[0][-1]
         return 0
 
     lax.fori_loop(0, rows // 8, rows_of, 0)
-    modes[...] = periodic_inverse(modes[...].reshape(count, -1), tables).reshape(modes.shape)
-    for block in range(py_count):
+
+
+def join_kernel(
+    levels, px_count, half_ref, modes_ref, alpha_ref, t0h, t0l, t1h, t1l, t2h, t2l, diag_ref, out_ref, modes
+):
+    blocks, _, rows, _ = modes_ref.shape
+    half = half_ref[0]
+    width = out_ref.shape[3]
+
+    def rows_of(sub, _):
+        here = pl.ds(pl.multiple_of(sub * 8, 8), 8)
+        near, far, own, other = join_start(levels, half == 1, diag_ref[here])
+        load = lambda block, outer: modes_ref[chain_place(block, blocks, half), jnp.abs(outer - half), here]
+        alphas, betas, heads, slopes = join_chain(load, blocks, near, far, own)
+        for _ in range(1, blocks):
+            other = near + far * other * (far / (1.0 - near * other))
+        met = alpha_ref[here]
+        outer = (met - other * alphas[-1]) / (1.0 - other * betas[-1])
+        for block in range(blocks - 1, -1, -1):
+            place = chain_place(block, blocks, half)
+            modes[place, 1 - half, here] = outer
+            if block:
+                outer = heads[block] - slopes[block] * outer
+                modes[place, half, here] = alphas[block - 1] - betas[block - 1] * outer
+            else:
+                modes[place, half, here] = jnp.zeros_like(outer)
+        return 0
+
+    lax.fori_loop(0, rows // 8, rows_of, 0)
+    for block in range(blocks):
         for side in range(2):
+            whole = periodic_inverse(modes[block, side], ((t0h, t0l), (t1h, t1l), (t2h, t2l)))
             for i in range(px_count):
-                out_ref[i * py_count + block, side] = modes[block, side, :, i * width : (i + 1) * width]
+                out_ref[i * blocks + block, side] = whole[:, i * width : (i + 1) * width]
 
 
 def spread_kernel(levels, joined_ref, ch, cl, root_ref, start_ref, below_ref, top_ref, end_ref, out_ref, ends_ref, store, total):
@@ -485,14 +514,14 @@
     lane = jnp.where(ids < 0, -1, ids % 128)
     hit = lax.broadcasted_iota(jnp.int32, (count, 128), 1) == lane[:, None]
     own = jnp.stack([jnp.sum(jnp.where(hit, rows, 0.0), axis=1) for rows in near])
-    arrived = lax.all_to_all(own, ("px", "py"), split_axis=1, concat_axis=1, tiled=True)
+    arrived = lax.all_to_all(own, ("px", "py_half", "py_low"), split_axis=1, concat_axis=1, tiled=True)
     w_cell, temp_cell = arrived[0], arrived[1]
     speeds = jnp.sqrt(w_cell * w_cell + 0.25)
     stress = drag_coef * speeds * w_cell
     heat_flux = heat_coef * speeds * (facet_temp - temp_cell)
     new_temp = facet_temp + (net_radiation - heat_flux - 0.5 * facet_temp) / heat_capacity
     returned = lax.all_to_all(
-        jnp.stack([stress, heat_flux]), ("px", "py"), split_axis=1, concat_axis=1, tiled=True
+        jnp.stack([stress, heat_flux]), ("px", "py_half", "py_low"), split_axis=1, concat_axis=1, tiled=True
     )
     same = ids[:, None] == ids[None, :]
     sums = [jnp.sum(jnp.where(same, returned[i][None, :], 0.0), axis=1) for i in range(2)]
@@ -512,10 +541,11 @@
     heat_coef,
 ):
     levels, rows, width = w_star.shape
-    px_count, py_count = lax.axis_size("px"), lax.axis_size("py")
-    devices = px_count * py_count
-    place_x, place_y = lax.axis_index("px"), lax.axis_index("py")
-    own_kx = width // devices
+    px_count, blocks = lax.axis_size("px"), lax.axis_size("py_low")
+    py_count = 2 * blocks
+    group = px_count * blocks
+    place_x, place_y, half = lax.axis_index("px"), lax.axis_index(("py_half", "py_low")), lax.axis_index("py_half")
+    own_kx = width // group
     y_cells = rows * px_count
 
     w_rows = w_star.reshape(levels * rows, width)
@@ -578,7 +608,7 @@
     phases = phase_of[offsets]
     weights = jnp.sum(phases[:, :, :, None, None] * circulant[None, None], axis=2)
 
-    mine = place_x * py_count + place_y
+    mine = place_x * blocks + lax.axis_index("py_low")
     own_sin = lax.dynamic_slice_in_dim(sin_x, mine * own_kx, own_kx)
     diag = -2.0 - own_sin[:, None] - jnp.asarray(sin_y, F32)[None, :]
 
@@ -621,7 +651,7 @@
     )(ids, w_near, w_rows, horiz_div, *x_tables, *to_modes, root, inv, start, top, end)
 
     all_ends = lax.all_gather(ends, "px")
-    packed = jax.ShapeDtypeStruct((devices, 2, own_kx, rows), F32)
+    packed = jax.ShapeDtypeStruct((group, 2, own_kx, rows), F32)
     working = [pltpu.VMEM((levels, 8, width), F32)] * 2
     edges = pl.pallas_call(
         lambda *refs: edge_kernel(levels, *refs),
@@ -643,17 +673,30 @@
         cost_estimate=pl.CostEstimate(flops=temp_rows.size, bytes_accessed=8 * temp_rows.size, transcendentals=0),
         name="theta",
     )(ids, temp_near, temp_rows).reshape(air_temp.shape)
-    edges = lax.all_to_all(edges, ("px", "py"), split_axis=0, concat_axis=0, tiled=True)
+    edges = lax.all_to_all(edges, ("px", "py_low"), split_axis=0, concat_axis=0, tiled=True)
+    half_id = half.astype(jnp.int32).reshape(1)
+    modes, alpha = pl.pallas_call(
+        lambda *refs: gather_modes_kernel(levels, px_count, *refs),
+        out_shape=(
+            jax.ShapeDtypeStruct((blocks, 2, own_kx, y_cells), F32),
+            jax.ShapeDtypeStruct((own_kx, y_cells), F32),
+        ),
+        in_specs=[SMEM] + [VMEM] * 8,
+        out_specs=(VMEM, VMEM),
+        compiler_params=PARAMS,
+        name="gather_modes",
+    )(half_id, edges, *y_tables, diag)
+    alpha = lax.ppermute(alpha, "py_half", [(0, 1), (1, 0)])
     joined = pl.pallas_call(
-        lambda *refs: join_kernel(levels, px_count, py_count, *refs),
+        lambda *refs: join_kernel(levels, px_count, *refs),
         out_shape=packed,
-        in_specs=[VMEM] * 8,
+        in_specs=[SMEM] + [VMEM] * 9,
         out_specs=VMEM,
-        scratch_shapes=[pltpu.VMEM((py_count, 2, own_kx, y_cells), F32)],
+        scratch_shapes=[pltpu.VMEM((blocks, 2, own_kx, y_cells), F32)],
         compiler_params=PARAMS,
         name="join",
-    )(edges, *y_tables, diag)
-    joined = lax.all_to_all(joined, ("px", "py"), split_axis=0, concat_axis=0, tiled=True)
+    )(half_id, modes, alpha, *y_tables, diag)
+    joined = lax.all_to_all(joined, ("px", "py_low"), split_axis=0, concat_axis=0, tiled=True)
     sides, more = pl.pallas_call(
         lambda *refs: spread_kernel(levels, *refs),
         out_shape=(jax.ShapeDtypeStruct((2, rows, width), F32), ends_shape),
@@ -708,22 +751,16 @@
 
 
 def solution(mesh):
-    placed = (
-        P("py", "px", None),
-        P("py", "px", None),
-        P("py", "px", None),
-        P("px", None),
-        P(("px", "py"), None),
-        P(("px", "py"), None),
-        P(("px", "py"), None),
-        P(("px", "py"), None),
-        P(("px", "py"), None),
-        P(("px", "py"), None),
-    )
+    px_count, py_count = mesh.devices.shape
+    split_mesh = jax.sharding.Mesh(
+        mesh.devices.reshape(px_count, 2, py_count // 2), ("px", "py_half", "py_low")
+    )
+    py, every = ("py_half", "py_low"), ("px", "py_half", "py_low")
+    placed = (P(py, "px", None),) * 3 + (P("px", None),) + (P(every, None),) * 6
     return jax.shard_map(
         body,
-        mesh=mesh,
+        mesh=split_mesh,
         in_specs=placed,
-        out_specs=(P("py", "px", None), P("py", "px", None), P(("px", "py"), None)),
+        out_specs=(P(py, "px", None), P(py, "px", None), P(every, None)),
         check_vma=False,
     )

time: 302 us -> 290 us (0.960)
  waiting for transfers between devices: 91.1 us -> 61.2 us
  Pallas kernels: 156 us -> 169 us
    all_to_all x4, waiting for transfers between devices: 91.1 us -> 46.7 us  [the longest x1 26.8 us: body(): lax.all_to_all(edges, ('px', 'py_low'), split_axis=0, concat_axis=0, tile...]
    ppermute x0 -> x1, waiting for transfers between devices: none -> 14.6 us  [body(): alpha = lax.ppermute(alpha, 'py_half', [(0, 1), (1, 0)])]
    pallas_call x1 -> x2, Pallas kernels: 7.93 us -> 21.2 us  [the longest x1 12.1 us: body(): pl.pallas_call(lambda *refs: join_kernel(levels, px_count, *refs), out_sh...]
  transfers between devices with their start and end apart: 4 -> 5, of which waited for: 4 -> 5; matrix products, arithmetic and copies ran while one was open for 2% -> 3% of each run, Pallas kernels for 5% -> 5%
where the time goes in v3:
time: 290 us; the launch traced here: 288 us
  Pallas kernels  169 us (58%)
  waiting for transfers between devices  61.2 us (21%)
  starting transfers between devices  20.2 us (7%)
  blocking collectives  17 us (6%)
  other arithmetic  14.1 us (5%)
  local copies, waits for them, and re-layouts  5.41 us (2%)
    pallas_call x1, Pallas kernels, body(): pl.pallas_call(lambda *refs: forward_kernel(levels, tile, *refs), out_sha...  52.5 us
    pallas_call x1, Pallas kernels, body(): pl.pallas_call(lambda *refs: inverse_kernel(levels, tile, *refs), out_sha...  40.8 us
    all_to_all x1, waiting for transfers between devices, body(): lax.all_to_all(edges, ('px', 'py_low'), split_axis=0, concat_axis=0, tile...  26.8 us
    pallas_call x1, Pallas kernels, near_walls(): pl.pallas_call(gather_kernel, out_shape=(shape, shape), in_specs=[SMEM, H...  20.2 us
    pallas_call x1, Pallas kernels, body(): pl.pallas_call(theta_kernel, out_shape=jax.ShapeDtypeStruct(temp_rows.sha...  15.7 us
    ppermute x1, waiting for transfers between devices, body(): alpha = lax.ppermute(alpha, 'py_half', [(0, 1), (1, 0)])  14.6 us
    all_to_all x1, waiting for transfers between devices, body(): lax.all_to_all(joined, ('px', 'py_low'), split_axis=0, concat_axis=0, til...  12.2 us
    pallas_call x1, Pallas kernels, body(): pl.pallas_call(lambda *refs: join_kernel(levels, px_count, *refs), out_sh...  12.1 us
  transfers between devices with their start and end apart: 5, of which 5 were waited for; matrix products, arithmetic and copies ran while one was open for 3% of the time, Pallas kernels for 5%

profile of v3, /device:TPU:0, one launch (start us, length us, event | category | flops | bytes accessed | tf_op | source)
XLA Modules:
  0.0 288.4 jit_solution(11064147456329759936)
XLA Ops:
  0.6 0.7 compare_select_fusion.3
  1.4 20.2 %facet_gather.1 = (f32[1024,128]{1,0:T(8,128)}, f32[1024,128]{1,0:T(8,128)}) custom-call(s32[1024]{0:T(1024)} %bitcast.24, f32[4096,1024]{1,0:T(8,128)} %bitcast.14, bf16[4096,1024]{1,0:T(8,128)(2,1)} %bitcast.16), custom_call_target="tpu_custom_call" | custom-call | tf_op jit(solution)/shard_map/facet_gather/pallas_call | solution.py:501
  21.7 1.7 select_reduce_fusion
  23.5 0.1 stack.35
  23.6 0.1 stack.34
  23.7 0.7 pad_maximum_fusion.1
  24.3 7.3 %all-to-all-start = ((f32[2,32,32]{2,0,1:T(2,128)}), f32[2,32,32]{2,0,1:T(2,128)S(1)}, u32[]{:S(2)}, u32[]{:S(2)}) async-start(f32[2,32,32]{2,0,1:T(2,128)} %pad_maximum_fusion.1), calls=%async_computation | async-start | bytes 65536 | tf_op jit(solution)/shard_map/all_to_all | solution.py:517
  31.7 0.1 reshape.439
  31.8 0.2 add_divide_fusion.4
  32.0 4.1 %multiply_divide_fusion = (f32[256,1024]{1,0:T(8,128)}, f32[256,1024]{1,0:T(8,128)}, f32[256,1024]{1,0:T(8,128)}, f32[256,1024]{1,0:T(8,128)}, f32[256,1024]{1,0:T(8,128)}) fusion(f32[1024]{0:T(1024)S(1)} %copy-done.5, f32[256]{0:T(256)S(1)} %copy-done.15, pred[]{:T(512)S(6)} %eq.38, pred[]{:T(512)S(6)} %eq.37), kind=kLoop, calls=%fused_computation.39 | loop fusion | flops 14417920 | bytes 5248002 | tf_op jit(solution)/shard_map/div | solution.py:586
  36.1 0.6 select_select_fusion.refs_3_.refs_6_
  36.8 0.6 gather_fusion
  37.3 1.5 all-to-all-done
  38.8 0.1 slice_reduce_fusion.3
  38.9 0.1 slice.21
  39.0 0.1 slice.23
  39.1 0.6 divide_add_fusion
  39.7 0.5 broadcast.554
  40.2 0.7 reduce.27
  40.9 0.1 stack.38
  41.0 0.1 stack.37
  41.1 0.7 pad_maximum_fusion.2
  41.7 4.4 %all-to-all-start.1 = ((f32[2,32,32]{2,0,1:T(2,128)}), f32[2,32,32]{2,0,1:T(2,128)S(1)}, u32[]{:S(2)}, u32[]{:S(2)}) async-start(f32[2,32,32]{2,0,1:T(2,128)} %pad_maximum_fusion.2), calls=%async_computation.1 | async-start | bytes 65536 | tf_op jit(solution)/shard_map/all_to_all | solution.py:523
  46.1 1.1 multiply_reduce_fusion.refs_2_.refs_5_
  47.2 6.1 %all-to-all-done.1 = f32[2,32,32]{2,0,1:T(2,128)S(1)} async-done(((f32[2,32,32]{2,0,1:T(2,128)}), f32[2,32,32]{2,0,1:T(2,128)S(1)}, u32[]{:S(2)}, u32[]{:S(2)}) %all-to-all-start.1) | async-done | bytes 8224 | tf_op jit(solution)/shard_map/all_to_all | solution.py:523
  53.3 0.1 slice_reduce_fusion
  53.5 1.0 fusion.1
  54.5 0.6 add.270.new_ref
  55.1 0.6 sub.130.refs_1_
  55.7 52.5 %forward.1 = (f32[16,256,1024]{2,1,0:T(8,128)}, f32[2,256,1024]{2,1,0:T(8,128)}, f32[2,16,1024]{2,1,0:T(8,128)}, f32[4096,1024]{1,0:T(8,128)}) custom-call(s32[1024]{0:T(1024)} %bitcast.25, f32[1024]{0:T(1024)} %sub.130.refs_1_, f32[4096,1024]{1,0:T(8,128)} %bitcast.15, f32[16,256,1024]{2,1,0:T(8,128)} %refs_3_.3, ...), custom_call_target="tpu_custom_call" | custom-call | tf_op jit(solution)/shard_map/forward/pallas_call | solution.py:624
  108.2 8.0 %all-gather = f32[8,16,1024]{2,1,0:T(8,128)} all-gather(f32[2,16,1024]{2,1,0:T(8,128)} %get-tuple-element.19), channel_id=2, replica_groups=mesh['px'=4,'py_half'=2,'py_low'=4] {'px'}, dimensions={0}, use_global_device_ids=true | all-gather | bytes 655360 | tf_op jit(solution)/shard_map/all_gather | solution.py:653
  116.2 9.8 %edges.1 = f32[16,2,64,256]{3,2,1,0:T(8,128)} custom-call(f32[2,256,1024]{2,1,0:T(8,128)} %get-tuple-element.18.refs_0_, f32[4,2,16,1024]{3,2,1,0:T(8,128)} %bitcast.20, f32[2,4,16,1024]{3,2,1,0:T(8,128)} %multiply_reduce_fusion.refs_2_.refs_5_, f32[16,16]{1,0:T(8,128)} %select_select_fusion.refs_3_.refs_6_, ...), custom_call_target="tpu_custom_call" | custom-call | tf_op jit(solution)/shard_map/edges/pallas_call | solution.py:656
  125.9 4.0 %all-to-all-start.2 = ((f32[16,2,64,256]{3,2,1,0:T(8,128)}), f32[16,2,64,256]{3,2,1,0:T(8,128)S(1)}, u32[]{:S(2)}, u32[]{:S(2)}) async-start(f32[16,2,64,256]{3,2,1,0:T(8,128)} %edges.1), calls=%async_computation.2 | async-start | bytes 4194304 | tf_op jit(solution)/shard_map/all_to_all | solution.py:676
  130.1 0.8 broadcast_add_fusion.refs_8_.refs_9_
  130.9 26.8 %all-to-all-done.2.refs_1_ = f32[16,2,64,256]{3,2,1,0:T(8,128)S(1)} async-done(((f32[16,2,64,256]{3,2,1,0:T(8,128)}), f32[16,2,64,256]{3,2,1,0:T(8,128)S(1)}, u32[]{:S(2)}, u32[]{:S(2)}) %all-to-all-start.2) | async-done | bytes 2097184 | tf_op jit(solution)/shard_map/all_to_all | solution.py:676
  157.7 1.3 copy-done.1
  159.0 9.2 %gather_modes.1 = (f32[4,2,64,1024]{3,2,1,0:T(8,128)}, f32[64,1024]{1,0:T(8,128)}) custom-call(s32[1]{0:T(128)} %bitcast.4.refs_0_, f32[16,2,64,256]{3,2,1,0:T(8,128)} %copy-done.1, bf16[256,256]{1,0:T(8,128)(2,1)} %constant.125.clone.refs_4_.refs_2_.refs_3_.refs_12_, bf16[256,256]{1,0:T(8,128)(2,1)} %constant.126.clone.refs_5_.refs_3_.refs_4_.refs_13_, ...), custom_call_target="tpu_custom_call" | custom-call | tf_op jit(solution)/shard_map/gather_modes/pallas_call | solution.py:678
  168.2 0.7 collective-permute-start
  168.9 14.6 %collective-permute-done.refs_2_ = f32[64,1024]{1,0:T(8,128)S(1)} collective-permute-done((f32[64,1024]{1,0:T(8,128)}, f32[64,1024]{1,0:T(8,128)S(1)}, u32[]{:S(2)}, u32[]{:S(2)}) %collective-permute-start) | collective-permute-done | bytes 262176 | tf_op jit(solution)/shard_map/ppermute | solution.py:689
  183.5 0.7 copy-done.3
  184.2 12.1 %join.1 = f32[16,2,64,256]{3,2,1,0:T(8,128)} custom-call(s32[1]{0:T(128)} %bitcast.4.refs_0_, f32[4,2,64,1024]{3,2,1,0:T(8,128)} %get-tuple-element.21.refs_1_, f32[64,1024]{1,0:T(8,128)} %copy-done.3, bf16[256,256]{1,0:T(8,128)(2,1)} %constant.125.clone.refs_4_.refs_2_.refs_3_.refs_12_, bf16[256,256]{1,0:T(8,128)(2,1)} %constant.126.clone.refs_5_.refs_3_.refs_4_.refs_13_, ...), custom_call_target="tpu_custom_call" | custom-call | tf_op jit(solution)/shard_map/join/pallas_call | solution.py:690
  196.2 3.7 %all-to-all-start.3 = ((f32[16,2,64,256]{3,2,1,0:T(8,128)}), f32[16,2,64,256]{3,2,1,0:T(8,128)S(1)}, u32[]{:S(2)}, u32[]{:S(2)}) async-start(f32[16,2,64,256]{3,2,1,0:T(8,128)} %join.1), calls=%async_computation.3 | async-start | bytes 4194304 | tf_op jit(solution)/shard_map/all_to_all | solution.py:699
  199.9 15.7 %theta.1 = bf16[4096,1024]{1,0:T(8,128)(2,1)} custom-call(s32[1024]{0:T(1024)} %bitcast.26, f32[1024]{0:T(1024)} %add.270.new_ref, bf16[4096,1024]{1,0:T(8,128)(2,1)} %bitcast.17), custom_call_target="tpu_custom_call" | custom-call | flops 4194304 | bytes 33554432 | tf_op jit(solution)/shard_map/theta/pallas_call | solution.py:666
  215.6 12.2 %all-to-all-done.3.refs_0_ = f32[16,2,64,256]{3,2,1,0:T(8,128)S(1)} async-done(((f32[16,2,64,256]{3,2,1,0:T(8,128)}), f32[16,2,64,256]{3,2,1,0:T(8,128)S(1)}, u32[]{:S(2)}, u32[]{:S(2)}) %all-to-all-start.3) | async-done | bytes 2097184 | tf_op jit(solution)/shard_map/all_to_all | solution.py:699
  227.9 1.3 copy-done
  229.2 9.3 %spread.1 = (f32[2,256,1024]{2,1,0:T(8,128)}, f32[2,16,1024]{2,1,0:T(8,128)}) custom-call(f32[16,2,64,256]{3,2,1,0:T(8,128)} %copy-done, bf16[256,256]{1,0:T(8,128)(2,1)} %constant.131.clone.refs_10_.refs_9_.refs_1_, bf16[256,256]{1,0:T(8,128)(2,1)} %constant.132.clone.refs_11_.refs_10_.refs_2_, ...), custom_call_target="tpu_custom_call" | custom-call | tf_op jit(solution)/shard_map/spread/pallas_call | solution.py:700
  238.5 9.0 %all-gather.1 = f32[8,16,1024]{2,1,0:T(8,128)} all-gather(f32[2,16,1024]{2,1,0:T(8,128)} %get-tuple-element.24), channel_id=3, replica_groups=mesh['px'=4,'py_half'=2,'py_low'=4] {'px'}, dimensions={0}, use_global_device_ids=true | all-gather | bytes 655360 | tf_op jit(solution)/shard_map/all_gather | solution.py:709
  247.5 40.8 %inverse.1 = f32[16,256,1024]{2,1,0:T(8,128)} custom-call(s32[1]{0:T(128)} %bitcast.refs_0_, f32[16,256,1024]{2,1,0:T(8,128)} %get-tuple-element.17.refs_1_, f32[2,256,1024]{2,1,0:T(8,128)} %get-tuple-element.23.refs_2_, f32[4,2,16,1024]{3,2,1,0:T(8,128)} %bitcast.21, f32[4,2,16,1024]{3,2,1,0:T(8,128)} %bitcast.22, ...), custom_call_target="tpu_custom_call" | custom-call | tf_op jit(solution)/shard_map/inverse/pallas_call | solution.py:714
  (43 shorter events, 0.4 us)
Async XLA Ops:
  1.3 30.4 %copy-start.16 = (f32[16]{0:T(128)S(1)}, f32[16]{0:T(128)}, u32[]{:S(2)}) copy-start(f32[16]{0:T(128)} %constant.143.clone) | copy-start | bytes 196
  1.3 30.4 %copy-start.17 = (f32[16]{0:T(128)S(1)}, f32[16]{0:T(128)}, u32[]{:S(2)}) copy-start(f32[16]{0:T(128)} %constant.142.clone) | copy-start | bytes 196
  1.3 30.4 %copy-start.18 = (f32[16]{0:T(128)S(1)}, f32[16]{0:T(128)}, u32[]{:S(2)}) copy-start(f32[16]{0:T(128)} %constant.141.clone) | copy-start | bytes 196
  1.3 30.4 %copy-start.5 = (f32[1024]{0:T(1024)S(1)}, f32[1024]{0:T(1024)}, u32[]{:S(2)}) copy-start(f32[1024]{0:T(1024)} %constant.135.clone) | copy-start | bytes 12292
  1.4 30.7 %copy-start.15 = (f32[256]{0:T(256)S(1)}, f32[256]{0:T(256)}, u32[]{:S(2)}) copy-start(f32[256]{0:T(256)} %constant.136.clone) | copy-start | bytes 3076
  21.6 14.5 %copy-start.6 = (f32[16,16]{1,0:T(8,128)S(1)}, f32[16,16]{1,0:T(8,128)}, u32[]{:S(2)}) copy-start(f32[16,16]{1,0:T(8,128)} %constant.140.clone) | copy-start | bytes 3076
  21.6 14.5 %copy-start.7 = (f32[16,16]{1,0:T(8,128)S(1)}, f32[16,16]{1,0:T(8,128)}, u32[]{:S(2)}) copy-start(f32[16,16]{1,0:T(8,128)} %constant.139.clone) | copy-start | bytes 3076
  21.6 14.5 %copy-start.8 = (f32[16,16]{1,0:T(8,128)S(1)}, f32[16,16]{1,0:T(8,128)}, u32[]{:S(2)}) copy-start(f32[16,16]{1,0:T(8,128)} %constant.138.clone) | copy-start | bytes 3076
  21.7 15.1 %copy-start.2 = (f32[4,4]{1,0:T(4,128)S(1)}, f32[4,4]{1,0:T(4,128)}, u32[]{:S(2)}) copy-start(f32[4,4]{1,0:T(4,128)} %constant.144.clone) | copy-start | bytes 196
  21.7 17.4 %copy-start.10 = (f32[1,1024]{1,0:T(1,128)S(1)}, f32[1,1024]{1,0:T(1,128)}, u32[]{:S(2)}) copy-start(f32[1,1024]{1,0:T(1,128)} %param.43) | copy-start | bytes 12292
  21.7 17.4 %copy-start.11 = (f32[1,1024]{1,0:T(1,128)S(1)}, f32[1,1024]{1,0:T(1,128)}, u32[]{:S(2)}) copy-start(f32[1,1024]{1,0:T(1,128)} %param.45) | copy-start | bytes 12292
  21.7 17.4 %copy-start.12 = (f32[1,1024]{1,0:T(1,128)S(1)}, f32[1,1024]{1,0:T(1,128)}, u32[]{:S(2)}) copy-start(f32[1,1024]{1,0:T(1,128)} %param.44) | copy-start | bytes 12292
  21.7 17.4 %copy-start.13 = (f32[1,1024]{1,0:T(1,128)S(1)}, f32[1,1024]{1,0:T(1,128)}, u32[]{:S(2)}) copy-start(f32[1,1024]{1,0:T(1,128)} %param.47) | copy-start | bytes 12292
  21.7 17.4 %copy-start.14 = (f32[1,1024]{1,0:T(1,128)S(1)}, f32[1,1024]{1,0:T(1,128)}, u32[]{:S(2)}) copy-start(f32[1,1024]{1,0:T(1,128)} %param.46) | copy-start | bytes 12292
  21.7 31.8 %copy-start.4 = (s32[1,1024]{1,0:T(1,128)S(1)}, s32[1,1024]{1,0:T(1,128)}, u32[]{:S(2)}) copy-start(s32[1,1024]{1,0:T(1,128)} %param.42) | copy-start | bytes 12292
  24.3 14.5 %all-to-all-start = ((f32[2,32,32]{2,0,1:T(2,128)}), f32[2,32,32]{2,0,1:T(2,128)S(1)}, u32[]{:S(2)}, u32[]{:S(2)}) async-start(f32[2,32,32]{2,0,1:T(2,128)} %pad_maximum_fusion.1), calls=%async_computation | async-start | bytes 65536 | tf_op jit(solution)/shard_map/all_to_all | solution.py:517
  41.7 11.6 %all-to-all-start.1 = ((f32[2,32,32]{2,0,1:T(2,128)}), f32[2,32,32]{2,0,1:T(2,128)S(1)}, u32[]{:S(2)}, u32[]{:S(2)}) async-start(f32[2,32,32]{2,0,1:T(2,128)} %pad_maximum_fusion.2), calls=%async_computation.1 | async-start | bytes 65536 | tf_op jit(solution)/shard_map/all_to_all | solution.py:523
  125.9 4.1 %copy-start.9 = (f32[1024]{0:T(1024)S(1)}, f32[1024]{0:T(1024)}, u32[]{:S(2)}) copy-start(f32[1024]{0:T(1024)} %constant.151) | copy-start | bytes 12292
  125.9 31.8 %all-to-all-start.2 = ((f32[16,2,64,256]{3,2,1,0:T(8,128)}), f32[16,2,64,256]{3,2,1,0:T(8,128)S(1)}, u32[]{:S(2)}, u32[]{:S(2)}) async-start(f32[16,2,64,256]{3,2,1,0:T(8,128)} %edges.1), calls=%async_computation.2 | async-start | bytes 4194304 | tf_op jit(solution)/shard_map/all_to_all | solution.py:676
  157.7 1.3 copy-start.1
  168.2 15.3 %collective-permute-start = (f32[64,1024]{1,0:T(8,128)}, f32[64,1024]{1,0:T(8,128)S(1)}, u32[]{:S(2)}, u32[]{:S(2)}) collective-permute-start(f32[64,1024]{1,0:T(8,128)} %get-tuple-element.22), channel_id=1, source_target_pairs={{0,4},{4,0},{1,5},{5,1},{2,6},{6,2},{3,7},{7,3},{8,12},{12,8},{9,1... | collective-permute-start | bytes 786440 | tf_op jit(solution)/shard_map/ppermute | solution.py:689
  183.5 0.7 copy-start.3
  196.2 31.6 %all-to-all-start.3 = ((f32[16,2,64,256]{3,2,1,0:T(8,128)}), f32[16,2,64,256]{3,2,1,0:T(8,128)S(1)}, u32[]{:S(2)}, u32[]{:S(2)}) async-start(f32[16,2,64,256]{3,2,1,0:T(8,128)} %join.1), calls=%async_computation.3 | async-start | bytes 4194304 | tf_op jit(solution)/shard_map/all_to_all | solution.py:699
  227.8 1.3 copy-start

commit v4 on v3

--- a/solution.py
+++ b/solution.py
@@ -78,7 +78,10 @@
 
 def dot3(left, right, dims=((1,), (0,))):
     one = lambda a, b: lax.dot_general(a, b, (dims, ((), ())), preferred_element_type=F32)
-    return one(left[0], right[0]) + (one(left[1], right[0]) + one(left[0], right[1]))
+    free = 1 - dims[0][0]
+    size = left[0].shape[free]
+    both = one(jnp.concatenate(left, axis=free), right[0])
+    return both[:size] + (both[size:] + one(left[0], right[1]))
 
 
 def read_pair(refs):
@@ -108,6 +111,12 @@
         base = base * base
         exponent >>= 1
     return result
+
+
+def recurrence_root(sine):
+    half = 0.5 * jnp.sqrt(sine)
+    root = jnp.sqrt(1.0 + half * half) - half
+    return root * root
 
 
 def first_sweeps(load, root, top, above, store, levels):
@@ -164,43 +173,51 @@
 
 def forward_kernel(
     levels, tile, ids_ref, w_new_ref, w_hbm, div_ref, t0h, t0l, t1h, t1l, t2h, t2l, ch, cl, root_ref, inv_ref,
-    start_ref, top_ref, end_ref, field_ref, edge_ref, ends_ref, corr_hbm, field, w_rows, above, lowest, store, total,
-    sems,
+    start_ref, top_ref, end_ref, field_hbm, edge_ref, ends_ref, corr_hbm, field, w_rows, above, lowest, store, total,
+    sems, w_sems,
 ):
     step = pl.program_id(0)
     tables = ((t0h, t0l), (t1h, t1l), (t2h, t2l))
 
-    def transform(value):
-        return dot3(read_pair((ch, cl)), split(periodic_forward(value, tables)))
+    pairs = levels // 2
 
     @pl.when(step == 0)
     def _():
-        load = pltpu.make_async_copy(w_hbm, w_rows, sems.at[0])
-        load.start()
+        loads = chunk_copies(w_hbm, w_rows, w_sems)
+        for load in loads:
+            load.start()
         above[...] = jnp.zeros_like(above)
         total[...] = jnp.zeros_like(total)
-        load.wait()
+        for load in loads:
+            load.wait()
         put_cells(ids_ref, w_new_ref, w_rows)
         pltpu.make_async_copy(w_rows, corr_hbm, sems.at[1]).start()
 
     row_count = above.shape[0]
 
-    @pl.when(step < levels)
+    @pl.when(step < pairs)
     def _():
-        value = w_rows[pl.ds(pl.multiple_of((levels - 1 - step) * row_count, row_count), row_count)]
-        field[levels - 1 - step] = transform(div_ref[0] + above[...] - value)
-        above[...] = value
-
-    @pl.when(step == levels - 1)
+        low = pl.multiple_of((pairs - 1 - step) * 2 * row_count, 2 * row_count)
+        value = w_rows[pl.ds(low, 2 * row_count)]
+        lower, upper = value[:row_count], value[row_count:]
+        source = jnp.concatenate([div_ref[0] + (upper - lower), div_ref[1] + (above[...] - upper)], axis=0)
+        modes = periodic_forward(source, tables)
+        for k in range(2):
+            part = modes[k * row_count : (k + 1) * row_count]
+            field[(pairs - 1 - step) * 2 + k] = dot3(read_pair((ch, cl)), split(part))
+        above[...] = lower
+
+    @pl.when(step == pairs - 1)
     def _():
-        lowest[...] = transform(w_rows[:row_count])
-
-    @pl.when(step >= levels)
+        pltpu.make_async_copy(field, field_hbm, sems.at[0]).start()
+        lowest[...] = dot3(read_pair((ch, cl)), split(periodic_forward(w_rows[:row_count], tables)))
+
+    @pl.when(step >= pairs)
     def _():
         def rows_of(sub, _):
             here = pl.multiple_of(sub * 8, 8)
             rows = pl.ds(here, 8)
-            full = pl.ds(pl.multiple_of((step - levels) * tile + here, 8), 8)
+            full = pl.ds(pl.multiple_of((step - pairs) * tile + here, 8), 8)
             root, top = root_ref[rows], top_ref[rows]
             load = lambda level: field[level, full]
             first, _ = first_sweeps(load, root, top, None, store, levels)
@@ -213,8 +230,6 @@
                     edge_ref[1, rows] = value
 
             second_sweeps(load, first * start_ref[rows], root, top, None, store, levels, emit)
-            for level in range(levels):
-                field_ref[level, rows] = load(level)
             return 0
 
         lax.fori_loop(0, tile // 8, rows_of, 0)
@@ -223,6 +238,7 @@
     def _():
         fold_ends(total, ends_ref, levels)
         pltpu.make_async_copy(w_rows, corr_hbm, sems.at[1]).wait()
+        pltpu.make_async_copy(field, field_hbm, sems.at[0]).wait()
 
 
 def edge_kernel(
@@ -249,17 +265,20 @@
         out_ref[:, side] = value.reshape(out_ref.shape[0], out_ref.shape[2], out_ref.shape[3])
 
 
-def join_start(levels, near_top, diag):
-    near = 1.0 / diag
-    far = near
-    ends = [1.0 / (diag + 1.0), 1.0 / (diag - 1.0)]
+def join_start(levels, near_top, root):
+    square = root * root
+    sums = jnp.ones_like(root)
     for _ in range(1, levels):
-        near = 1.0 / (diag - near)
-        far = -far * near
-        ends = [1.0 / (diag - e) for e in ends]
-    own = jnp.where(near_top, ends[1], ends[0])
-    other = jnp.where(near_top, ends[0], ends[1])
-    return (near, far, own, other)
+        sums = 1.0 + square * sums
+    whole = power(root, 2 * levels)
+    one = 1.0 / (sums + whole)
+    near = -root * sums * one
+    far = -power(root, levels) * one
+    part = power(root, 2 * levels - 1)
+    bottom = -root * (1.0 + part) / (1.0 + whole * root)
+    pairs = (1.0 + root) * sums
+    top = -root * (pairs - part) / (pairs + whole)
+    return (near, far, jnp.where(near_top, top, bottom), jnp.where(near_top, bottom, top))
 
 
 def join_chain(load, blocks, near, far, beta):
@@ -282,17 +301,19 @@
     return block + half * (blocks - 1 - 2 * block)
 
 
-def gather_modes_kernel(levels, px_count, half_ref, edge_ref, t0h, t0l, t1h, t1l, t2h, t2l, diag_ref, out_ref, alpha_ref):
+def gather_modes_kernel(levels, px_count, half_ref, edge_ref, t0h, t0l, t1h, t1l, t2h, t2l, root_ref, out_ref, alpha_ref):
     blocks, _, rows, _ = out_ref.shape
     half = half_ref[0]
     for block in range(blocks):
         for side in range(2):
             whole = jnp.concatenate([edge_ref[i * blocks + block, side] for i in range(px_count)], axis=1)
-            out_ref[block, side] = periodic_forward(whole, ((t0h, t0l), (t1h, t1l), (t2h, t2l)))
+            out_ref[block, side] = whole
+    flat = out_ref[...].reshape(blocks * 2 * rows, out_ref.shape[3])
+    out_ref[...] = periodic_forward(flat, ((t0h, t0l), (t1h, t1l), (t2h, t2l))).reshape(out_ref.shape)
 
     def rows_of(sub, _):
         here = pl.ds(pl.multiple_of(sub * 8, 8), 8)
-        near, far, own, _ = join_start(levels, half == 1, diag_ref[here])
+        near, far, own, _ = join_start(levels, half == 1, root_ref[here])
         load = lambda block, outer: out_ref[chain_place(block, blocks, half), jnp.abs(outer - half), here]
         alpha_ref[here] = join_chain(load, blocks, near, far, own)[0][-1]
         return 0
@@ -301,7 +322,7 @@
 
 
 def join_kernel(
-    levels, px_count, half_ref, modes_ref, alpha_ref, t0h, t0l, t1h, t1l, t2h, t2l, diag_ref, out_ref, modes
+    levels, px_count, half_ref, modes_ref, alpha_ref, t0h, t0l, t1h, t1l, t2h, t2l, root_ref, out_ref, modes
 ):
     blocks, _, rows, _ = modes_ref.shape
     half = half_ref[0]
@@ -309,7 +330,7 @@
 
     def rows_of(sub, _):
         here = pl.ds(pl.multiple_of(sub * 8, 8), 8)
-        near, far, own, other = join_start(levels, half == 1, diag_ref[here])
+        near, far, own, other = join_start(levels, half == 1, root_ref[here])
         load = lambda block, outer: modes_ref[chain_place(block, blocks, half), jnp.abs(outer - half), here]
         alphas, betas, heads, slopes = join_chain(load, blocks, near, far, own)
         for _ in range(1, blocks):
@@ -327,11 +348,12 @@
         return 0
 
     lax.fori_loop(0, rows // 8, rows_of, 0)
+    flat = modes[...].reshape(blocks * 2 * rows, modes.shape[3])
+    whole = periodic_inverse(flat, ((t0h, t0l), (t1h, t1l), (t2h, t2l))).reshape(modes.shape)
     for block in range(blocks):
         for side in range(2):
-            whole = periodic_inverse(modes[block, side], ((t0h, t0l), (t1h, t1l), (t2h, t2l)))
             for i in range(px_count):
-                out_ref[i * blocks + block, side] = whole[:, i * width : (i + 1) * width]
+                out_ref[i * blocks + block, side] = whole[block, side, :, i * width : (i + 1) * width]
 
 
 def spread_kernel(levels, joined_ref, ch, cl, root_ref, start_ref, below_ref, top_ref, end_ref, out_ref, ends_ref, store, total):
@@ -363,7 +385,7 @@
     below_ref, top_ref, end_ref, t0h, t0l, t1h, t1l, t2h, t2l, ch, cl, w_ref, roof_ref, out_ref, field, pattern, store,
 ):
     step = pl.program_id(0)
-    tiles = pl.num_programs(0) - levels
+    tiles = pl.num_programs(0) - levels // 2
     tables = ((t0h, t0l), (t1h, t1l), (t2h, t2l))
 
     @pl.when(step == 0)
@@ -400,80 +422,129 @@
 
     @pl.when(step >= tiles)
     def _():
-        level = step - tiles
-        rows_y = dot3(read_pair((ch, cl)), split(field[level]))
-        slope = periodic_inverse(rows_y, tables)
-        solid = place_ref[0] * levels + level < roof_ref[...]
-        out_ref[0] = jnp.where(solid, 0.0, w_ref[0] - slope)
-
-
-def divide(value, size):
-    if size & (size - 1):
-        return lax.div(value, size)
-    return lax.shift_right_logical(value, size.bit_length() - 1)
-
-
-def remainder(value, size):
-    return lax.rem(value, size) if size & (size - 1) else value & (size - 1)
-
-
-def tile_at(cell, width, tall):
-    row, column = divide(cell, width), remainder(cell, width)
+        level = (step - tiles) * 2
+        rows_y = [dot3(read_pair((ch, cl)), split(field[level + k])) for k in range(2)]
+        slope = periodic_inverse(jnp.concatenate(rows_y, axis=0), tables)
+        count = roof_ref.shape[0]
+        for k in range(2):
+            solid = place_ref[0] * levels + level + k < roof_ref[...]
+            out_ref[k] = jnp.where(solid, 0.0, w_ref[k] - slope[k * count : (k + 1) * count])
+
+
+def facet_places(ids, width):
+    safe = jnp.maximum(ids, 0)
+    row, column = safe // width, safe % width
+    return jnp.stack([row // 8, column // 128, jnp.where(ids < 0, -1, row % 8 * 128 + column % 128)])
+
+
+def tile_at(places_ref, facet):
     return (
-        pl.ds(pl.multiple_of(divide(row, tall) * tall, tall), tall),
-        pl.ds(pl.multiple_of(divide(column, 128) * 128, 128), 128),
-    )
-
-
-def gather_kernel(ids_ref, w_hbm, temp_hbm, w_out, temp_out, w_ref, temp_ref, sems):
-    copies = [
-        pltpu.make_async_copy(w_hbm, w_ref, sems.at[0]),
-        pltpu.make_async_copy(temp_hbm, temp_ref, sems.at[1]),
-    ]
-    for copy in copies:
-        copy.start()
-    width = w_ref.shape[1]
+        pl.ds(pl.multiple_of(places_ref[0, facet] * 8, 8), 8),
+        pl.ds(pl.multiple_of(places_ref[1, facet] * 128, 128), 128),
+    )
+
+
+def pair_at(places_ref, facet):
+    return (
+        pl.ds(pl.multiple_of(lax.shift_right_logical(places_ref[0, facet], 1) * 16, 16), 16),
+        pl.ds(pl.multiple_of(places_ref[1, facet] * 128, 128), 128),
+    )
+
+
+def pick_cells(ids_ref, ref, rows_ref, flat_ref):
     sublane = lax.broadcasted_iota(jnp.int32, (8, 128), 0)
-
-    def pick(i, ref, out):
+    position = sublane * 128 + lax.broadcasted_iota(jnp.int32, (8, 128), 1)
+
+    def pick(i, _):
         rows = None
         for lane in range(8):
-            cell = jnp.maximum(ids_ref[i * 8 + lane], 0)
-            row = divide(cell, width)
+            facet = i * 8 + lane
+            mark = ids_ref[2, facet]
             if ref.dtype == F32:
-                tile = ref[tile_at(cell, width, 8)]
+                tile = ref[tile_at(ids_ref, facet)]
             else:
-                both = ref[tile_at(cell, width, 16)].astype(F32)
-                tile = jnp.where(remainder(row, 16) < 8, both[:8], both[8:])
-            tile = pltpu.roll(tile, remainder(lane + 8 - remainder(row, 8), 8), 0)
+                both = ref[pair_at(ids_ref, facet)].astype(F32)
+                tile = jnp.where(ids_ref[0, facet] & 1 == 0, both[:8], both[8:])
+            tile = jnp.where(position == mark, tile, 0.0)
+            tile = pltpu.roll(tile, (lane - lax.shift_right_arithmetic(mark, 7)) & 7, 0)
             rows = tile if rows is None else jnp.where(sublane == lane, tile, rows)
-        out[pl.ds(pl.multiple_of(i * 8, 8), 8)] = rows
+        rows_ref[pl.ds(pl.multiple_of(i * 8, 8), 8)] = rows
         return 0
 
-    groups = ids_ref.shape[0] // 8
-    copies[0].wait()
-    lax.fori_loop(0, groups, lambda i, _: pick(i, w_ref, w_out), 0)
-    copies[1].wait()
-    lax.fori_loop(0, groups, lambda i, _: pick(i, temp_ref, temp_out), 0)
+    lax.fori_loop(0, rows_ref.shape[0] // 8, pick, 0)
+    ones = jnp.ones((8, 128), F32)
+    for group in range(flat_ref.shape[0]):
+        rows = rows_ref[group * 128 : (group + 1) * 128]
+        flat = lax.dot_general(
+            ones, rows, (((1,), (1,)), ((), ())), precision=lax.Precision.HIGHEST, preferred_element_type=F32
+        )
+        flat_ref[group : group + 1] = flat[:1]
+
+
+def level_solve_tables(sine, levels, is_first, is_last):
+    root = recurrence_root(sine)
+    top = jnp.where(is_last, root / (1.0 + root), 0.0)
+    square = root * root
+    kappa = jnp.zeros_like(root)
+    for _ in range(levels):
+        kappa = square * (1.0 + kappa)
+    decay = power(root, levels)
+    inverse = 1.0 / root
+    bottom = jnp.where(is_first, 1.0 - inverse, 1.0)
+    inv = 1.0 / (1.0 + bottom * (kappa - top * decay * decay))
+    return (root, inv, bottom * inv, inv * inverse, top)
+
+
+CHUNKS = 8
+
+
+def chunk_copies(source, target, sems):
+    rows = source.shape[0] // CHUNKS
+    parts = [pl.ds(i * rows, rows) for i in range(CHUNKS)]
+    return [pltpu.make_async_copy(source.at[p], target.at[p], sems.at[i]) for i, p in enumerate(parts)]
+
+
+def gather_kernel(
+    levels, ids_ref, ends_ref, w_hbm, temp_hbm, sin_x_ref, sin_y_ref, out_ref, o0, o1, o2, o3, o4, rows_ref, w_ref,
+    temp_ref, tables, sems, w_sems, temp_sems,
+):
+    w_parts, temp_parts = chunk_copies(w_hbm, w_ref, w_sems), chunk_copies(temp_hbm, temp_ref, temp_sems)
+    for copy in w_parts:
+        copy.start()
+
+    def fill(i, _):
+        rows = pl.ds(pl.multiple_of(i * 8, 8), 8)
+        sine = sin_y_ref[rows, :1] + sin_x_ref[...]
+        for k, value in enumerate(level_solve_tables(sine, levels, ends_ref[0] == 1, ends_ref[1] == 1)):
+            tables[k, rows] = value
+        return 0
+
+    lax.fori_loop(0, sin_y_ref.shape[0] // 8, fill, 0)
+    leaving = [pltpu.make_async_copy(tables.at[k], o, sems.at[k]) for k, o in enumerate((o0, o1, o2, o3, o4))]
+    for copy in w_parts:
+        copy.wait()
+    for copy in temp_parts + leaving:
+        copy.start()
+    pick_cells(ids_ref, w_ref, rows_ref, out_ref.at[0])
+    for copy in temp_parts:
+        copy.wait()
+    pick_cells(ids_ref, temp_ref, rows_ref, out_ref.at[1])
+    for copy in leaving:
+        copy.wait()
 
 
 def put_cells(ids_ref, new_ref, out):
-    width = out.shape[1]
     sublane = lax.broadcasted_iota(jnp.int32, (8, 128), 0)
-    lane = lax.broadcasted_iota(jnp.int32, (8, 128), 1)
-    position = sublane * 128 + lane
+    position = sublane * 128 + lax.broadcasted_iota(jnp.int32, (8, 128), 1)
 
     def put(i, _):
         for k in range(8):
             facet = i * 8 + k
-            cell = ids_ref[facet]
-            safe = jnp.maximum(cell, 0)
-            at = remainder(divide(safe, width), 8) * 128 + remainder(safe, 128)
-            hit = position == jnp.where(cell < 0, -1, at)
-            pltpu.store(out.at[tile_at(safe, width, 8)], jnp.full((8, 128), new_ref[facet]), mask=hit)
+            hit = position == ids_ref[2, facet]
+            pltpu.store(out.at[tile_at(ids_ref, facet)], jnp.full((8, 128), new_ref[facet]), mask=hit)
         return 0
 
-    lax.fori_loop(0, ids_ref.shape[0] // 8, put, 0)
+    lax.fori_loop(0, new_ref.shape[0] // 8, put, 0)
 
 
 def theta_kernel(ids_ref, new_ref, temp_ref, out_ref, wide):
@@ -495,37 +566,124 @@
     lax.fori_loop(0, rows // chunk, narrow, 0)
 
 
-def near_walls(w_rows, temp_rows, ids, facet_temp, net_radiation, heat_capacity, drag_coef, heat_coef):
+def by_owner(flat, slots):
+    shares = 128 // slots
+    return jnp.stack([pltpu.roll(flat, (128 - k * slots) % 128, 1) if k else flat for k in range(shares)])
+
+
+def exchange_kernel(
+    sizes, slots, own_ref, facet_ref, radiation_ref, capacity_ref, drag_ref, heat_ref, back_ref, new_ref, sample, got,
+    flux, back, sent, received,
+):
+    names = ("px", "py_half", "py_low")
+    count = sizes[0] * sizes[1] * sizes[2]
+    shares = 128 // slots
+    places = [lax.axis_index(name) for name in names]
+    me = (places[0] * sizes[1] + places[1]) * sizes[2] + places[2]
+
+    def each_peer(act):
+        def one(step, _):
+            low = lax.rem(places[2] + step, sizes[2])
+            rest = lax.div(step, sizes[2])
+            middle = lax.rem(places[1] + rest, sizes[1])
+            first = lax.rem(places[0] + lax.div(rest, sizes[1]), sizes[0])
+            act((first * sizes[1] + middle) * sizes[2] + low, (first, middle, low))
+            return 0
+
+        lax.fori_loop(1, count, one, 0)
+
+    def at(ref, device):
+        return ref.at[lax.rem(device, shares), lax.div(device, shares)]
+
+    def copy(phase, source, target, peer, device, landing):
+        return pltpu.make_async_remote_copy(
+            at(source, peer),
+            at(target, landing),
+            sent.at[phase, peer],
+            received.at[phase, landing],
+            device_id=device,
+            device_id_type=pl.DeviceIdType.MESH,
+        )
+
+    def start(phase, source, target):
+        each_peer(lambda peer, device: copy(phase, source, target, peer, device, me).start())
+
+    def finish(phase, source, target):
+        each_peer(lambda peer, device: copy(phase, source, target, peer, device, peer).wait())
+
+    barrier = pltpu.get_barrier_semaphore()
+    each_peer(
+        lambda peer, device: pl.semaphore_signal(
+            barrier, inc=1, device_id=device, device_id_type=pl.DeviceIdType.MESH
+        )
+    )
+    for i in range(2):
+        sample[:, :, i] = by_owner(own_ref[i], slots)
+    pl.semaphore_wait(barrier, count - 1)
+    start(0, sample, got)
+    mine = (lax.rem(me, shares), lax.div(me, shares))
+    got[mine] = sample[mine]
+    facet, radiation, capacity, drag, heat = [
+        by_owner(ref[...], slots) for ref in (facet_ref, radiation_ref, capacity_ref, drag_ref, heat_ref)
+    ]
+    finish(0, sample, got)
+    w_cell, temp_cell = got[:, :, 0], got[:, :, 1]
+    speeds = jnp.sqrt(w_cell * w_cell + 0.25)
+    heat_flux = heat * speeds * (facet - temp_cell)
+    flux[:, :, 0] = drag * speeds * w_cell
+    flux[:, :, 1] = heat_flux
+    start(1, flux, back)
+    back[mine] = flux[mine]
+    new_temp = facet + (radiation - heat_flux - 0.5 * facet) / capacity
+    finish(1, flux, back)
+    lane = lax.broadcasted_iota(jnp.int32, new_temp.shape[1:], 1)
+    for target, parts in ((new_ref, new_temp), (back_ref.at[0], back[:, :, 0]), (back_ref.at[1], back[:, :, 1])):
+        total = None
+        for k in range(shares):
+            part = jnp.where(lane < slots, parts[k], 0.0)
+            part = pltpu.roll(part, k * slots, 1) if k else part
+            total = part if total is None else total + part
+        target[...] = total
+
+
+def near_walls(w_rows, temp_rows, sin_x, sin_y, ends, ids, places, facet_temp, net_radiation, heat_capacity, drag_coef, heat_coef):
     count = ids.shape[0]
-    shape = jax.ShapeDtypeStruct((count, 128), F32)
-    near = pl.pallas_call(
-        gather_kernel,
-        out_shape=(shape, shape),
-        in_specs=[SMEM, HBM, HBM],
-        out_specs=(VMEM, VMEM),
+    sizes = tuple(lax.axis_size(name) for name in ("px", "py_half", "py_low"))
+    slots = count // (sizes[0] * sizes[1] * sizes[2])
+    flat = (count // 128, 128)
+    rows, width = sin_y.shape[0], sin_x.shape[1]
+    own, *tables = pl.pallas_call(
+        lambda *refs: gather_kernel(w_rows.shape[0] // rows, *refs),
+        out_shape=[jax.ShapeDtypeStruct((2, *flat), F32)] + [jax.ShapeDtypeStruct((rows, width), F32)] * 5,
+        in_specs=[SMEM, SMEM, HBM, HBM, VMEM, VMEM],
+        out_specs=[VMEM] + [HBM] * 5,
         scratch_shapes=[
+            pltpu.VMEM((count, 128), F32),
             pltpu.VMEM(w_rows.shape, F32),
             pltpu.VMEM(temp_rows.shape, BF16),
-            pltpu.SemaphoreType.DMA((2,)),
+            pltpu.VMEM((5, rows, width), F32),
+            pltpu.SemaphoreType.DMA((5,)),
+            pltpu.SemaphoreType.DMA((CHUNKS,)),
+            pltpu.SemaphoreType.DMA((CHUNKS,)),
         ],
         compiler_params=PARAMS,
         name="facet_gather",
-    )(ids, w_rows, temp_rows)
-    lane = jnp.where(ids < 0, -1, ids % 128)
-    hit = lax.broadcasted_iota(jnp.int32, (count, 128), 1) == lane[:, None]
-    own = jnp.stack([jnp.sum(jnp.where(hit, rows, 0.0), axis=1) for rows in near])
-    arrived = lax.all_to_all(own, ("px", "py_half", "py_low"), split_axis=1, concat_axis=1, tiled=True)
-    w_cell, temp_cell = arrived[0], arrived[1]
-    speeds = jnp.sqrt(w_cell * w_cell + 0.25)
-    stress = drag_coef * speeds * w_cell
-    heat_flux = heat_coef * speeds * (facet_temp - temp_cell)
-    new_temp = facet_temp + (net_radiation - heat_flux - 0.5 * facet_temp) / heat_capacity
-    returned = lax.all_to_all(
-        jnp.stack([stress, heat_flux]), ("px", "py_half", "py_low"), split_axis=1, concat_axis=1, tiled=True
-    )
+    )(places, ends, w_rows, temp_rows, sin_x, sin_y)
+    tall = (128 // slots, flat[0], 2, 128)
+    devices = sizes[0] * sizes[1] * sizes[2]
+    returned, new_temp = pl.pallas_call(
+        lambda *refs: exchange_kernel(sizes, slots, *refs),
+        out_shape=(jax.ShapeDtypeStruct((2, *flat), F32), jax.ShapeDtypeStruct(flat, F32)),
+        in_specs=[VMEM] * 6,
+        out_specs=(VMEM, VMEM),
+        scratch_shapes=[pltpu.VMEM(tall, F32)] * 4 + [pltpu.SemaphoreType.DMA((2, devices))] * 2,
+        compiler_params=pltpu.CompilerParams(collective_id=1, has_side_effects=True),
+        name="facet_exchange",
+    )(own, *[a.reshape(flat) for a in (facet_temp, net_radiation, heat_capacity, drag_coef, heat_coef)])
+    own, returned = own.reshape(2, count), returned.reshape(2, count)
     same = ids[:, None] == ids[None, :]
     sums = [jnp.sum(jnp.where(same, returned[i][None, :], 0.0), axis=1) for i in range(2)]
-    return (own[0] - sums[0], own[1] + sums[1], new_temp)
+    return (own[0] - sums[0], own[1] + sums[1], new_temp.reshape(count), tables)
 
 
 def body(
@@ -551,17 +709,7 @@
     w_rows = w_star.reshape(levels * rows, width)
     temp_rows = air_temp.reshape(levels * rows, width)
     ids = facet_cells[0]
-    w_near, temp_near, new_temp = near_walls(
-        w_rows,
-        temp_rows,
-        ids,
-        facet_temp[0],
-        net_radiation[0],
-        heat_capacity[0],
-        drag_coef[0],
-        heat_coef[0],
-    )
-
+    places = facet_places(ids, width)
     x_parts, sin_x = periodic_tables(width)
     y_parts, sin_y = periodic_tables(y_cells)
     cosines, sin_block = cosine_table(rows)
@@ -570,20 +718,22 @@
     to_modes, to_rows = two_halves(cosines), two_halves(np.ascontiguousarray(cosines.T))
     sin_x = jnp.asarray(sin_x, F32)
 
-    sine = jnp.asarray(sin_block, F32)[:, None] + sin_x[None, :]
-    half_root = 0.5 * jnp.sqrt(sine)
-    root = jnp.sqrt(1.0 + half_root * half_root) - half_root
-    root = root * root
     is_first, is_last = place_y == 0, place_y == py_count - 1
-    top = jnp.where(is_last, root / (1.0 + root), 0.0)
-    kappa = jnp.zeros_like(root)
-    for _ in range(levels):
-        kappa = root * root * (1.0 + kappa)
-    decay = power(root, levels)
-    bottom = jnp.where(is_first, 1.0 - 1.0 / root, 1.0)
-    inv = 1.0 / (1.0 + bottom * (kappa - top * decay * decay))
-    start = bottom * inv
-    from_below = inv / root
+    w_near, temp_near, new_temp, (root, inv, start, from_below, top) = near_walls(
+        w_rows,
+        temp_rows,
+        sin_x[None, :],
+        jnp.asarray(np.repeat(sin_block[:, None], 128, axis=1), F32),
+        jnp.stack([is_first, is_last]).astype(jnp.int32),
+        ids,
+        places,
+        facet_temp[0],
+        net_radiation[0],
+        heat_capacity[0],
+        drag_coef[0],
+        heat_coef[0],
+    )
+
     end = np.where(np.arange(rows) == 0, np.sqrt(1.0 / rows), cosines[:, 0])
     end = jnp.asarray(np.repeat(end[:, None], 128, axis=1), F32)
 
@@ -603,6 +753,7 @@
     circulant = jnp.stack(
         [1.0 / (1.0 - 2.0 * same_end + 2.0 * math.cos(2.0 * math.pi * s / px_count) * far_end) for s in turns]
     )
+    circulant = lax.optimization_barrier(circulant)
     phase_of = jnp.asarray(np.cos(2.0 * np.pi * turns[:, None] * turns[None, :] / px_count) / px_count, F32)
     offsets = jnp.stack([(place_x - turns) % px_count, (place_x - 1 - turns) % px_count])
     phases = phase_of[offsets]
@@ -610,15 +761,16 @@
 
     mine = place_x * blocks + lax.axis_index("py_low")
     own_sin = lax.dynamic_slice_in_dim(sin_x, mine * own_kx, own_kx)
-    diag = -2.0 - own_sin[:, None] - jnp.asarray(sin_y, F32)[None, :]
+    join_root = recurrence_root(own_sin[:, None] + jnp.asarray(sin_y, F32)[None, :])
 
     tile = math.gcd(rows, 32)
     tiles = rows // tile
     flat = lambda i: pl.BlockSpec((tile, width), i)
     fixed = lambda a: pl.BlockSpec(a.shape, lambda i: (0,) * a.ndim)
-    late = lambda i: (jnp.maximum(i - levels, 0), 0)
-    down = lambda i: (jnp.maximum(levels - 1 - i, 0), 0, 0)
-    slab = pl.BlockSpec((1, rows, width), down)
+    pairs = levels // 2
+    late = lambda i: (jnp.maximum(i - pairs, 0), 0)
+    down = lambda i: (jnp.maximum(pairs - 1 - i, 0), 0, 0)
+    slab = pl.BlockSpec((2, rows, width), down)
     end_late = pl.BlockSpec((tile, 128), late)
     ends_shape = jax.ShapeDtypeStruct((2, levels, width), F32)
     field, edges, ends, w_corr = pl.pallas_call(
@@ -629,10 +781,10 @@
             ends_shape,
             jax.ShapeDtypeStruct(w_rows.shape, F32),
         ),
-        grid=(levels + tiles,),
+        grid=(pairs + tiles,),
         in_specs=[SMEM, SMEM, HBM, slab] + [fixed(t) for t in (*x_tables, *to_modes)] + [flat(late)] * 4 + [end_late],
         out_specs=(
-            pl.BlockSpec((levels, tile, width), lambda i: (0, *late(i))),
+            HBM,
             pl.BlockSpec((2, tile, width), lambda i: (0, *late(i))),
             fixed(ends_shape),
             HBM,
@@ -645,10 +797,11 @@
             pltpu.VMEM((levels, 8, width), F32),
             pltpu.VMEM((levels, 8, width), F32),
             pltpu.SemaphoreType.DMA((2,)),
+            pltpu.SemaphoreType.DMA((CHUNKS,)),
         ],
         compiler_params=PARAMS,
         name="forward",
-    )(ids, w_near, w_rows, horiz_div, *x_tables, *to_modes, root, inv, start, top, end)
+    )(places, w_near, w_rows, horiz_div, *x_tables, *to_modes, root, inv, start, top, end)
 
     all_ends = lax.all_gather(ends, "px")
     packed = jax.ShapeDtypeStruct((group, 2, own_kx, rows), F32)
@@ -672,7 +825,7 @@
         compiler_params=PARAMS,
         cost_estimate=pl.CostEstimate(flops=temp_rows.size, bytes_accessed=8 * temp_rows.size, transcendentals=0),
         name="theta",
-    )(ids, temp_near, temp_rows).reshape(air_temp.shape)
+    )(places, temp_near, temp_rows).reshape(air_temp.shape)
     edges = lax.all_to_all(edges, ("px", "py_low"), split_axis=0, concat_axis=0, tiled=True)
     half_id = half.astype(jnp.int32).reshape(1)
     modes, alpha = pl.pallas_call(
@@ -685,7 +838,7 @@
         out_specs=(VMEM, VMEM),
         compiler_params=PARAMS,
         name="gather_modes",
-    )(half_id, edges, *y_tables, diag)
+    )(half_id, edges, *y_tables, join_root)
     alpha = lax.ppermute(alpha, "py_half", [(0, 1), (1, 0)])
     joined = pl.pallas_call(
         lambda *refs: join_kernel(levels, px_count, *refs),
@@ -695,7 +848,7 @@
         scratch_shapes=[pltpu.VMEM((blocks, 2, own_kx, y_cells), F32)],
         compiler_params=PARAMS,
         name="join",
-    )(half_id, modes, alpha, *y_tables, diag)
+    )(half_id, modes, alpha, *y_tables, join_root)
     joined = lax.all_to_all(joined, ("px", "py_low"), split_axis=0, concat_axis=0, tiled=True)
     sides, more = pl.pallas_call(
         lambda *refs: spread_kernel(levels, *refs),
@@ -710,11 +863,11 @@
 
     early = lambda i: (jnp.minimum(i, tiles - 1), 0)
     up = lambda i: (jnp.maximum(i - tiles, 0), 0, 0)
-    slab = pl.BlockSpec((1, rows, width), up)
+    slab = pl.BlockSpec((2, rows, width), up)
     w_new = pl.pallas_call(
         lambda *refs: inverse_kernel(levels, tile, *refs),
         out_shape=jax.ShapeDtypeStruct(w_star.shape, F32),
-        grid=(tiles + levels,),
+        grid=(tiles + pairs,),
         in_specs=[
             SMEM,
             pl.BlockSpec((levels, tile, width), lambda i: (0, *early(i))),

time: 290 us -> 274 us (0.945)
  starting transfers between devices: 20.2 us -> 8.3 us
  Pallas kernels: 169 us -> 178 us
  waiting for transfers between devices: 61.2 us -> 54.4 us
  other arithmetic: 14.1 us -> 9.19 us
    pallas_call x1 -> x2, Pallas kernels: 20.2 us -> 44.8 us  [the longest x1 25.5 us: near_walls(): pl.pallas_call(lambda *refs: gather_kernel(w_rows.shape[0] // rows, *refs...]
    all_to_all x2 -> x0, starting transfers between devices: 11.7 us -> none  [the longest x1 7.3 us: near_walls(): lax.all_to_all(own, ('px', 'py_half', 'py_low'), split_axis=1, concat_axi...]
    all_to_all x2 -> x0, waiting for transfers between devices: 7.57 us -> none  [the longest x1 6.11 us: near_walls(): lax.all_to_all(jnp.stack([stress, heat_flux]), ('px', 'py_half', 'py_low'...]
    pallas_call x1, Pallas kernels: 12.1 us -> 6.55 us  [body(): pl.pallas_call(lambda *refs: join_kernel(levels, px_count, *refs), out_sh...]
    div x1 -> x0, other arithmetic: 4.1 us -> none  [body(): from_below = inv / root]
    pallas_call x1, Pallas kernels: 52.5 us -> 48.6 us  [body(): pl.pallas_call(lambda *refs: forward_kernel(levels, tile, *refs), out_sha...]
    pallas_call x1, Pallas kernels: 9.15 us -> 5.96 us  [body(): pl.pallas_call(lambda *refs: gather_modes_kernel(levels, px_count, *refs)...]
  transfers between devices with their start and end apart: 5 -> 3, of which waited for: 5 -> 3; matrix products, arithmetic and copies ran while one was open for 3% -> 0% of each run, Pallas kernels for 5% -> 5%
where the time goes in v4:
time: 274 us; the launch traced here: 273 us
  Pallas kernels  178 us (65%)
  waiting for transfers between devices  54.4 us (20%)
  blocking collectives  17.3 us (6%)
  other arithmetic  9.19 us (3%)
  starting transfers between devices  8.3 us (3%)
  local copies, waits for them, and re-layouts  5.36 us (2%)
    pallas_call x1, Pallas kernels, body(): pl.pallas_call(lambda *refs: forward_kernel(levels, tile, *refs), out_sha...  48.6 us
    pallas_call x1, Pallas kernels, body(): pl.pallas_call(lambda *refs: inverse_kernel(levels, tile, *refs), out_sha...  38 us
    all_to_all x1, waiting for transfers between devices, body(): lax.all_to_all(edges, ('px', 'py_low'), split_axis=0, concat_axis=0, tile...  26.7 us
    pallas_call x1, Pallas kernels, near_walls(): pl.pallas_call(lambda *refs: gather_kernel(w_rows.shape[0] // rows, *refs...  25.5 us
    pallas_call x1, Pallas kernels, near_walls(): pl.pallas_call(lambda *refs: exchange_kernel(sizes, slots, *refs), out_sh...  19.4 us
    pallas_call x1, Pallas kernels, body(): pl.pallas_call(theta_kernel, out_shape=jax.ShapeDtypeStruct(temp_rows.sha...  14.9 us
    ppermute x1, waiting for transfers between devices, body(): alpha = lax.ppermute(alpha, 'py_half', [(0, 1), (1, 0)])  14.7 us
    all_to_all x1, waiting for transfers between devices, body(): lax.all_to_all(joined, ('px', 'py_low'), split_axis=0, concat_axis=0, til...  13 us
  transfers between devices with their start and end apart: 3, of which 3 were waited for; matrix products, arithmetic and copies ran while one was open for 0% of the time, Pallas kernels for 5%

profile of v4, /device:TPU:0, one launch (start us, length us, event | category | flops | bytes accessed | tf_op | source)
XLA Modules:
  0.0 273.4 jit_solution(17304247137748268173)
XLA Ops:
  0.7 0.1 reshape.391
  0.8 0.8 and_select_fusion.4
  1.5 0.7 compare_select_fusion.2
  2.3 0.7 broadcast_select_fusion.1
  3.0 0.9 add_divide_fusion.3
  3.9 0.6 add_convert_fusion.refs_1_
  4.5 0.6 pad_add_fusion.refs_0_.ids_ref
  5.1 0.0 copy-start.4
  5.1 25.5 %facet_gather.1 = (f32[2,8,128]{2,1,0:T(8,128)}, f32[256,1024]{1,0:T(8,128)}, f32[256,1024]{1,0:T(8,128)}, f32[256,1024]{1,0:T(8,128)}, f32[256,1024]{1,0:T(8,128)}, /*index=5*/f32[256,1024]{1,0:T(8,128)}) custom-call(s32[3,1024]{1,0:T(4,128)} %pad_add_fusion.refs_0_.ids_ref, s32[2]{0:T(128)} %add_convert_fusion.refs_1_, f32[4096,1024]{1,0:T(8,128)} %bitcast.30, ...), custom_call_target="tpu_custom_call" | custom-call | tf_op jit(solution)/shard_map/facet_gather/pallas_call | solution.py:655
  30.6 19.4 %facet_exchange.1 = (f32[2,8,128]{2,1,0:T(8,128)}, f32[8,128]{1,0:T(8,128)}) custom-call(f32[2,8,128]{2,1,0:T(8,128)} %get-tuple-element.21.refs_0_, f32[8,128]{1,0:T(8,128)} %bitcast.41, f32[8,128]{1,0:T(8,128)} %bitcast.42, f32[8,128]{1,0:T(8,128)} %bitcast.43, f32[8,128]{1,0:T(8,128)} %bitcast.44, f32[8,128]{1,0:T(8,128)} %bitcast.45), custom_call_target="tpu_custom_call" | custom-call | tf_op jit(solution)/shard_map/facet_exchange/pallas_call | solution.py:674
  49.9 0.7 slice_bitcast_fusion.1
  50.6 0.0 copy-done.4
  50.6 1.0 fusion.1
  51.6 1.3 bitcast_add_fusion
  52.9 0.0 copy-start.2
  52.9 0.0 copy-start.6
  52.9 0.0 copy-start.7
  52.9 0.0 copy-start.8
  52.9 48.6 %forward.1 = (f32[16,256,1024]{2,1,0:T(8,128)}, f32[2,256,1024]{2,1,0:T(8,128)}, f32[2,16,1024]{2,1,0:T(8,128)}, f32[4096,1024]{1,0:T(8,128)}) custom-call(s32[3,1024]{1,0:T(4,128)} %pad_add_fusion.refs_0_.ids_ref, f32[1024]{0:T(1024)} %get-tuple-element.44.refs_1_, f32[4096,1024]{1,0:T(8,128)} %bitcast.31, f32[16,256,1024]{2,1,0:T(8,128)} %refs_3_.3, ...), custom_call_target="tpu_custom_call" | custom-call | tf_op jit(solution)/shard_map/forward/pallas_call | solution.py:776
  101.5 8.4 %all-gather = f32[8,16,1024]{2,1,0:T(8,128)} all-gather(f32[2,16,1024]{2,1,0:T(8,128)} %get-tuple-element.29), channel_id=2, replica_groups=mesh['px'=4,'py_half'=2,'py_low'=4] {'px'}, dimensions={0}, use_global_device_ids=true | all-gather | bytes 655360 | tf_op jit(solution)/shard_map/all_gather | solution.py:806
  109.9 0.0 copy-done.2
  109.9 0.6 gather_fusion
  110.4 1.0 multiply_reduce_fusion.refs_2_.refs_5_
  111.5 0.0 copy-done.6
  111.5 0.0 copy-done.7
  111.5 0.0 copy-done.8
  111.5 0.6 select_select_fusion.refs_3_.refs_6_
  112.1 9.8 %edges.1 = f32[16,2,64,256]{3,2,1,0:T(8,128)} custom-call(f32[2,256,1024]{2,1,0:T(8,128)} %get-tuple-element.28.refs_0_, f32[4,2,16,1024]{3,2,1,0:T(8,128)} %bitcast.36, f32[2,4,16,1024]{3,2,1,0:T(8,128)} %multiply_reduce_fusion.refs_2_.refs_5_, f32[16,16]{1,0:T(8,128)} %select_select_fusion.refs_3_.refs_6_, ...), custom_call_target="tpu_custom_call" | custom-call | tf_op jit(solution)/shard_map/edges/pallas_call | solution.py:809
  121.9 4.0 %all-to-all-start = ((f32[16,2,64,256]{3,2,1,0:T(8,128)}), f32[16,2,64,256]{3,2,1,0:T(8,128)S(1)}, u32[]{:S(2)}, u32[]{:S(2)}) async-start(f32[16,2,64,256]{3,2,1,0:T(8,128)} %edges.1), calls=%async_computation | async-start | bytes 4194304 | tf_op jit(solution)/shard_map/all_to_all | solution.py:829
  125.9 0.0 copy-done.5
  125.9 0.1 dynamic_slice.3
  126.0 0.9 subtract_multiply_fusion.refs_8_.refs_9_
  127.0 26.7 %all-to-all-done.refs_1_ = f32[16,2,64,256]{3,2,1,0:T(8,128)S(1)} async-done(((f32[16,2,64,256]{3,2,1,0:T(8,128)}), f32[16,2,64,256]{3,2,1,0:T(8,128)S(1)}, u32[]{:S(2)}, u32[]{:S(2)}) %all-to-all-start) | async-done | bytes 2097184 | tf_op jit(solution)/shard_map/all_to_all | solution.py:829
  153.6 1.3 copy-done.1
  154.9 6.0 %gather_modes.1 = (f32[4,2,64,1024]{3,2,1,0:T(8,128)}, f32[64,1024]{1,0:T(8,128)}) custom-call(s32[1]{0:T(128)} %bitcast.13.refs_0_, f32[16,2,64,256]{3,2,1,0:T(8,128)} %copy-done.1, bf16[256,256]{1,0:T(8,128)(2,1)} %constant.173.clone.refs_4_.refs_2_.refs_3_.refs_12_, bf16[256,256]{1,0:T(8,128)(2,1)} %constant.174.clone.refs_5_.refs_3_.refs_4_.refs_13_, ...), custom_call_target="tpu_custom_call" | custom-call | tf_op jit(solution)/shard_map/gather_modes/pallas_call | solution.py:831
  160.9 0.6 collective-permute-start
  161.5 14.7 %collective-permute-done.refs_2_ = f32[64,1024]{1,0:T(8,128)S(1)} collective-permute-done((f32[64,1024]{1,0:T(8,128)}, f32[64,1024]{1,0:T(8,128)S(1)}, u32[]{:S(2)}, u32[]{:S(2)}) %collective-permute-start) | collective-permute-done | bytes 262176 | tf_op jit(solution)/shard_map/ppermute | solution.py:842
  176.2 0.7 copy-done.3
  176.9 6.6 %join.1 = f32[16,2,64,256]{3,2,1,0:T(8,128)} custom-call(s32[1]{0:T(128)} %bitcast.13.refs_0_, f32[4,2,64,1024]{3,2,1,0:T(8,128)} %get-tuple-element.31.refs_1_, f32[64,1024]{1,0:T(8,128)} %copy-done.3, bf16[256,256]{1,0:T(8,128)(2,1)} %constant.173.clone.refs_4_.refs_2_.refs_3_.refs_12_, bf16[256,256]{1,0:T(8,128)(2,1)} %constant.174.clone.refs_5_.refs_3_.refs_4_.refs_13_, ...), custom_call_target="tpu_custom_call" | custom-call | tf_op jit(solution)/shard_map/join/pallas_call | solution.py:843
  183.5 3.7 %all-to-all-start.1 = ((f32[16,2,64,256]{3,2,1,0:T(8,128)}), f32[16,2,64,256]{3,2,1,0:T(8,128)S(1)}, u32[]{:S(2)}, u32[]{:S(2)}) async-start(f32[16,2,64,256]{3,2,1,0:T(8,128)} %join.1), calls=%async_computation.1 | async-start | bytes 4194304 | tf_op jit(solution)/shard_map/all_to_all | solution.py:852
  187.2 14.9 %theta.1 = bf16[4096,1024]{1,0:T(8,128)(2,1)} custom-call(s32[3,1024]{1,0:T(4,128)} %pad_add_fusion.refs_0_.ids_ref, f32[1024]{0:T(1024)} %get-tuple-element.37.new_ref, bf16[4096,1024]{1,0:T(8,128)(2,1)} %bitcast.33), custom_call_target="tpu_custom_call" | custom-call | flops 4194304 | bytes 33554432 | tf_op jit(solution)/shard_map/theta/pallas_call | solution.py:819
  202.1 13.0 %all-to-all-done.1.refs_0_ = f32[16,2,64,256]{3,2,1,0:T(8,128)S(1)} async-done(((f32[16,2,64,256]{3,2,1,0:T(8,128)}), f32[16,2,64,256]{3,2,1,0:T(8,128)S(1)}, u32[]{:S(2)}, u32[]{:S(2)}) %all-to-all-start.1) | async-done | bytes 2097184 | tf_op jit(solution)/shard_map/all_to_all | solution.py:852
  215.1 1.3 copy-done
  216.4 9.3 %spread.1 = (f32[2,256,1024]{2,1,0:T(8,128)}, f32[2,16,1024]{2,1,0:T(8,128)}) custom-call(f32[16,2,64,256]{3,2,1,0:T(8,128)} %copy-done, bf16[256,256]{1,0:T(8,128)(2,1)} %constant.179.clone.refs_10_.refs_9_.refs_1_, bf16[256,256]{1,0:T(8,128)(2,1)} %constant.180.clone.refs_11_.refs_10_.refs_2_, ...), custom_call_target="tpu_custom_call" | custom-call | tf_op jit(solution)/shard_map/spread/pallas_call | solution.py:853
  225.7 9.0 %all-gather.1 = f32[8,16,1024]{2,1,0:T(8,128)} all-gather(f32[2,16,1024]{2,1,0:T(8,128)} %get-tuple-element.35), channel_id=3, replica_groups=mesh['px'=4,'py_half'=2,'py_low'=4] {'px'}, dimensions={0}, use_global_device_ids=true | all-gather | bytes 655360 | tf_op jit(solution)/shard_map/all_gather | solution.py:862
  234.7 38.0 %inverse.1 = f32[16,256,1024]{2,1,0:T(8,128)} custom-call(s32[1]{0:T(128)} %bitcast.refs_0_, f32[16,256,1024]{2,1,0:T(8,128)} %get-tuple-element.27.refs_1_, f32[2,256,1024]{2,1,0:T(8,128)} %get-tuple-element.34.refs_2_, f32[4,2,16,1024]{3,2,1,0:T(8,128)} %bitcast.37, f32[4,2,16,1024]{3,2,1,0:T(8,128)} %bitcast.38, ...), custom_call_target="tpu_custom_call" | custom-call | tf_op jit(solution)/shard_map/inverse/pallas_call | solution.py:867
  272.8 0.0 copy-done.9
  272.8 0.6 copy.49
  (9 shorter events, 0.1 us)
Async XLA Ops:
  5.1 45.5 %copy-start.4 = (s32[1,1024]{1,0:T(1,128)S(1)}, s32[1,1024]{1,0:T(1,128)}, u32[]{:S(2)}) copy-start(s32[1,1024]{1,0:T(1,128)} %param.42) | copy-start | bytes 12292
  52.9 57.0 %copy-start.2 = (f32[4,4]{1,0:T(4,128)S(1)}, f32[4,4]{1,0:T(4,128)}, u32[]{:S(2)}) copy-start(f32[4,4]{1,0:T(4,128)} %constant.192.clone) | copy-start | bytes 196
  52.9 58.6 %copy-start.6 = (f32[16,16]{1,0:T(8,128)S(1)}, f32[16,16]{1,0:T(8,128)}, u32[]{:S(2)}) copy-start(f32[16,16]{1,0:T(8,128)} %constant.188.clone) | copy-start | bytes 3076
  52.9 58.6 %copy-start.7 = (f32[16,16]{1,0:T(8,128)S(1)}, f32[16,16]{1,0:T(8,128)}, u32[]{:S(2)}) copy-start(f32[16,16]{1,0:T(8,128)} %constant.187.clone) | copy-start | bytes 3076
  52.9 58.6 %copy-start.8 = (f32[16,16]{1,0:T(8,128)S(1)}, f32[16,16]{1,0:T(8,128)}, u32[]{:S(2)}) copy-start(f32[16,16]{1,0:T(8,128)} %constant.186.clone) | copy-start | bytes 3076
  121.9 4.1 %copy-start.5 = (f32[1024]{0:T(1024)S(1)}, f32[1024]{0:T(1024)}, u32[]{:S(2)}) copy-start(f32[1024]{0:T(1024)} %constant.183.clone) | copy-start | bytes 12292
  121.9 31.8 %all-to-all-start = ((f32[16,2,64,256]{3,2,1,0:T(8,128)}), f32[16,2,64,256]{3,2,1,0:T(8,128)S(1)}, u32[]{:S(2)}, u32[]{:S(2)}) async-start(f32[16,2,64,256]{3,2,1,0:T(8,128)} %edges.1), calls=%async_computation | async-start | bytes 4194304 | tf_op jit(solution)/shard_map/all_to_all | solution.py:829
  153.6 1.3 copy-start.1
  160.9 15.3 %collective-permute-start = (f32[64,1024]{1,0:T(8,128)}, f32[64,1024]{1,0:T(8,128)S(1)}, u32[]{:S(2)}, u32[]{:S(2)}) collective-permute-start(f32[64,1024]{1,0:T(8,128)} %get-tuple-element.32), channel_id=1, source_target_pairs={{0,4},{4,0},{1,5},{5,1},{2,6},{6,2},{3,7},{7,3},{8,12},{12,8},{9,1... | collective-permute-start | bytes 786440 | tf_op jit(solution)/shard_map/ppermute | solution.py:842
  176.2 0.7 copy-start.3
  183.5 31.6 %all-to-all-start.1 = ((f32[16,2,64,256]{3,2,1,0:T(8,128)}), f32[16,2,64,256]{3,2,1,0:T(8,128)S(1)}, u32[]{:S(2)}, u32[]{:S(2)}) async-start(f32[16,2,64,256]{3,2,1,0:T(8,128)} %join.1), calls=%async_computation.1 | async-start | bytes 4194304 | tf_op jit(solution)/shard_map/all_to_all | solution.py:852
  215.1 1.3 copy-start
  234.7 38.1 %copy-start.9 = (f32[8,128]{1,0:T(8,128)S(1)}, f32[8,128]{1,0:T(8,128)}, u32[]{:S(2)}) copy-start(f32[8,128]{1,0:T(8,128)} %get-tuple-element.38) | copy-start | bytes 12292

commit v5 on v4

--- a/solution.py
+++ b/solution.py
@@ -469,9 +469,16 @@
             tile = pltpu.roll(tile, (lane - lax.shift_right_arithmetic(mark, 7)) & 7, 0)
             rows = tile if rows is None else jnp.where(sublane == lane, tile, rows)
         rows_ref[pl.ds(pl.multiple_of(i * 8, 8), 8)] = rows
+
+    group_count = rows_ref.shape[0] // 8
+    per_trip = math.gcd(group_count, 8)
+
+    def trip(i, _):
+        for k in range(per_trip):
+            pick(i * per_trip + k, None)
         return 0
 
-    lax.fori_loop(0, rows_ref.shape[0] // 8, pick, 0)
+    lax.fori_loop(0, group_count // per_trip, trip, 0)
     ones = jnp.ones((8, 128), F32)
     for group in range(flat_ref.shape[0]):
         rows = rows_ref[group * 128 : (group + 1) * 128]
@@ -505,10 +512,10 @@
 
 
 def gather_kernel(
-    levels, ids_ref, ends_ref, w_hbm, temp_hbm, sin_x_ref, sin_y_ref, out_ref, o0, o1, o2, o3, o4, rows_ref, w_ref,
-    temp_ref, tables, sems, w_sems, temp_sems,
+    levels, ids_ref, ends_ref, w_hbm, sin_x_ref, sin_y_ref, out_ref, o0, o1, o2, o3, o4, rows_ref, w_ref, tables, sems,
+    w_sems,
 ):
-    w_parts, temp_parts = chunk_copies(w_hbm, w_ref, w_sems), chunk_copies(temp_hbm, temp_ref, temp_sems)
+    w_parts = chunk_copies(w_hbm, w_ref, w_sems)
     for copy in w_parts:
         copy.start()
 
@@ -523,28 +530,31 @@
     leaving = [pltpu.make_async_copy(tables.at[k], o, sems.at[k]) for k, o in enumerate((o0, o1, o2, o3, o4))]
     for copy in w_parts:
         copy.wait()
-    for copy in temp_parts + leaving:
+    for copy in leaving:
         copy.start()
-    pick_cells(ids_ref, w_ref, rows_ref, out_ref.at[0])
-    for copy in temp_parts:
-        copy.wait()
-    pick_cells(ids_ref, temp_ref, rows_ref, out_ref.at[1])
+    pick_cells(ids_ref, w_ref, rows_ref, out_ref)
     for copy in leaving:
         copy.wait()
+
+
+def gather_temp_kernel(ids_ref, temp_ref, out_ref, rows_ref):
+    pick_cells(ids_ref, temp_ref, rows_ref, out_ref)
 
 
 def put_cells(ids_ref, new_ref, out):
     sublane = lax.broadcasted_iota(jnp.int32, (8, 128), 0)
     position = sublane * 128 + lax.broadcasted_iota(jnp.int32, (8, 128), 1)
 
+    per_trip = math.gcd(new_ref.shape[0], 32)
+
     def put(i, _):
-        for k in range(8):
-            facet = i * 8 + k
+        for k in range(per_trip):
+            facet = i * per_trip + k
             hit = position == ids_ref[2, facet]
             pltpu.store(out.at[tile_at(ids_ref, facet)], jnp.full((8, 128), new_ref[facet]), mask=hit)
         return 0
 
-    lax.fori_loop(0, new_ref.shape[0] // 8, put, 0)
+    lax.fori_loop(0, new_ref.shape[0] // per_trip, put, 0)
 
 
 def theta_kernel(ids_ref, new_ref, temp_ref, out_ref, wide):
@@ -571,17 +581,19 @@
     return jnp.stack([pltpu.roll(flat, (128 - k * slots) % 128, 1) if k else flat for k in range(shares)])
 
 
-def exchange_kernel(
-    sizes, slots, own_ref, facet_ref, radiation_ref, capacity_ref, drag_ref, heat_ref, back_ref, new_ref, sample, got,
-    flux, back, sent, received,
-):
-    names = ("px", "py_half", "py_low")
-    count = sizes[0] * sizes[1] * sizes[2]
-    shares = 128 // slots
-    places = [lax.axis_index(name) for name in names]
-    me = (places[0] * sizes[1] + places[1]) * sizes[2] + places[2]
-
-    def each_peer(act):
+class Links:
+    def __init__(self, sizes, slots, sent, received):
+        names = ("px", "py_half", "py_low")
+        self.sizes, self.shares = sizes, 128 // slots
+        self.count = sizes[0] * sizes[1] * sizes[2]
+        self.places = [lax.axis_index(name) for name in names]
+        self.me = (self.places[0] * sizes[1] + self.places[1]) * sizes[2] + self.places[2]
+        self.mine = (lax.rem(self.me, self.shares), lax.div(self.me, self.shares))
+        self.sent, self.received = sent, received
+
+    def each_peer(self, act):
+        sizes, places = self.sizes, self.places
+
         def one(step, _):
             low = lax.rem(places[2] + step, sizes[2])
             rest = lax.div(step, sizes[2])
@@ -590,63 +602,92 @@
             act((first * sizes[1] + middle) * sizes[2] + low, (first, middle, low))
             return 0
 
-        lax.fori_loop(1, count, one, 0)
-
-    def at(ref, device):
-        return ref.at[lax.rem(device, shares), lax.div(device, shares)]
-
-    def copy(phase, source, target, peer, device, landing):
+        lax.fori_loop(1, self.count, one, 0)
+
+    def copy(self, phase, source, target, peer, device, landing):
+        at = lambda ref, index: ref.at[lax.rem(index, self.shares), lax.div(index, self.shares)]
         return pltpu.make_async_remote_copy(
             at(source, peer),
             at(target, landing),
-            sent.at[phase, peer],
-            received.at[phase, landing],
+            self.sent.at[phase, peer],
+            self.received.at[phase, landing],
             device_id=device,
             device_id_type=pl.DeviceIdType.MESH,
         )
 
-    def start(phase, source, target):
-        each_peer(lambda peer, device: copy(phase, source, target, peer, device, me).start())
-
-    def finish(phase, source, target):
-        each_peer(lambda peer, device: copy(phase, source, target, peer, device, peer).wait())
-
-    barrier = pltpu.get_barrier_semaphore()
-    each_peer(
-        lambda peer, device: pl.semaphore_signal(
-            barrier, inc=1, device_id=device, device_id_type=pl.DeviceIdType.MESH
+    def greet(self):
+        barrier = pltpu.get_barrier_semaphore()
+        self.each_peer(
+            lambda peer, device: pl.semaphore_signal(
+                barrier, inc=1, device_id=device, device_id_type=pl.DeviceIdType.MESH
+            )
         )
-    )
-    for i in range(2):
-        sample[:, :, i] = by_owner(own_ref[i], slots)
-    pl.semaphore_wait(barrier, count - 1)
-    start(0, sample, got)
-    mine = (lax.rem(me, shares), lax.div(me, shares))
-    got[mine] = sample[mine]
-    facet, radiation, capacity, drag, heat = [
-        by_owner(ref[...], slots) for ref in (facet_ref, radiation_ref, capacity_ref, drag_ref, heat_ref)
+        return barrier
+
+    def start(self, phase, source, target):
+        self.each_peer(lambda peer, device: self.copy(phase, source, target, peer, device, self.me).start())
+        target[self.mine] = source[self.mine]
+
+    def finish(self, phase, source, target):
+        self.each_peer(lambda peer, device: self.copy(phase, source, target, peer, device, peer).wait())
+
+
+def from_owners(parts, slots):
+    lane = lax.broadcasted_iota(jnp.int32, parts.shape[1:], 1)
+    total = None
+    for k in range(parts.shape[0]):
+        part = jnp.where(lane < slots, parts[k], 0.0)
+        part = pltpu.roll(part, k * slots, 1) if k else part
+        total = part if total is None else total + part
+    return total
+
+
+def stress_kernel(
+    sizes, slots, own_ref, facet_ref, drag_ref, heat_ref, back_ref, w_ref, sample, got, flux, back, sent, received
+):
+    links = Links(sizes, slots, sent, received)
+    barrier = links.greet()
+    sample[:, :, 0] = by_owner(own_ref[...], slots)
+    pl.semaphore_wait(barrier, links.count - 1)
+    links.start(0, sample, got)
+    facet, drag, heat = [by_owner(ref[...], slots) for ref in (facet_ref, drag_ref, heat_ref)]
+    links.finish(0, sample, got)
+    w_cell = got[:, :, 0]
+    speeds = jnp.sqrt(w_cell * w_cell + 0.25)
+    flux[:, :, 0] = drag * speeds * w_cell
+    flux[:, :, 1] = heat * speeds
+    flux[:, :, 2] = facet
+    links.start(1, flux, back)
+    w_ref[...] = w_cell
+    links.finish(1, flux, back)
+    for k in range(3):
+        back_ref[k] = from_owners(back[:, :, k], slots)
+
+
+def facet_temp_kernel(
+    sizes, slots, own_ref, facet_ref, radiation_ref, capacity_ref, heat_ref, w_ref, new_ref, sample, got, sent, received
+):
+    links = Links(sizes, slots, sent, received)
+    barrier = links.greet()
+    sample[:, :, 0] = by_owner(own_ref[...], slots)
+    pl.semaphore_wait(barrier, links.count - 1)
+    links.start(0, sample, got)
+    facet, radiation, capacity, heat = [
+        by_owner(ref[...], slots) for ref in (facet_ref, radiation_ref, capacity_ref, heat_ref)
     ]
-    finish(0, sample, got)
-    w_cell, temp_cell = got[:, :, 0], got[:, :, 1]
-    speeds = jnp.sqrt(w_cell * w_cell + 0.25)
-    heat_flux = heat * speeds * (facet - temp_cell)
-    flux[:, :, 0] = drag * speeds * w_cell
-    flux[:, :, 1] = heat_flux
-    start(1, flux, back)
-    back[mine] = flux[mine]
-    new_temp = facet + (radiation - heat_flux - 0.5 * facet) / capacity
-    finish(1, flux, back)
-    lane = lax.broadcasted_iota(jnp.int32, new_temp.shape[1:], 1)
-    for target, parts in ((new_ref, new_temp), (back_ref.at[0], back[:, :, 0]), (back_ref.at[1], back[:, :, 1])):
-        total = None
-        for k in range(shares):
-            part = jnp.where(lane < slots, parts[k], 0.0)
-            part = pltpu.roll(part, k * slots, 1) if k else part
-            total = part if total is None else total + part
-        target[...] = total
-
-
-def near_walls(w_rows, temp_rows, sin_x, sin_y, ends, ids, places, facet_temp, net_radiation, heat_capacity, drag_coef, heat_coef):
+    w_cell = w_ref[...]
+    scale = heat * jnp.sqrt(w_cell * w_cell + 0.25)
+    links.finish(0, sample, got)
+    flux = scale * (facet - got[:, :, 0])
+    new_ref[...] = from_owners(facet + (radiation - flux - 0.5 * facet) / capacity, slots)
+
+
+def facet_sums(ids, returned):
+    same = ids[:, None] == ids[None, :]
+    return jnp.sum(jnp.where(same, returned.reshape(1, -1), 0.0), axis=1)
+
+
+def near_walls(w_rows, sin_x, sin_y, ends, ids, places, facet_temp, drag_coef, heat_coef):
     count = ids.shape[0]
     sizes = tuple(lax.axis_size(name) for name in ("px", "py_half", "py_low"))
     slots = count // (sizes[0] * sizes[1] * sizes[2])
@@ -654,36 +695,62 @@
     rows, width = sin_y.shape[0], sin_x.shape[1]
     own, *tables = pl.pallas_call(
         lambda *refs: gather_kernel(w_rows.shape[0] // rows, *refs),
-        out_shape=[jax.ShapeDtypeStruct((2, *flat), F32)] + [jax.ShapeDtypeStruct((rows, width), F32)] * 5,
-        in_specs=[SMEM, SMEM, HBM, HBM, VMEM, VMEM],
+        out_shape=[jax.ShapeDtypeStruct(flat, F32)] + [jax.ShapeDtypeStruct((rows, width), F32)] * 5,
+        in_specs=[SMEM, SMEM, HBM, VMEM, VMEM],
         out_specs=[VMEM] + [HBM] * 5,
         scratch_shapes=[
             pltpu.VMEM((count, 128), F32),
             pltpu.VMEM(w_rows.shape, F32),
-            pltpu.VMEM(temp_rows.shape, BF16),
             pltpu.VMEM((5, rows, width), F32),
             pltpu.SemaphoreType.DMA((5,)),
-            pltpu.SemaphoreType.DMA((CHUNKS,)),
             pltpu.SemaphoreType.DMA((CHUNKS,)),
         ],
         compiler_params=PARAMS,
         name="facet_gather",
-    )(places, ends, w_rows, temp_rows, sin_x, sin_y)
-    tall = (128 // slots, flat[0], 2, 128)
-    devices = sizes[0] * sizes[1] * sizes[2]
-    returned, new_temp = pl.pallas_call(
-        lambda *refs: exchange_kernel(sizes, slots, *refs),
-        out_shape=(jax.ShapeDtypeStruct((2, *flat), F32), jax.ShapeDtypeStruct(flat, F32)),
+    )(places, ends, w_rows, sin_x, sin_y)
+    by_rows = (128 // slots, flat[0], 128)
+    tall = lambda values: pltpu.VMEM((128 // slots, flat[0], values, 128), F32)
+    returned, w_cell = pl.pallas_call(
+        lambda *refs: stress_kernel(sizes, slots, *refs),
+        out_shape=(jax.ShapeDtypeStruct((3, *flat), F32), jax.ShapeDtypeStruct(by_rows, F32)),
+        in_specs=[VMEM] * 4,
+        out_specs=(VMEM, VMEM),
+        scratch_shapes=[tall(1), tall(1), tall(3), tall(3)]
+        + [pltpu.SemaphoreType.DMA((2, sizes[0] * sizes[1] * sizes[2]))] * 2,
+        compiler_params=pltpu.CompilerParams(collective_id=1, has_side_effects=True),
+        name="stress_exchange",
+    )(own, facet_temp.reshape(flat), drag_coef.reshape(flat), heat_coef.reshape(flat))
+    return (own.reshape(count) - facet_sums(ids, returned[0]), returned, w_cell, tables)
+
+
+def warm_air(temp_rows, ids, places, returned, w_cell, facet_temp, net_radiation, heat_capacity, heat_coef):
+    count = ids.shape[0]
+    sizes = tuple(lax.axis_size(name) for name in ("px", "py_half", "py_low"))
+    slots = count // (sizes[0] * sizes[1] * sizes[2])
+    flat = (count // 128, 128)
+    own = pl.pallas_call(
+        gather_temp_kernel,
+        out_shape=jax.ShapeDtypeStruct(flat, F32),
+        in_specs=[SMEM, VMEM],
+        out_specs=VMEM,
+        scratch_shapes=[pltpu.VMEM((count, 128), F32)],
+        compiler_params=PARAMS,
+        cost_estimate=pl.CostEstimate(flops=0, bytes_accessed=4 * temp_rows.size, transcendentals=0),
+        name="temp_gather",
+    )(places, temp_rows)
+    tall = pltpu.VMEM((128 // slots, flat[0], 1, 128), F32)
+    new_temp = pl.pallas_call(
+        lambda *refs: facet_temp_kernel(sizes, slots, *refs),
+        out_shape=jax.ShapeDtypeStruct(flat, F32),
         in_specs=[VMEM] * 6,
-        out_specs=(VMEM, VMEM),
-        scratch_shapes=[pltpu.VMEM(tall, F32)] * 4 + [pltpu.SemaphoreType.DMA((2, devices))] * 2,
-        compiler_params=pltpu.CompilerParams(collective_id=1, has_side_effects=True),
-        name="facet_exchange",
-    )(own, *[a.reshape(flat) for a in (facet_temp, net_radiation, heat_capacity, drag_coef, heat_coef)])
-    own, returned = own.reshape(2, count), returned.reshape(2, count)
-    same = ids[:, None] == ids[None, :]
-    sums = [jnp.sum(jnp.where(same, returned[i][None, :], 0.0), axis=1) for i in range(2)]
-    return (own[0] - sums[0], own[1] + sums[1], new_temp.reshape(count), tables)
+        out_specs=VMEM,
+        scratch_shapes=[tall] * 2 + [pltpu.SemaphoreType.DMA((1, sizes[0] * sizes[1] * sizes[2]))] * 2,
+        compiler_params=pltpu.CompilerParams(collective_id=2, has_side_effects=True),
+        cost_estimate=pl.CostEstimate(flops=0, bytes_accessed=2**24, transcendentals=0),
+        name="facet_temp",
+    )(own, *[a.reshape(flat) for a in (facet_temp, net_radiation, heat_capacity, heat_coef)], w_cell)
+    heat_flux = returned[1] * (returned[2] - own)
+    return (own.reshape(count) + facet_sums(ids, heat_flux), new_temp.reshape(count))
 
 
 def body(
@@ -719,17 +786,14 @@
     sin_x = jnp.asarray(sin_x, F32)
 
     is_first, is_last = place_y == 0, place_y == py_count - 1
-    w_near, temp_near, new_temp, (root, inv, start, from_below, top) = near_walls(
+    w_near, returned, w_cell, (root, inv, start, from_below, top) = near_walls(
         w_rows,
-        temp_rows,
         sin_x[None, :],
         jnp.asarray(np.repeat(sin_block[:, None], 128, axis=1), F32),
         jnp.stack([is_first, is_last]).astype(jnp.int32),
         ids,
         places,
         facet_temp[0],
-        net_radiation[0],
-        heat_capacity[0],
         drag_coef[0],
         heat_coef[0],
     )
@@ -815,18 +879,21 @@
         compiler_params=PARAMS,
         name="edges",
     )(edges, all_ends, weights, vectors, root, inv, start, top, end, *to_modes)
-    temp_near, edges = lax.optimization_barrier((temp_near, edges))
-    theta_new = pl.pallas_call(
-        theta_kernel,
-        out_shape=jax.ShapeDtypeStruct(temp_rows.shape, BF16),
-        in_specs=[SMEM, SMEM, VMEM],
-        out_specs=VMEM,
-        scratch_shapes=[pltpu.VMEM(temp_rows.shape, F32)],
-        compiler_params=PARAMS,
-        cost_estimate=pl.CostEstimate(flops=temp_rows.size, bytes_accessed=8 * temp_rows.size, transcendentals=0),
-        name="theta",
-    )(places, temp_near, temp_rows).reshape(air_temp.shape)
+    w_cell, edges = lax.optimization_barrier((w_cell, edges))
+    places_late, edges = lax.optimization_barrier((places, edges))
+    temp_near, new_temp = warm_air(
+        temp_rows,
+        ids,
+        places_late,
+        returned,
+        w_cell,
+        facet_temp[0],
+        net_radiation[0],
+        heat_capacity[0],
+        heat_coef[0],
+    )
     edges = lax.all_to_all(edges, ("px", "py_low"), split_axis=0, concat_axis=0, tiled=True)
+    edges, temp_near, new_temp = lax.optimization_barrier((edges, temp_near, new_temp))
     half_id = half.astype(jnp.int32).reshape(1)
     modes, alpha = pl.pallas_call(
         lambda *refs: gather_modes_kernel(levels, px_count, *refs),
@@ -849,6 +916,17 @@
         compiler_params=PARAMS,
         name="join",
     )(half_id, modes, alpha, *y_tables, join_root)
+    joined, temp_near = lax.optimization_barrier((joined, temp_near))
+    theta_new = pl.pallas_call(
+        theta_kernel,
+        out_shape=jax.ShapeDtypeStruct(temp_rows.shape, BF16),
+        in_specs=[SMEM, SMEM, VMEM],
+        out_specs=VMEM,
+        scratch_shapes=[pltpu.VMEM(temp_rows.shape, F32)],
+        compiler_params=PARAMS,
+        cost_estimate=pl.CostEstimate(flops=temp_rows.size, bytes_accessed=8 * temp_rows.size, transcendentals=0),
+        name="theta",
+    )(places, temp_near, temp_rows).reshape(air_temp.shape)
     joined = lax.all_to_all(joined, ("px", "py_low"), split_axis=0, concat_axis=0, tiled=True)
     sides, more = pl.pallas_call(
         lambda *refs: spread_kernel(levels, *refs),

time: 274 us -> 270 us (0.985)
  waiting for transfers between devices: 54.4 us -> 27.7 us
  Pallas kernels: 178 us -> 198 us
    pallas_call x1 -> x3, Pallas kernels: 19.4 us -> 50.5 us  [the longest x1 19.3 us: near_walls(): pl.pallas_call(lambda *refs: stress_kernel(sizes, slots, *refs), out_shap...]
    all_to_all x1, waiting for transfers between devices: 26.7 us -> 0.01 us  [body(): lax.all_to_all(edges, ('px', 'py_low'), split_axis=0, concat_axis=0, tile...]
    pallas_call x1, Pallas kernels: 25.5 us -> 14.9 us  [near_walls(): pl.pallas_call(lambda *refs: gather_kernel(w_rows.shape[0] // rows, *refs...]
  transfers between devices with their start and end apart: 3 -> 3, of which waited for: 3 -> 2; matrix products, arithmetic and copies ran while one was open for 0% -> 1% of each run, Pallas kernels for 5% -> 17%
where the time goes in v5:
time: 270 us; the launch traced here: 269 us
  Pallas kernels  198 us (73%)
  waiting for transfers between devices  27.7 us (10%)
  blocking collectives  17.4 us (6%)
  other arithmetic  11.2 us (4%)
  starting transfers between devices  8.28 us (3%)
  local copies, waits for them, and re-layouts  5.36 us (2%)
    pallas_call x1, Pallas kernels, body(): pl.pallas_call(lambda *refs: forward_kernel(levels, tile, *refs), out_sha...  48.2 us
    pallas_call x1, Pallas kernels, body(): pl.pallas_call(lambda *refs: inverse_kernel(levels, tile, *refs), out_sha...  38 us
    pallas_call x1, Pallas kernels, near_walls(): pl.pallas_call(lambda *refs: stress_kernel(sizes, slots, *refs), out_shap...  19.3 us
    pallas_call x1, Pallas kernels, warm_air(): pl.pallas_call(lambda *refs: facet_temp_kernel(sizes, slots, *refs), out_...  18.3 us
    pallas_call x1, Pallas kernels, near_walls(): pl.pallas_call(lambda *refs: gather_kernel(w_rows.shape[0] // rows, *refs...  14.9 us
    pallas_call x1, Pallas kernels, body(): pl.pallas_call(theta_kernel, out_shape=jax.ShapeDtypeStruct(temp_rows.sha...  14.5 us
    ppermute x1, waiting for transfers between devices, body(): alpha = lax.ppermute(alpha, 'py_half', [(0, 1), (1, 0)])  14.3 us
    all_to_all x1, waiting for transfers between devices, body(): lax.all_to_all(joined, ('px', 'py_low'), split_axis=0, concat_axis=0, til...  13.4 us
  transfers between devices with their start and end apart: 3, of which 2 were waited for; matrix products, arithmetic and copies ran while one was open for 1% of the time, Pallas kernels for 17%

profile of v5, /device:TPU:0, one launch (start us, length us, event | category | flops | bytes accessed | tf_op | source)
XLA Modules:
  0.0 268.6 jit_solution(12293195365458800909)
XLA Ops:
  0.7 0.1 reshape.396
  0.8 0.8 and_select_fusion.4
  1.5 0.7 compare_select_fusion.2
  2.3 0.7 broadcast_select_fusion.1
  3.0 0.9 add_divide_fusion.3
  3.9 0.6 add_convert_fusion.refs_1_
  4.5 0.6 pad_add_fusion.refs_0_.ids_ref
  5.1 14.9 %facet_gather.1 = (f32[8,128]{1,0:T(8,128)}, f32[256,1024]{1,0:T(8,128)}, f32[256,1024]{1,0:T(8,128)}, f32[256,1024]{1,0:T(8,128)}, f32[256,1024]{1,0:T(8,128)}, /*index=5*/f32[256,1024]{1,0:T(8,128)}) custom-call(s32[3,1024]{1,0:T(4,128)} %pad_add_fusion.refs_0_.ids_ref, s32[2]{0:T(128)} %add_convert_fusion.refs_1_, f32[4096,1024]{1,0:T(8,128)} %bitcast.39, ...), custom_call_target="tpu_custom_call" | custom-call | tf_op jit(solution)/shard_map/facet_gather/pallas_call | solution.py:696
  20.0 19.3 %stress_exchange.1 = (f32[3,8,128]{2,1,0:T(8,128)}, f32[4,8,128]{2,1,0:T(8,128)}) custom-call(f32[8,128]{1,0:T(8,128)} %get-tuple-element.28.refs_0_, f32[8,128]{1,0:T(8,128)} %bitcast.52, f32[8,128]{1,0:T(8,128)} %bitcast.58, f32[8,128]{1,0:T(8,128)} %bitcast.54), custom_call_target="tpu_custom_call" | custom-call | tf_op jit(solution)/shard_map/stress_exchange/pallas_call | solution.py:713
  39.3 0.7 slice_bitcast_fusion
  40.0 0.0 copy-done.4
  40.0 0.5 fusion
  40.5 1.3 bitcast_subtract_fusion.1.refs_1_
  41.8 48.2 %forward.1 = (f32[16,256,1024]{2,1,0:T(8,128)}, f32[2,256,1024]{2,1,0:T(8,128)}, f32[2,16,1024]{2,1,0:T(8,128)}, f32[4096,1024]{1,0:T(8,128)}) custom-call(s32[3,1024]{1,0:T(4,128)} %pad_add_fusion.refs_0_.ids_ref, f32[1024]{0:T(1024)} %bitcast_subtract_fusion.1.refs_1_, f32[4096,1024]{1,0:T(8,128)} %bitcast.40, f32[16,256,1024]{2,1,0:T(8,128)} %refs_3_.3, ...), custom_call_target="tpu_custom_call" | custom-call | tf_op jit(solution)/shard_map/forward/pallas_call | solution.py:840
  90.0 8.4 %all-gather = f32[8,16,1024]{2,1,0:T(8,128)} all-gather(f32[2,16,1024]{2,1,0:T(8,128)} %get-tuple-element.37), channel_id=2, replica_groups=mesh['px'=4,'py_half'=2,'py_low'=4] {'px'}, dimensions={0}, use_global_device_ids=true | all-gather | bytes 655360 | tf_op jit(solution)/shard_map/all_gather | solution.py:870
  98.4 0.0 copy-done.2
  98.4 0.6 gather_fusion
  99.0 1.0 multiply_reduce_fusion.refs_2_.refs_5_
  100.0 0.0 copy-done.8
  100.0 0.0 copy-done.9
  100.0 0.0 copy-done.10
  100.0 0.6 select_select_fusion.refs_3_.refs_6_
  100.6 9.8 %edges.1 = f32[16,2,64,256]{3,2,1,0:T(8,128)} custom-call(f32[2,256,1024]{2,1,0:T(8,128)} %get-tuple-element.36.refs_0_, f32[4,2,16,1024]{3,2,1,0:T(8,128)} %bitcast.45, f32[2,4,16,1024]{3,2,1,0:T(8,128)} %multiply_reduce_fusion.refs_2_.refs_5_, f32[16,16]{1,0:T(8,128)} %select_select_fusion.refs_3_.refs_6_, ...), custom_call_target="tpu_custom_call" | custom-call | tf_op jit(solution)/shard_map/edges/pallas_call | solution.py:873
  110.4 4.0 %all-to-all-start = ((f32[16,2,64,256]{3,2,1,0:T(8,128)}), f32[16,2,64,256]{3,2,1,0:T(8,128)S(1)}, u32[]{:S(2)}, u32[]{:S(2)}) async-start(f32[16,2,64,256]{3,2,1,0:T(8,128)} %edges.1), calls=%async_computation | async-start | bytes 4194304 | tf_op jit(solution)/shard_map/all_to_all | solution.py:895
  114.5 0.0 copy-done.5
  114.5 0.1 dynamic_slice.3
  114.5 12.9 %temp_gather.1.refs_0_ = f32[8,128]{1,0:T(8,128)} custom-call(s32[3,1024]{1,0:T(4,128)} %pad_add_fusion.refs_0_.ids_ref, bf16[4096,1024]{1,0:T(8,128)(2,1)} %bitcast.41), custom_call_target="tpu_custom_call" | custom-call | bytes 16777216 | tf_op jit(solution)/shard_map/temp_gather/pallas_call | solution.py:731
  127.5 18.3 %facet_temp.1 = f32[8,128]{1,0:T(8,128)} custom-call(f32[8,128]{1,0:T(8,128)} %temp_gather.1.refs_0_, f32[8,128]{1,0:T(8,128)} %bitcast.53, f32[8,128]{1,0:T(8,128)} %bitcast.56, f32[8,128]{1,0:T(8,128)} %bitcast.57, f32[8,128]{1,0:T(8,128)} %bitcast.55, f32[4,8,128]{2,1,0:T(8,128)} %get-tuple-element.41.refs_5_), custom_call_target="tpu_custom_call" | custom-call | bytes 16777216 | tf_op jit(solution)/shard_map/facet_temp/pallas_call | solution.py:742
  145.8 0.0 copy-done.7
  145.8 0.7 fusion.7
  146.5 0.5 fusion.1
  147.1 1.3 bitcast_add_fusion.new_ref
  148.4 0.9 subtract_multiply_fusion.refs_8_.refs_9_
  149.3 0.0 all-to-all-done.refs_1_
  149.3 1.3 copy-done.1
  150.6 6.0 %gather_modes.1 = (f32[4,2,64,1024]{3,2,1,0:T(8,128)}, f32[64,1024]{1,0:T(8,128)}) custom-call(s32[1]{0:T(128)} %bitcast.10.refs_0_, f32[16,2,64,256]{3,2,1,0:T(8,128)} %copy-done.1, bf16[256,256]{1,0:T(8,128)(2,1)} %constant.173.clone.refs_4_.refs_2_.refs_3_.refs_12_, bf16[256,256]{1,0:T(8,128)(2,1)} %constant.174.clone.refs_5_.refs_3_.refs_4_.refs_13_, ...), custom_call_target="tpu_custom_call" | custom-call | tf_op jit(solution)/shard_map/gather_modes/pallas_call | solution.py:898
  156.6 0.5 collective-permute-start
  157.1 14.3 %collective-permute-done.refs_2_ = f32[64,1024]{1,0:T(8,128)S(1)} collective-permute-done((f32[64,1024]{1,0:T(8,128)}, f32[64,1024]{1,0:T(8,128)S(1)}, u32[]{:S(2)}, u32[]{:S(2)}) %collective-permute-start) | collective-permute-done | bytes 262176 | tf_op jit(solution)/shard_map/ppermute | solution.py:909
  171.4 0.7 copy-done.3
  172.1 6.6 %join.1 = f32[16,2,64,256]{3,2,1,0:T(8,128)} custom-call(s32[1]{0:T(128)} %bitcast.10.refs_0_, f32[4,2,64,1024]{3,2,1,0:T(8,128)} %get-tuple-element.43.refs_1_, f32[64,1024]{1,0:T(8,128)} %copy-done.3, bf16[256,256]{1,0:T(8,128)(2,1)} %constant.173.clone.refs_4_.refs_2_.refs_3_.refs_12_, bf16[256,256]{1,0:T(8,128)(2,1)} %constant.174.clone.refs_5_.refs_3_.refs_4_.refs_13_, ...), custom_call_target="tpu_custom_call" | custom-call | tf_op jit(solution)/shard_map/join/pallas_call | solution.py:910
  178.7 3.7 %all-to-all-start.1 = ((f32[16,2,64,256]{3,2,1,0:T(8,128)}), f32[16,2,64,256]{3,2,1,0:T(8,128)S(1)}, u32[]{:S(2)}, u32[]{:S(2)}) async-start(f32[16,2,64,256]{3,2,1,0:T(8,128)} %join.1), calls=%async_computation.1 | async-start | bytes 4194304 | tf_op jit(solution)/shard_map/all_to_all | solution.py:930
  182.4 14.5 %theta.1 = bf16[4096,1024]{1,0:T(8,128)(2,1)} custom-call(s32[3,1024]{1,0:T(4,128)} %pad_add_fusion.refs_0_.ids_ref, f32[1024]{0:T(1024)} %bitcast_add_fusion.new_ref, bf16[4096,1024]{1,0:T(8,128)(2,1)} %bitcast.42), custom_call_target="tpu_custom_call" | custom-call | flops 4194304 | bytes 33554432 | tf_op jit(solution)/shard_map/theta/pallas_call | solution.py:920
  196.9 13.4 %all-to-all-done.1.refs_0_ = f32[16,2,64,256]{3,2,1,0:T(8,128)S(1)} async-done(((f32[16,2,64,256]{3,2,1,0:T(8,128)}), f32[16,2,64,256]{3,2,1,0:T(8,128)S(1)}, u32[]{:S(2)}, u32[]{:S(2)}) %all-to-all-start.1) | async-done | bytes 2097184 | tf_op jit(solution)/shard_map/all_to_all | solution.py:930
  210.3 1.3 copy-done
  211.6 9.3 %spread.1 = (f32[2,256,1024]{2,1,0:T(8,128)}, f32[2,16,1024]{2,1,0:T(8,128)}) custom-call(f32[16,2,64,256]{3,2,1,0:T(8,128)} %copy-done, bf16[256,256]{1,0:T(8,128)(2,1)} %constant.179.clone.refs_10_.refs_9_.refs_1_, bf16[256,256]{1,0:T(8,128)(2,1)} %constant.180.clone.refs_11_.refs_10_.refs_2_, ...), custom_call_target="tpu_custom_call" | custom-call | tf_op jit(solution)/shard_map/spread/pallas_call | solution.py:931
  221.0 9.0 %all-gather.1 = f32[8,16,1024]{2,1,0:T(8,128)} all-gather(f32[2,16,1024]{2,1,0:T(8,128)} %get-tuple-element.49), channel_id=3, replica_groups=mesh['px'=4,'py_half'=2,'py_low'=4] {'px'}, dimensions={0}, use_global_device_ids=true | all-gather | bytes 655360 | tf_op jit(solution)/shard_map/all_gather | solution.py:940
  229.9 38.0 %inverse.1 = f32[16,256,1024]{2,1,0:T(8,128)} custom-call(s32[1]{0:T(128)} %bitcast.refs_0_, f32[16,256,1024]{2,1,0:T(8,128)} %get-tuple-element.34.refs_1_, f32[2,256,1024]{2,1,0:T(8,128)} %get-tuple-element.48.refs_2_, f32[4,2,16,1024]{3,2,1,0:T(8,128)} %bitcast.46, f32[4,2,16,1024]{3,2,1,0:T(8,128)} %bitcast.47, ...), custom_call_target="tpu_custom_call" | custom-call | tf_op jit(solution)/shard_map/inverse/pallas_call | solution.py:945
  268.0 0.6 copy.49
  (16 shorter events, 0.1 us)
Async XLA Ops:
  5.1 34.9 %copy-start.4 = (s32[1,1024]{1,0:T(1,128)S(1)}, s32[1,1024]{1,0:T(1,128)}, u32[]{:S(2)}) copy-start(s32[1,1024]{1,0:T(1,128)} %param.42) | copy-start | bytes 12292
  41.8 56.6 %copy-start.2 = (f32[4,4]{1,0:T(4,128)S(1)}, f32[4,4]{1,0:T(4,128)}, u32[]{:S(2)}) copy-start(f32[4,4]{1,0:T(4,128)} %constant.192.clone) | copy-start | bytes 196
  41.8 58.2 %copy-start.8 = (f32[16,16]{1,0:T(8,128)S(1)}, f32[16,16]{1,0:T(8,128)}, u32[]{:S(2)}) copy-start(f32[16,16]{1,0:T(8,128)} %constant.188.clone) | copy-start | bytes 3076
  41.8 58.2 %copy-start.9 = (f32[16,16]{1,0:T(8,128)S(1)}, f32[16,16]{1,0:T(8,128)}, u32[]{:S(2)}) copy-start(f32[16,16]{1,0:T(8,128)} %constant.187.clone) | copy-start | bytes 3076
  41.8 58.2 %copy-start.10 = (f32[16,16]{1,0:T(8,128)S(1)}, f32[16,16]{1,0:T(8,128)}, u32[]{:S(2)}) copy-start(f32[16,16]{1,0:T(8,128)} %constant.186.clone) | copy-start | bytes 3076
  110.4 4.1 %copy-start.5 = (f32[1024]{0:T(1024)S(1)}, f32[1024]{0:T(1024)}, u32[]{:S(2)}) copy-start(f32[1024]{0:T(1024)} %constant.183.clone) | copy-start | bytes 12292
  110.4 38.9 %all-to-all-start = ((f32[16,2,64,256]{3,2,1,0:T(8,128)}), f32[16,2,64,256]{3,2,1,0:T(8,128)S(1)}, u32[]{:S(2)}, u32[]{:S(2)}) async-start(f32[16,2,64,256]{3,2,1,0:T(8,128)} %edges.1), calls=%async_computation | async-start | bytes 4194304 | tf_op jit(solution)/shard_map/all_to_all | solution.py:895
  114.5 31.3 %copy-start.7 = (f32[3,8,128]{2,1,0:T(8,128)S(1)}, f32[3,8,128]{2,1,0:T(8,128)}, u32[]{:S(2)}) copy-start(f32[3,8,128]{2,1,0:T(8,128)} %get-tuple-element.29) | copy-start | bytes 36868
  149.3 1.3 copy-start.1
  156.6 14.8 %collective-permute-start = (f32[64,1024]{1,0:T(8,128)}, f32[64,1024]{1,0:T(8,128)S(1)}, u32[]{:S(2)}, u32[]{:S(2)}) collective-permute-start(f32[64,1024]{1,0:T(8,128)} %get-tuple-element.44), channel_id=1, source_target_pairs={{0,4},{4,0},{1,5},{5,1},{2,6},{6,2},{3,7},{7,3},{8,12},{12,8},{9,1... | collective-permute-start | bytes 786440 | tf_op jit(solution)/shard_map/ppermute | solution.py:909
  171.4 0.7 copy-start.3
  178.7 31.6 %all-to-all-start.1 = ((f32[16,2,64,256]{3,2,1,0:T(8,128)}), f32[16,2,64,256]{3,2,1,0:T(8,128)S(1)}, u32[]{:S(2)}, u32[]{:S(2)}) async-start(f32[16,2,64,256]{3,2,1,0:T(8,128)} %join.1), calls=%async_computation.1 | async-start | bytes 4194304 | tf_op jit(solution)/shard_map/all_to_all | solution.py:930
  210.3 1.3 copy-start
  229.9 38.1 %copy-start.6 = (f32[8,128]{1,0:T(8,128)S(1)}, f32[8,128]{1,0:T(8,128)}, u32[]{:S(2)}) copy-start(f32[8,128]{1,0:T(8,128)} %facet_temp.1) | copy-start | bytes 12292

commit v6 on v5

--- a/solution.py
+++ b/solution.py
@@ -245,24 +245,32 @@
     levels, edge_ref, ends_ref, weights_ref, vectors_ref, root_ref, inv_ref, start_ref, top_ref, end_ref, ch, cl,
     out_ref, pattern, store, fixed,
 ):
-    block_fluxes(
-        [(ends_ref[b, 0], ends_ref[b, 1]) for b in range(ends_ref.shape[0])], weights_ref, vectors_ref, levels, pattern
-    )
+    step = pl.program_id(0)
+    tile = edge_ref.shape[1]
+
+    @pl.when(step == 0)
+    def _():
+        ends = [(ends_ref[b, 0], ends_ref[b, 1]) for b in range(ends_ref.shape[0])]
+        block_fluxes(ends, weights_ref, vectors_ref, levels, pattern)
 
     def rows_of(sub, _):
-        rows = pl.ds(pl.multiple_of(sub * 8, 8), 8)
+        here = pl.multiple_of(sub * 8, 8)
+        rows, full = pl.ds(here, 8), pl.ds(pl.multiple_of(step * tile + here, 8), 8)
         root, top = root_ref[rows], top_ref[rows]
         first, last = first_sweeps(lambda level: pattern[level], root, top, None, store, levels)
         weight = end_ref[rows, :1]
-        fixed[0, rows] = edge_ref[0, rows] - weight * (first * inv_ref[rows])
+        fixed[0, full] = edge_ref[0, rows] - weight * (first * inv_ref[rows])
         last = last + power(root, levels) * (first * start_ref[rows])
-        fixed[1, rows] = edge_ref[1, rows] - weight * (root * (top - 1.0) * last)
+        fixed[1, full] = edge_ref[1, rows] - weight * (root * (top - 1.0) * last)
         return 0
 
-    lax.fori_loop(0, edge_ref.shape[1] // 8, rows_of, 0)
-    for side in range(2):
-        value = dot3(split(fixed[side].T), read_pair((ch, cl)))
-        out_ref[:, side] = value.reshape(out_ref.shape[0], out_ref.shape[2], out_ref.shape[3])
+    lax.fori_loop(0, tile // 8, rows_of, 0)
+
+    @pl.when(step == pl.num_programs(0) - 1)
+    def _():
+        for side in range(2):
+            value = dot3(split(fixed[side].T), read_pair((ch, cl)))
+            out_ref[:, side] = value.reshape(out_ref.shape[0], out_ref.shape[2], out_ref.shape[3])
 
 
 def join_start(levels, near_top, root):
@@ -356,17 +364,27 @@
                 out_ref[i * blocks + block, side] = whole[block, side, :, i * width : (i + 1) * width]
 
 
-def spread_kernel(levels, joined_ref, ch, cl, root_ref, start_ref, below_ref, top_ref, end_ref, out_ref, ends_ref, store, total):
-    kx_width = joined_ref.shape[0] * joined_ref.shape[2]
-    for side in range(2):
-        value = joined_ref[:, side].reshape(kx_width, joined_ref.shape[3])
-        out_ref[side] = dot3(read_pair((ch, cl)), split(value), ((1,), (1,)))
-    total[...] = jnp.zeros_like(total)
+def spread_kernel(
+    levels, joined_ref, ch, cl, root_ref, start_ref, below_ref, top_ref, end_ref, out_ref, ends_ref, store, total, sides
+):
+    step = pl.program_id(0)
+    tile = out_ref.shape[1]
+
+    @pl.when(step == 0)
+    def _():
+        kx_width = joined_ref.shape[0] * joined_ref.shape[2]
+        for side in range(2):
+            value = joined_ref[:, side].reshape(kx_width, joined_ref.shape[3])
+            sides[side] = dot3(read_pair((ch, cl)), split(value), ((1,), (1,)))
+        total[...] = jnp.zeros_like(total)
 
     def rows_of(sub, _):
-        rows = pl.ds(pl.multiple_of(sub * 8, 8), 8)
+        here = pl.multiple_of(sub * 8, 8)
+        rows, full = pl.ds(here, 8), pl.ds(pl.multiple_of(step * tile + here, 8), 8)
         root, top = root_ref[rows], top_ref[rows]
-        below, above = out_ref[0, rows], out_ref[1, rows]
+        below, above = sides[0, full], sides[1, full]
+        out_ref[0, rows] = below
+        out_ref[1, rows] = above
         start = start_ref[rows] * (power(root, levels) * above) - below_ref[rows] * below
         weight = end_ref[rows, :1]
 
@@ -376,8 +394,11 @@
         second_sweeps(None, start, root, top, above, store, levels, emit)
         return 0
 
-    lax.fori_loop(0, out_ref.shape[1] // 8, rows_of, 0)
-    fold_ends(total, ends_ref, levels)
+    lax.fori_loop(0, tile // 8, rows_of, 0)
+
+    @pl.when(step == pl.num_programs(0) - 1)
+    def _():
+        fold_ends(total, ends_ref, levels)
 
 
 def inverse_kernel(
@@ -723,10 +744,8 @@
     return (own.reshape(count) - facet_sums(ids, returned[0]), returned, w_cell, tables)
 
 
-def warm_air(temp_rows, ids, places, returned, w_cell, facet_temp, net_radiation, heat_capacity, heat_coef):
+def warm_air(temp_rows, ids, places, returned):
     count = ids.shape[0]
-    sizes = tuple(lax.axis_size(name) for name in ("px", "py_half", "py_low"))
-    slots = count // (sizes[0] * sizes[1] * sizes[2])
     flat = (count // 128, 128)
     own = pl.pallas_call(
         gather_temp_kernel,
@@ -738,6 +757,14 @@
         cost_estimate=pl.CostEstimate(flops=0, bytes_accessed=4 * temp_rows.size, transcendentals=0),
         name="temp_gather",
     )(places, temp_rows)
+    heat_flux = returned[1] * (returned[2] - own)
+    return (own, own.reshape(count) + facet_sums(ids, heat_flux))
+
+
+def warm_facets(own, w_cell, facet_temp, net_radiation, heat_capacity, heat_coef):
+    flat = own.shape
+    sizes = tuple(lax.axis_size(name) for name in ("px", "py_half", "py_low"))
+    slots = own.size // (sizes[0] * sizes[1] * sizes[2])
     tall = pltpu.VMEM((128 // slots, flat[0], 1, 128), F32)
     new_temp = pl.pallas_call(
         lambda *refs: facet_temp_kernel(sizes, slots, *refs),
@@ -749,8 +776,7 @@
         cost_estimate=pl.CostEstimate(flops=0, bytes_accessed=2**24, transcendentals=0),
         name="facet_temp",
     )(own, *[a.reshape(flat) for a in (facet_temp, net_radiation, heat_capacity, heat_coef)], w_cell)
-    heat_flux = returned[1] * (returned[2] - own)
-    return (own.reshape(count) + facet_sums(ids, heat_flux), new_temp.reshape(count))
+    return new_temp.reshape(facet_temp.shape)
 
 
 def body(
@@ -830,7 +856,7 @@
     tile = math.gcd(rows, 32)
     tiles = rows // tile
     flat = lambda i: pl.BlockSpec((tile, width), i)
-    fixed = lambda a: pl.BlockSpec(a.shape, lambda i: (0,) * a.ndim)
+    fixed = lambda a: pl.BlockSpec(a.shape, lambda i: (0,) * len(a.shape))
     pairs = levels // 2
     late = lambda i: (jnp.maximum(i - pairs, 0), 0)
     down = lambda i: (jnp.maximum(pairs - 1 - i, 0), 0, 0)
@@ -868,32 +894,28 @@
     )(places, w_near, w_rows, horiz_div, *x_tables, *to_modes, root, inv, start, top, end)
 
     all_ends = lax.all_gather(ends, "px")
+    here = lambda i: (i, 0)
     packed = jax.ShapeDtypeStruct((group, 2, own_kx, rows), F32)
     working = [pltpu.VMEM((levels, 8, width), F32)] * 2
     edges = pl.pallas_call(
         lambda *refs: edge_kernel(levels, *refs),
         out_shape=packed,
-        in_specs=[VMEM] * 11,
-        out_specs=VMEM,
+        grid=(tiles,),
+        in_specs=[pl.BlockSpec((2, tile, width), lambda i: (0, i, 0))]
+        + [fixed(a) for a in (all_ends, weights, vectors)]
+        + [flat(here)] * 4
+        + [pl.BlockSpec((tile, 128), here)]
+        + [fixed(t) for t in to_modes],
+        out_specs=fixed(packed),
         scratch_shapes=working + [pltpu.VMEM((2, rows, width), F32)],
         compiler_params=PARAMS,
         name="edges",
     )(edges, all_ends, weights, vectors, root, inv, start, top, end, *to_modes)
     w_cell, edges = lax.optimization_barrier((w_cell, edges))
     places_late, edges = lax.optimization_barrier((places, edges))
-    temp_near, new_temp = warm_air(
-        temp_rows,
-        ids,
-        places_late,
-        returned,
-        w_cell,
-        facet_temp[0],
-        net_radiation[0],
-        heat_capacity[0],
-        heat_coef[0],
-    )
+    temp_own, temp_near = warm_air(temp_rows, ids, places_late, returned)
     edges = lax.all_to_all(edges, ("px", "py_low"), split_axis=0, concat_axis=0, tiled=True)
-    edges, temp_near, new_temp = lax.optimization_barrier((edges, temp_near, new_temp))
+    edges, temp_near = lax.optimization_barrier((edges, temp_near))
     half_id = half.astype(jnp.int32).reshape(1)
     modes, alpha = pl.pallas_call(
         lambda *refs: gather_modes_kernel(levels, px_count, *refs),
@@ -906,17 +928,7 @@
         compiler_params=PARAMS,
         name="gather_modes",
     )(half_id, edges, *y_tables, join_root)
-    alpha = lax.ppermute(alpha, "py_half", [(0, 1), (1, 0)])
-    joined = pl.pallas_call(
-        lambda *refs: join_kernel(levels, px_count, *refs),
-        out_shape=packed,
-        in_specs=[SMEM] + [VMEM] * 9,
-        out_specs=VMEM,
-        scratch_shapes=[pltpu.VMEM((blocks, 2, own_kx, y_cells), F32)],
-        compiler_params=PARAMS,
-        name="join",
-    )(half_id, modes, alpha, *y_tables, join_root)
-    joined, temp_near = lax.optimization_barrier((joined, temp_near))
+    alpha, temp_near = lax.optimization_barrier((alpha, temp_near))
     theta_new = pl.pallas_call(
         theta_kernel,
         out_shape=jax.ShapeDtypeStruct(temp_rows.shape, BF16),
@@ -927,13 +939,32 @@
         cost_estimate=pl.CostEstimate(flops=temp_rows.size, bytes_accessed=8 * temp_rows.size, transcendentals=0),
         name="theta",
     )(places, temp_near, temp_rows).reshape(air_temp.shape)
+    alpha = lax.ppermute(alpha, "py_half", [(0, 1), (1, 0)])
+    alpha, theta_new = lax.optimization_barrier((alpha, theta_new))
+    joined = pl.pallas_call(
+        lambda *refs: join_kernel(levels, px_count, *refs),
+        out_shape=packed,
+        in_specs=[SMEM] + [VMEM] * 9,
+        out_specs=VMEM,
+        scratch_shapes=[pltpu.VMEM((blocks, 2, own_kx, y_cells), F32)],
+        compiler_params=PARAMS,
+        name="join",
+    )(half_id, modes, alpha, *y_tables, join_root)
+    joined, temp_own = lax.optimization_barrier((joined, temp_own))
+    new_temp = warm_facets(
+        temp_own, w_cell, facet_temp[0], net_radiation[0], heat_capacity[0], heat_coef[0]
+    )
     joined = lax.all_to_all(joined, ("px", "py_low"), split_axis=0, concat_axis=0, tiled=True)
     sides, more = pl.pallas_call(
         lambda *refs: spread_kernel(levels, *refs),
         out_shape=(jax.ShapeDtypeStruct((2, rows, width), F32), ends_shape),
-        in_specs=[VMEM] * 8,
-        out_specs=(VMEM, VMEM),
-        scratch_shapes=working,
+        grid=(tiles,),
+        in_specs=[fixed(packed)]
+        + [fixed(t) for t in to_modes]
+        + [flat(here)] * 4
+        + [pl.BlockSpec((tile, 128), here)],
+        out_specs=(pl.BlockSpec((2, tile, width), lambda i: (0, i, 0)), fixed(ends_shape)),
+        scratch_shapes=working + [pltpu.VMEM((2, rows, width), F32)],
         compiler_params=PARAMS,
         name="spread",
     )(joined, *to_modes, root, start, from_below, top, end)

time: 270 us -> 269 us (level)
  waiting for transfers between devices: 27.7 us -> 11.5 us
  Pallas kernels: 198 us -> 214 us
    ppermute x1, waiting for transfers between devices: 14.3 us -> 0.29 us  [body(): alpha = lax.ppermute(alpha, 'py_half', [(0, 1), (1, 0)])]
    pallas_call x1, Pallas kernels: 18.3 us -> 32.3 us  [warm_facets(): pl.pallas_call(lambda *refs: facet_temp_kernel(sizes, slots, *refs), out_...]
    all_to_all x1, waiting for transfers between devices: 13.4 us -> 0.01 us  [body(): lax.all_to_all(joined, ('px', 'py_low'), split_axis=0, concat_axis=0, til...]
    all_to_all x1, waiting for transfers between devices: 0.01 us -> 11.2 us  [body(): lax.all_to_all(edges, ('px', 'py_low'), split_axis=0, concat_axis=0, tile...]
  transfers between devices with their start and end apart: 3 -> 3, of which waited for: 2 -> 2; matrix products, arithmetic and copies ran while one was open for 1% -> 1% of each run, Pallas kernels for 17% -> 22%
where the time goes in v6:
time: 269 us; the launch traced here: 268 us
  Pallas kernels  214 us (80%)
  blocking collectives  16.7 us (6%)
  waiting for transfers between devices  11.5 us (4%)
  other arithmetic  11.2 us (4%)
  starting transfers between devices  8.29 us (3%)
  local copies, waits for them, and re-layouts  5.36 us (2%)
    pallas_call x1, Pallas kernels, body(): pl.pallas_call(lambda *refs: forward_kernel(levels, tile, *refs), out_sha...  48.2 us
    pallas_call x1, Pallas kernels, body(): pl.pallas_call(lambda *refs: inverse_kernel(levels, tile, *refs), out_sha...  38 us
    pallas_call x1, Pallas kernels, warm_facets(): pl.pallas_call(lambda *refs: facet_temp_kernel(sizes, slots, *refs), out_...  32.3 us
    pallas_call x1, Pallas kernels, near_walls(): pl.pallas_call(lambda *refs: stress_kernel(sizes, slots, *refs), out_shap...  19.3 us
    pallas_call x1, Pallas kernels, near_walls(): pl.pallas_call(lambda *refs: gather_kernel(w_rows.shape[0] // rows, *refs...  14.9 us
    pallas_call x1, Pallas kernels, body(): pl.pallas_call(theta_kernel, out_shape=jax.ShapeDtypeStruct(temp_rows.sha...  14.5 us
    pallas_call x1, Pallas kernels, warm_air(): pl.pallas_call(gather_temp_kernel, out_shape=jax.ShapeDtypeStruct(flat, F...  12.9 us
    all_to_all x1, waiting for transfers between devices, body(): lax.all_to_all(edges, ('px', 'py_low'), split_axis=0, concat_axis=0, tile...  11.2 us
  transfers between devices with their start and end apart: 3, of which 2 were waited for; matrix products, arithmetic and copies ran while one was open for 1% of the time, Pallas kernels for 22%

profile of v6, /device:TPU:0, one launch (start us, length us, event | category | flops | bytes accessed | tf_op | source)
XLA Modules:
  0.0 267.7 jit_solution(16768628409443022062)
XLA Ops:
  0.7 0.1 reshape.392
  0.8 0.8 and_select_fusion.4
  1.5 0.7 compare_select_fusion.2
  2.3 0.7 broadcast_select_fusion.1
  3.0 0.9 add_divide_fusion.3
  3.9 0.6 add_convert_fusion.refs_1_
  4.5 0.6 pad_add_fusion.refs_0_.ids_ref
  5.1 14.9 %facet_gather.1 = (f32[8,128]{1,0:T(8,128)}, f32[256,1024]{1,0:T(8,128)}, f32[256,1024]{1,0:T(8,128)}, f32[256,1024]{1,0:T(8,128)}, f32[256,1024]{1,0:T(8,128)}, /*index=5*/f32[256,1024]{1,0:T(8,128)}) custom-call(s32[3,1024]{1,0:T(4,128)} %pad_add_fusion.refs_0_.ids_ref, s32[2]{0:T(128)} %add_convert_fusion.refs_1_, f32[4096,1024]{1,0:T(8,128)} %bitcast.38, ...), custom_call_target="tpu_custom_call" | custom-call | tf_op jit(solution)/shard_map/facet_gather/pallas_call | solution.py:717
  20.0 19.3 %stress_exchange.1 = (f32[3,8,128]{2,1,0:T(8,128)}, f32[4,8,128]{2,1,0:T(8,128)}) custom-call(f32[8,128]{1,0:T(8,128)} %get-tuple-element.31.refs_0_, f32[8,128]{1,0:T(8,128)} %bitcast.51, f32[8,128]{1,0:T(8,128)} %bitcast.57, f32[8,128]{1,0:T(8,128)} %bitcast.53), custom_call_target="tpu_custom_call" | custom-call | tf_op jit(solution)/shard_map/stress_exchange/pallas_call | solution.py:734
  39.3 0.7 slice_bitcast_fusion
  40.0 0.0 copy-done.4
  40.0 0.5 fusion
  40.5 1.3 bitcast_subtract_fusion.1.refs_1_
  41.8 48.2 %forward.1 = (f32[16,256,1024]{2,1,0:T(8,128)}, f32[2,256,1024]{2,1,0:T(8,128)}, f32[2,16,1024]{2,1,0:T(8,128)}, f32[4096,1024]{1,0:T(8,128)}) custom-call(s32[3,1024]{1,0:T(4,128)} %pad_add_fusion.refs_0_.ids_ref, f32[1024]{0:T(1024)} %bitcast_subtract_fusion.1.refs_1_, f32[4096,1024]{1,0:T(8,128)} %bitcast.39, f32[16,256,1024]{2,1,0:T(8,128)} %refs_3_.3, ...), custom_call_target="tpu_custom_call" | custom-call | tf_op jit(solution)/shard_map/forward/pallas_call | solution.py:866
  90.0 8.4 %all-gather = f32[8,16,1024]{2,1,0:T(8,128)} all-gather(f32[2,16,1024]{2,1,0:T(8,128)} %get-tuple-element.40), channel_id=2, replica_groups=mesh['px'=4,'py_half'=2,'py_low'=4] {'px'}, dimensions={0}, use_global_device_ids=true | all-gather | bytes 655360 | tf_op jit(solution)/shard_map/all_gather | solution.py:896
  98.4 0.0 copy-done.2
  98.4 0.6 gather_fusion
  99.0 1.0 multiply_reduce_fusion.refs_2_.refs_5_
  100.0 0.0 copy-done.8
  100.0 0.0 copy-done.9
  100.0 0.0 copy-done.10
  100.0 0.6 select_select_fusion.refs_3_.refs_6_
  100.6 10.7 %edges.1 = f32[16,2,64,256]{3,2,1,0:T(8,128)} custom-call(f32[2,256,1024]{2,1,0:T(8,128)} %get-tuple-element.39.refs_0_, f32[4,2,16,1024]{3,2,1,0:T(8,128)} %bitcast.44, f32[2,4,16,1024]{3,2,1,0:T(8,128)} %multiply_reduce_fusion.refs_2_.refs_5_, f32[16,16]{1,0:T(8,128)} %select_select_fusion.refs_3_.refs_6_, ...), custom_call_target="tpu_custom_call" | custom-call | tf_op jit(solution)/shard_map/edges/pallas_call | solution.py:900
  111.3 4.0 %all-to-all-start = ((f32[16,2,64,256]{3,2,1,0:T(8,128)}), f32[16,2,64,256]{3,2,1,0:T(8,128)S(1)}, u32[]{:S(2)}, u32[]{:S(2)}) async-start(f32[16,2,64,256]{3,2,1,0:T(8,128)} %edges.1), calls=%async_computation | async-start | bytes 4194304 | tf_op jit(solution)/shard_map/all_to_all | solution.py:917
  115.4 0.0 copy-done.5
  115.4 0.1 dynamic_slice.3
  115.5 12.9 %temp_gather.1.refs_0_ = f32[8,128]{1,0:T(8,128)} custom-call(s32[3,1024]{1,0:T(4,128)} %pad_add_fusion.refs_0_.ids_ref, bf16[4096,1024]{1,0:T(8,128)(2,1)} %bitcast.40), custom_call_target="tpu_custom_call" | custom-call | bytes 16777216 | tf_op jit(solution)/shard_map/temp_gather/pallas_call | solution.py:750
  128.4 0.7 fusion.7
  129.1 0.5 fusion.1
  129.6 1.3 bitcast_add_fusion.new_ref
  130.9 0.9 subtract_multiply_fusion.refs_8_.refs_9_
  131.8 11.2 %all-to-all-done.refs_1_ = f32[16,2,64,256]{3,2,1,0:T(8,128)S(1)} async-done(((f32[16,2,64,256]{3,2,1,0:T(8,128)}), f32[16,2,64,256]{3,2,1,0:T(8,128)S(1)}, u32[]{:S(2)}, u32[]{:S(2)}) %all-to-all-start) | async-done | bytes 2097184 | tf_op jit(solution)/shard_map/all_to_all | solution.py:917
  143.1 1.3 copy-done.1
  144.4 6.0 %gather_modes.1 = (f32[4,2,64,1024]{3,2,1,0:T(8,128)}, f32[64,1024]{1,0:T(8,128)}) custom-call(s32[1]{0:T(128)} %bitcast.10.refs_0_, f32[16,2,64,256]{3,2,1,0:T(8,128)} %copy-done.1, bf16[256,256]{1,0:T(8,128)(2,1)} %constant.173.clone.refs_4_.refs_2_.refs_3_.refs_12_, bf16[256,256]{1,0:T(8,128)(2,1)} %constant.174.clone.refs_5_.refs_3_.refs_4_.refs_13_, ...), custom_call_target="tpu_custom_call" | custom-call | tf_op jit(solution)/shard_map/gather_modes/pallas_call | solution.py:920
  150.4 0.5 collective-permute-start
  150.9 14.5 %theta.1 = bf16[4096,1024]{1,0:T(8,128)(2,1)} custom-call(s32[3,1024]{1,0:T(4,128)} %pad_add_fusion.refs_0_.ids_ref, f32[1024]{0:T(1024)} %bitcast_add_fusion.new_ref, bf16[4096,1024]{1,0:T(8,128)(2,1)} %bitcast.41), custom_call_target="tpu_custom_call" | custom-call | flops 4194304 | bytes 33554432 | tf_op jit(solution)/shard_map/theta/pallas_call | solution.py:932
  165.4 0.3 collective-permute-done.refs_2_
  165.7 0.7 copy-done.3
  166.4 6.6 %join.1 = f32[16,2,64,256]{3,2,1,0:T(8,128)} custom-call(s32[1]{0:T(128)} %bitcast.10.refs_0_, f32[4,2,64,1024]{3,2,1,0:T(8,128)} %get-tuple-element.45.refs_1_, f32[64,1024]{1,0:T(8,128)} %copy-done.3, bf16[256,256]{1,0:T(8,128)(2,1)} %constant.173.clone.refs_4_.refs_2_.refs_3_.refs_12_, bf16[256,256]{1,0:T(8,128)(2,1)} %constant.174.clone.refs_5_.refs_3_.refs_4_.refs_13_, ...), custom_call_target="tpu_custom_call" | custom-call | tf_op jit(solution)/shard_map/join/pallas_call | solution.py:944
  172.9 3.7 %all-to-all-start.1 = ((f32[16,2,64,256]{3,2,1,0:T(8,128)}), f32[16,2,64,256]{3,2,1,0:T(8,128)S(1)}, u32[]{:S(2)}, u32[]{:S(2)}) async-start(f32[16,2,64,256]{3,2,1,0:T(8,128)} %join.1), calls=%async_computation.1 | async-start | bytes 4194304 | tf_op jit(solution)/shard_map/all_to_all | solution.py:957
  176.7 32.3 %facet_temp.1 = f32[8,128]{1,0:T(8,128)} custom-call(f32[8,128]{1,0:T(8,128)} %temp_gather.1.refs_0_, f32[8,128]{1,0:T(8,128)} %bitcast.52, f32[8,128]{1,0:T(8,128)} %bitcast.55, f32[8,128]{1,0:T(8,128)} %bitcast.56, f32[8,128]{1,0:T(8,128)} %bitcast.54, f32[4,8,128]{2,1,0:T(8,128)} %get-tuple-element.58.refs_5_), custom_call_target="tpu_custom_call" | custom-call | bytes 16777216 | tf_op jit(solution)/shard_map/facet_temp/pallas_call | solution.py:769
  209.0 0.0 all-to-all-done.1.refs_0_
  209.0 0.0 copy-start
  209.0 1.3 copy-done
  210.3 10.5 %spread.1 = (f32[2,256,1024]{2,1,0:T(8,128)}, f32[2,16,1024]{2,1,0:T(8,128)}) custom-call(f32[16,2,64,256]{3,2,1,0:T(8,128)} %copy-done, bf16[256,256]{1,0:T(8,128)(2,1)} %constant.179.clone.refs_10_.refs_9_.refs_1_, bf16[256,256]{1,0:T(8,128)(2,1)} %constant.180.clone.refs_11_.refs_10_.refs_2_, ...), custom_call_target="tpu_custom_call" | custom-call | tf_op jit(solution)/shard_map/spread/pallas_call | solution.py:958
  220.8 8.3 %all-gather.1 = f32[8,16,1024]{2,1,0:T(8,128)} all-gather(f32[2,16,1024]{2,1,0:T(8,128)} %get-tuple-element.54), channel_id=3, replica_groups=mesh['px'=4,'py_half'=2,'py_low'=4] {'px'}, dimensions={0}, use_global_device_ids=true | all-gather | bytes 655360 | tf_op jit(solution)/shard_map/all_gather | solution.py:971
  229.1 38.0 %inverse.1 = f32[16,256,1024]{2,1,0:T(8,128)} custom-call(s32[1]{0:T(128)} %bitcast.refs_0_, f32[16,256,1024]{2,1,0:T(8,128)} %get-tuple-element.37.refs_1_, f32[2,256,1024]{2,1,0:T(8,128)} %get-tuple-element.53.refs_2_, f32[4,2,16,1024]{3,2,1,0:T(8,128)} %bitcast.45, f32[4,2,16,1024]{3,2,1,0:T(8,128)} %bitcast.46, ...), custom_call_target="tpu_custom_call" | custom-call | tf_op jit(solution)/shard_map/inverse/pallas_call | solution.py:976
  267.2 0.6 copy.49
  (16 shorter events, 0.1 us)
Async XLA Ops:
  5.1 34.9 %copy-start.4 = (s32[1,1024]{1,0:T(1,128)S(1)}, s32[1,1024]{1,0:T(1,128)}, u32[]{:S(2)}) copy-start(s32[1,1024]{1,0:T(1,128)} %param.42) | copy-start | bytes 12292
  41.8 56.6 %copy-start.2 = (f32[4,4]{1,0:T(4,128)S(1)}, f32[4,4]{1,0:T(4,128)}, u32[]{:S(2)}) copy-start(f32[4,4]{1,0:T(4,128)} %constant.192.clone) | copy-start | bytes 196
  41.8 58.2 %copy-start.8 = (f32[16,16]{1,0:T(8,128)S(1)}, f32[16,16]{1,0:T(8,128)}, u32[]{:S(2)}) copy-start(f32[16,16]{1,0:T(8,128)} %constant.188.clone) | copy-start | bytes 3076
  41.8 58.2 %copy-start.9 = (f32[16,16]{1,0:T(8,128)S(1)}, f32[16,16]{1,0:T(8,128)}, u32[]{:S(2)}) copy-start(f32[16,16]{1,0:T(8,128)} %constant.187.clone) | copy-start | bytes 3076
  41.8 58.2 %copy-start.10 = (f32[16,16]{1,0:T(8,128)S(1)}, f32[16,16]{1,0:T(8,128)}, u32[]{:S(2)}) copy-start(f32[16,16]{1,0:T(8,128)} %constant.186.clone) | copy-start | bytes 3076
  111.3 4.1 %copy-start.5 = (f32[1024]{0:T(1024)S(1)}, f32[1024]{0:T(1024)}, u32[]{:S(2)}) copy-start(f32[1024]{0:T(1024)} %constant.183.clone) | copy-start | bytes 12292
  111.3 31.8 %all-to-all-start = ((f32[16,2,64,256]{3,2,1,0:T(8,128)}), f32[16,2,64,256]{3,2,1,0:T(8,128)S(1)}, u32[]{:S(2)}, u32[]{:S(2)}) async-start(f32[16,2,64,256]{3,2,1,0:T(8,128)} %edges.1), calls=%async_computation | async-start | bytes 4194304 | tf_op jit(solution)/shard_map/all_to_all | solution.py:917
  115.5 12.9 %copy-start.7 = (f32[3,8,128]{2,1,0:T(8,128)S(1)}, f32[3,8,128]{2,1,0:T(8,128)}, u32[]{:S(2)}) copy-start(f32[3,8,128]{2,1,0:T(8,128)} %get-tuple-element.32) | copy-start | bytes 36868
  143.1 1.3 copy-start.1
  150.4 15.3 %collective-permute-start = (f32[64,1024]{1,0:T(8,128)}, f32[64,1024]{1,0:T(8,128)S(1)}, u32[]{:S(2)}, u32[]{:S(2)}) collective-permute-start(f32[64,1024]{1,0:T(8,128)} %get-tuple-element.48), channel_id=1, source_target_pairs={{0,4},{4,0},{1,5},{5,1},{2,6},{6,2},{3,7},{7,3},{8,12},{12,8},{9,1... | collective-permute-start | bytes 786440 | tf_op jit(solution)/shard_map/ppermute | solution.py:942
  165.7 0.7 copy-start.3
  172.9 36.1 %all-to-all-start.1 = ((f32[16,2,64,256]{3,2,1,0:T(8,128)}), f32[16,2,64,256]{3,2,1,0:T(8,128)S(1)}, u32[]{:S(2)}, u32[]{:S(2)}) async-start(f32[16,2,64,256]{3,2,1,0:T(8,128)} %join.1), calls=%async_computation.1 | async-start | bytes 4194304 | tf_op jit(solution)/shard_map/all_to_all | solution.py:957
  209.0 1.3 copy-start
  229.1 38.1 %copy-start.6 = (f32[8,128]{1,0:T(8,128)S(1)}, f32[8,128]{1,0:T(8,128)}, u32[]{:S(2)}) copy-start(f32[8,128]{1,0:T(8,128)} %facet_temp.1) | copy-start | bytes 12292

commit v7 on v5

--- a/solution.py
+++ b/solution.py
@@ -15,6 +15,7 @@
 VMEM = pl.BlockSpec(memory_space=pltpu.VMEM)
 SMEM = pl.BlockSpec(memory_space=pltpu.SMEM)
 PARAMS = pltpu.CompilerParams(vmem_limit_bytes=58 * 2**20)
+SMALL = pltpu.CompilerParams(vmem_limit_bytes=28 * 2**20)
 
 
 def two_halves(table):
@@ -723,10 +724,8 @@
     return (own.reshape(count) - facet_sums(ids, returned[0]), returned, w_cell, tables)
 
 
-def warm_air(temp_rows, ids, places, returned, w_cell, facet_temp, net_radiation, heat_capacity, heat_coef):
+def warm_air(temp_rows, ids, places, returned):
     count = ids.shape[0]
-    sizes = tuple(lax.axis_size(name) for name in ("px", "py_half", "py_low"))
-    slots = count // (sizes[0] * sizes[1] * sizes[2])
     flat = (count // 128, 128)
     own = pl.pallas_call(
         gather_temp_kernel,
@@ -738,6 +737,14 @@
         cost_estimate=pl.CostEstimate(flops=0, bytes_accessed=4 * temp_rows.size, transcendentals=0),
         name="temp_gather",
     )(places, temp_rows)
+    heat_flux = returned[1] * (returned[2] - own)
+    return (own, own.reshape(count) + facet_sums(ids, heat_flux))
+
+
+def warm_facets(own, w_cell, facet_temp, net_radiation, heat_capacity, heat_coef):
+    flat = own.shape
+    sizes = tuple(lax.axis_size(name) for name in ("px", "py_half", "py_low"))
+    slots = own.size // (sizes[0] * sizes[1] * sizes[2])
     tall = pltpu.VMEM((128 // slots, flat[0], 1, 128), F32)
     new_temp = pl.pallas_call(
         lambda *refs: facet_temp_kernel(sizes, slots, *refs),
@@ -749,8 +756,7 @@
         cost_estimate=pl.CostEstimate(flops=0, bytes_accessed=2**24, transcendentals=0),
         name="facet_temp",
     )(own, *[a.reshape(flat) for a in (facet_temp, net_radiation, heat_capacity, heat_coef)], w_cell)
-    heat_flux = returned[1] * (returned[2] - own)
-    return (own.reshape(count) + facet_sums(ids, heat_flux), new_temp.reshape(count))
+    return new_temp.reshape(facet_temp.shape)
 
 
 def body(
@@ -830,7 +836,7 @@
     tile = math.gcd(rows, 32)
     tiles = rows // tile
     flat = lambda i: pl.BlockSpec((tile, width), i)
-    fixed = lambda a: pl.BlockSpec(a.shape, lambda i: (0,) * a.ndim)
+    fixed = lambda a: pl.BlockSpec(a.shape, lambda i: (0,) * len(a.shape))
     pairs = levels // 2
     late = lambda i: (jnp.maximum(i - pairs, 0), 0)
     down = lambda i: (jnp.maximum(pairs - 1 - i, 0), 0, 0)
@@ -876,24 +882,14 @@
         in_specs=[VMEM] * 11,
         out_specs=VMEM,
         scratch_shapes=working + [pltpu.VMEM((2, rows, width), F32)],
-        compiler_params=PARAMS,
+        compiler_params=SMALL,
         name="edges",
     )(edges, all_ends, weights, vectors, root, inv, start, top, end, *to_modes)
     w_cell, edges = lax.optimization_barrier((w_cell, edges))
     places_late, edges = lax.optimization_barrier((places, edges))
-    temp_near, new_temp = warm_air(
-        temp_rows,
-        ids,
-        places_late,
-        returned,
-        w_cell,
-        facet_temp[0],
-        net_radiation[0],
-        heat_capacity[0],
-        heat_coef[0],
-    )
+    temp_own, temp_near = warm_air(temp_rows, ids, places_late, returned)
     edges = lax.all_to_all(edges, ("px", "py_low"), split_axis=0, concat_axis=0, tiled=True)
-    edges, temp_near, new_temp = lax.optimization_barrier((edges, temp_near, new_temp))
+    edges, temp_near = lax.optimization_barrier((edges, temp_near))
     half_id = half.astype(jnp.int32).reshape(1)
     modes, alpha = pl.pallas_call(
         lambda *refs: gather_modes_kernel(levels, px_count, *refs),
@@ -903,17 +899,22 @@
         ),
         in_specs=[SMEM] + [VMEM] * 8,
         out_specs=(VMEM, VMEM),
-        compiler_params=PARAMS,
+        compiler_params=SMALL,
         name="gather_modes",
     )(half_id, edges, *y_tables, join_root)
+    alpha, temp_own = lax.optimization_barrier((alpha, temp_own))
+    new_temp = warm_facets(
+        temp_own, w_cell, facet_temp[0], net_radiation[0], heat_capacity[0], heat_coef[0]
+    )
     alpha = lax.ppermute(alpha, "py_half", [(0, 1), (1, 0)])
+    alpha, new_temp = lax.optimization_barrier((alpha, new_temp))
     joined = pl.pallas_call(
         lambda *refs: join_kernel(levels, px_count, *refs),
         out_shape=packed,
         in_specs=[SMEM] + [VMEM] * 9,
         out_specs=VMEM,
         scratch_shapes=[pltpu.VMEM((blocks, 2, own_kx, y_cells), F32)],
-        compiler_params=PARAMS,
+        compiler_params=SMALL,
         name="join",
     )(half_id, modes, alpha, *y_tables, join_root)
     joined, temp_near = lax.optimization_barrier((joined, temp_near))
@@ -934,7 +935,7 @@
         in_specs=[VMEM] * 8,
         out_specs=(VMEM, VMEM),
         scratch_shapes=working,
-        compiler_params=PARAMS,
+        compiler_params=SMALL,
         name="spread",
     )(joined, *to_modes, root, start, from_below, top, end)
     more = lax.all_gather(more, "px")

time: 270 us -> 280 us (1.037)
  local copies, waits for them, and re-layouts: 5.36 us -> 25.4 us
  Pallas kernels: 198 us -> 187 us
    unnamed x23 -> x73, local copies, waits for them, and re-layouts: 3.96 us -> 24 us
    ppermute x1, waiting for transfers between devices: 14.3 us -> 0.01 us  [body(): alpha = lax.ppermute(alpha, 'py_half', [(0, 1), (1, 0)])]
    all_to_all x1, waiting for transfers between devices: 0.01 us -> 12 us  [body(): lax.all_to_all(edges, ('px', 'py_low'), split_axis=0, concat_axis=0, tile...]
    pallas_call x1, Pallas kernels: 9.8 us -> 5.25 us  [body(): pl.pallas_call(lambda *refs: edge_kernel(levels, *refs), out_shape=packed...]
  transfers between devices with their start and end apart: 3 -> 3, of which waited for: 2 -> 2; matrix products, arithmetic and copies ran while one was open for 1% -> 1% of each run, Pallas kernels for 17% -> 16%
where the time goes in v7:
time: 280 us; the launch traced here: 278 us
  Pallas kernels  187 us (67%)
  local copies, waits for them, and re-layouts  25.4 us (9%)
  waiting for transfers between devices  25.4 us (9%)
  blocking collectives  17.4 us (6%)
  other arithmetic  11.7 us (4%)
  starting transfers between devices  9.62 us (3%)
    pallas_call x1, Pallas kernels, body(): pl.pallas_call(lambda *refs: forward_kernel(levels, tile, *refs), out_sha...  48.8 us
    pallas_call x1, Pallas kernels, body(): pl.pallas_call(lambda *refs: inverse_kernel(levels, tile, *refs), out_sha...  38 us
    unnamed x73, local copies, waits for them, and re-layouts  24 us
    pallas_call x1, Pallas kernels, near_walls(): pl.pallas_call(lambda *refs: stress_kernel(sizes, slots, *refs), out_shap...  19.3 us
    pallas_call x1, Pallas kernels, warm_facets(): pl.pallas_call(lambda *refs: facet_temp_kernel(sizes, slots, *refs), out_...  17.8 us
    pallas_call x1, Pallas kernels, near_walls(): pl.pallas_call(lambda *refs: gather_kernel(w_rows.shape[0] // rows, *refs...  14.9 us
    pallas_call x1, Pallas kernels, body(): pl.pallas_call(theta_kernel, out_shape=jax.ShapeDtypeStruct(temp_rows.sha...  14.5 us
    all_to_all x1, waiting for transfers between devices, body(): lax.all_to_all(joined, ('px', 'py_low'), split_axis=0, concat_axis=0, til...  13.4 us
  transfers between devices with their start and end apart: 3, of which 2 were waited for; matrix products, arithmetic and copies ran while one was open for 1% of the time, Pallas kernels for 16%

profile of v7, /device:TPU:0, one launch (start us, length us, event | category | flops | bytes accessed | tf_op | source)
XLA Modules:
  0.0 277.8 jit_solution(4231213076928943684)
XLA Ops:
  0.8 0.8 and_select_fusion.4
  1.5 0.7 compare_select_fusion.2
  2.3 0.7 broadcast_select_fusion.1
  3.0 0.9 add_divide_fusion.3
  3.9 0.7 pad_maximum_fusion
  5.8 14.9 %facet_gather.1 = (f32[8,128]{1,0:T(8,128)}, f32[256,1024]{1,0:T(8,128)}, f32[256,1024]{1,0:T(8,128)}, f32[256,1024]{1,0:T(8,128)}, f32[256,1024]{1,0:T(8,128)}, /*index=5*/f32[256,1024]{1,0:T(8,128)}) custom-call(s32[3,1024]{1,0:T(4,128)} %pad_add_fusion.refs_0_.ids_ref, s32[2]{0:T(128)} %add_convert_fusion.refs_1_, f32[4096,1024]{1,0:T(8,128)} %bitcast.41, ...), custom_call_target="tpu_custom_call" | custom-call | tf_op jit(solution)/shard_map/facet_gather/pallas_call | solution.py:697
  20.7 19.3 %stress_exchange.1 = (f32[3,8,128]{2,1,0:T(8,128)}, f32[4,8,128]{2,1,0:T(8,128)}) custom-call(f32[8,128]{1,0:T(8,128)} %get-tuple-element.31.refs_0_, f32[8,128]{1,0:T(8,128)} %bitcast.52, f32[8,128]{1,0:T(8,128)} %bitcast.58, f32[8,128]{1,0:T(8,128)} %bitcast.54), custom_call_target="tpu_custom_call" | custom-call | tf_op jit(solution)/shard_map/stress_exchange/pallas_call | solution.py:714
  41.2 1.3 bitcast_subtract_fusion.1.refs_1_
  42.5 48.8 %forward.1 = (f32[16,256,1024]{2,1,0:T(8,128)}, f32[2,256,1024]{2,1,0:T(8,128)}, f32[2,16,1024]{2,1,0:T(8,128)}, f32[4096,1024]{1,0:T(8,128)}) custom-call(s32[3,1024]{1,0:T(4,128)} %pad_add_fusion.refs_0_.ids_ref, f32[1024]{0:T(1024)} %bitcast_subtract_fusion.1.refs_1_, f32[4096,1024]{1,0:T(8,128)} %bitcast.42, f32[16,256,1024]{2,1,0:T(8,128)} %refs_3_.3, ...), custom_call_target="tpu_custom_call" | custom-call | tf_op jit(solution)/shard_map/forward/pallas_call | solution.py:846
  91.4 8.4 %all-gather = f32[8,16,1024]{2,1,0:T(8,128)} all-gather(f32[2,16,1024]{2,1,0:T(8,128)} %get-tuple-element.40), channel_id=2, replica_groups=mesh['px'=4,'py_half'=2,'py_low'=4] {'px'}, dimensions={0}, use_global_device_ids=true | all-gather | bytes 655360 | tf_op jit(solution)/shard_map/all_gather | solution.py:876
  100.3 1.3 multiply_reduce_fusion.refs_2_.refs_5_
  101.6 0.8 select_select_fusion.refs_3_.refs_6_
  102.5 1.0 copy-done.9
  103.5 1.2 copy-done.12
  104.8 1.6 copy-done.25
  106.4 5.2 %edges.1 = f32[16,2,64,256]{3,2,1,0:T(8,128)S(1)} custom-call(f32[2,256,1024]{2,1,0:T(8,128)S(1)} %copy-done.25, f32[4,2,16,1024]{3,2,1,0:T(8,128)S(1)} %bitcast.40, f32[2,4,16,1024]{3,2,1,0:T(8,128)S(1)} %multiply_reduce_fusion.refs_2_.refs_5_, f32[16,16]{1,0:T(8,128)S(1)} %select_select_fusion.refs_3_.refs_6_, f32[256,1024]{1,0:T(8,128)S(1)} %copy-done, ...), custom_call_target="tpu_custom_call" | custom-call | tf_op jit(solution)/shard_map/edges/pallas_call | solution.py:879
  111.6 1.3 copy-done.8
  112.9 4.7 %all-to-all-start = ((f32[16,2,64,256]{3,2,1,0:T(8,128)}), f32[16,2,64,256]{3,2,1,0:T(8,128)}, u32[]{:S(2)}, u32[]{:S(2)}) async-start(f32[16,2,64,256]{3,2,1,0:T(8,128)} %copy-done.8), calls=%async_computation | async-start | bytes 4194304 | tf_op jit(solution)/shard_map/all_to_all | solution.py:891
  117.8 12.9 %temp_gather.1.refs_0_ = f32[8,128]{1,0:T(8,128)} custom-call(s32[3,1024]{1,0:T(4,128)} %pad_add_fusion.refs_0_.ids_ref, bf16[4096,1024]{1,0:T(8,128)(2,1)} %bitcast.43), custom_call_target="tpu_custom_call" | custom-call | bytes 16777216 | tf_op jit(solution)/shard_map/temp_gather/pallas_call | solution.py:730
  130.7 0.7 fusion.7
  132.0 1.3 bitcast_add_fusion.new_ref
  133.5 12.0 %all-to-all-done.refs_1_ = f32[16,2,64,256]{3,2,1,0:T(8,128)} async-done(((f32[16,2,64,256]{3,2,1,0:T(8,128)}), f32[16,2,64,256]{3,2,1,0:T(8,128)}, u32[]{:S(2)}, u32[]{:S(2)}) %all-to-all-start) | async-done | bytes 2097184 | tf_op jit(solution)/shard_map/all_to_all | solution.py:891
  145.5 1.0 copy-done.3
  146.5 1.0 copy-done.5
  147.6 0.9 copy-done.14
  148.5 0.9 copy-done.16
  149.4 0.9 copy-done.18
  150.3 0.9 copy-done.20
  151.2 4.8 %gather_modes.1 = (f32[4,2,64,1024]{3,2,1,0:T(8,128)S(1)}, f32[64,1024]{1,0:T(8,128)}) custom-call(s32[1]{0:T(128)} %bitcast.10.refs_0_, f32[16,2,64,256]{3,2,1,0:T(8,128)} %all-to-all-done.refs_1_, bf16[256,256]{1,0:T(8,128)(2,1)S(1)} %copy-done.20, bf16[256,256]{1,0:T(8,128)(2,1)S(1)} %copy-done.18, bf16[256,256]{1,0:T(8,128)(2,1)S(1)} %copy-done.16, ...), custom_call_target="tpu_custom_call" | custom-call | tf_op jit(solution)/shard_map/gather_modes/pallas_call | solution.py:894
  156.0 1.3 copy-done.23
  157.7 17.8 %facet_temp.1 = f32[8,128]{1,0:T(8,128)} custom-call(f32[8,128]{1,0:T(8,128)} %temp_gather.1.refs_0_, f32[8,128]{1,0:T(8,128)} %bitcast.53, f32[8,128]{1,0:T(8,128)} %bitcast.56, f32[8,128]{1,0:T(8,128)} %bitcast.57, f32[8,128]{1,0:T(8,128)} %bitcast.55, f32[4,8,128]{2,1,0:T(8,128)} %get-tuple-element.49.refs_5_), custom_call_target="tpu_custom_call" | custom-call | bytes 16777216 | tf_op jit(solution)/shard_map/facet_temp/pallas_call | solution.py:749
  175.6 1.0 copy-done.4
  176.6 1.0 copy-done.6
  177.6 0.9 copy-done.15
  178.5 0.9 copy-done.17
  179.4 0.9 copy-done.19
  180.4 0.9 copy-done.21
  181.3 1.6 copy-done.24
  182.8 4.0 %join.1 = f32[16,2,64,256]{3,2,1,0:T(8,128)S(1)} custom-call(s32[1]{0:T(128)} %bitcast.10.refs_0_, f32[4,2,64,1024]{3,2,1,0:T(8,128)S(1)} %copy-done.24, f32[64,1024]{1,0:T(8,128)} %collective-permute-done.refs_2_, bf16[256,256]{1,0:T(8,128)(2,1)S(1)} %copy-done.21, bf16[256,256]{1,0:T(8,128)(2,1)S(1)} %copy-done.19, bf16[256,256]{1,0:T(8,128)(2,1)S(1)} %copy-done.17, ...), custom_call_target="tpu_custom_call" | custom-call | tf_op jit(solution)/shard_map/join/pallas_call | solution.py:911
  186.9 1.3 copy-done.7
  188.2 4.4 %all-to-all-start.1 = ((f32[16,2,64,256]{3,2,1,0:T(8,128)}), f32[16,2,64,256]{3,2,1,0:T(8,128)}, u32[]{:S(2)}, u32[]{:S(2)}) async-start(f32[16,2,64,256]{3,2,1,0:T(8,128)} %copy-done.7), calls=%async_computation.1 | async-start | bytes 4194304 | tf_op jit(solution)/shard_map/all_to_all | solution.py:931
  192.6 14.5 %theta.1 = bf16[4096,1024]{1,0:T(8,128)(2,1)} custom-call(s32[3,1024]{1,0:T(4,128)} %pad_add_fusion.refs_0_.ids_ref, f32[1024]{0:T(1024)} %bitcast_add_fusion.new_ref, bf16[4096,1024]{1,0:T(8,128)(2,1)} %bitcast.44), custom_call_target="tpu_custom_call" | custom-call | flops 4194304 | bytes 33554432 | tf_op jit(solution)/shard_map/theta/pallas_call | solution.py:921
  207.2 13.4 %all-to-all-done.1.refs_0_ = f32[16,2,64,256]{3,2,1,0:T(8,128)} async-done(((f32[16,2,64,256]{3,2,1,0:T(8,128)}), f32[16,2,64,256]{3,2,1,0:T(8,128)}, u32[]{:S(2)}, u32[]{:S(2)}) %all-to-all-start.1) | async-done | bytes 2097184 | tf_op jit(solution)/shard_map/all_to_all | solution.py:931
  220.6 1.2 copy-done.11
  221.8 7.1 %spread.1 = (f32[2,256,1024]{2,1,0:T(8,128)S(1)}, f32[2,16,1024]{2,1,0:T(8,128)S(1)}) custom-call(f32[16,2,64,256]{3,2,1,0:T(8,128)} %all-to-all-done.1.refs_0_, bf16[256,256]{1,0:T(8,128)(2,1)S(1)} %copy-done.29, bf16[256,256]{1,0:T(8,128)(2,1)S(1)} %copy-done.27, f32[256,1024]{1,0:T(8,128)S(1)} %copy-done, f32[256,1024]{1,0:T(8,128)S(1)} %copy-done.1, ...), custom_call_target="tpu_custom_call" | custom-call | tf_op jit(solution)/shard_map/spread/pallas_call | solution.py:932
  228.9 1.3 copy-done.22
  230.2 9.0 %all-gather.1 = f32[8,16,1024]{2,1,0:T(8,128)} all-gather(f32[2,16,1024]{2,1,0:T(8,128)S(1)} %get-tuple-element.55), channel_id=3, replica_groups=mesh['px'=4,'py_half'=2,'py_low'=4] {'px'}, dimensions={0}, use_global_device_ids=true | all-gather | bytes 655360 | tf_op jit(solution)/shard_map/all_gather | solution.py:941
  239.1 38.0 %inverse.1 = f32[16,256,1024]{2,1,0:T(8,128)} custom-call(s32[1]{0:T(128)} %bitcast.refs_0_, f32[16,256,1024]{2,1,0:T(8,128)} %get-tuple-element.37.refs_1_, f32[2,256,1024]{2,1,0:T(8,128)} %copy-done.22, f32[4,2,16,1024]{3,2,1,0:T(8,128)} %bitcast.39, f32[4,2,16,1024]{3,2,1,0:T(8,128)} %bitcast.47, f32[2,4,16,1024]{3,2,1,0:T(8,128)} %copy-done.10, ...), custom_call_target="tpu_custom_call" | custom-call | tf_op jit(solution)/shard_map/inverse/pallas_call | solution.py:946
  (66 shorter events, 5.1 us)
Async XLA Ops:
  5.8 34.9 %copy-start.32 = (s32[1,1024]{1,0:T(1,128)S(1)}, s32[1,1024]{1,0:T(1,128)}, u32[]{:S(2)}) copy-start(s32[1,1024]{1,0:T(1,128)} %param.42) | copy-start | bytes 12292
  42.5 57.3 %copy-start.31 = (f32[4,4]{1,0:T(4,128)S(1)}, f32[4,4]{1,0:T(4,128)}, u32[]{:S(2)}) copy-start(f32[4,4]{1,0:T(4,128)} %constant.192.clone) | copy-start | bytes 196
  42.5 60.0 %copy-start = (f32[256,1024]{1,0:T(8,128)S(1)}, f32[256,1024]{1,0:T(8,128)}, u32[]{:S(2)}) copy-start(f32[256,1024]{1,0:T(8,128)} %get-tuple-element.33.refs_12_.refs_4_.refs_3_.refs_7_) | copy-start | bytes 3145732
  42.5 60.0 %copy-start.1 = (f32[256,1024]{1,0:T(8,128)S(1)}, f32[256,1024]{1,0:T(8,128)}, u32[]{:S(2)}) copy-start(f32[256,1024]{1,0:T(8,128)} %get-tuple-element.35.refs_14_.refs_6_.refs_4_.refs_8_) | copy-start | bytes 3145732
  42.5 60.0 %copy-start.2 = (f32[256,1024]{1,0:T(8,128)S(1)}, f32[256,1024]{1,0:T(8,128)}, u32[]{:S(2)}) copy-start(f32[256,1024]{1,0:T(8,128)} %get-tuple-element.36.refs_15_.refs_7_.refs_6_.refs_10_) | copy-start | bytes 3145732
  42.5 60.0 %copy-start.13 = (f32[256,128]{1,0:T(8,128)S(1)}, f32[256,128]{1,0:T(8,128)}, u32[]{:S(2)}) copy-start(f32[256,128]{1,0:T(8,128)} %constant.185.clone.refs_16_.refs_8_.refs_7_.refs_11_) | copy-start | bytes 393220
  42.5 60.0 %copy-start.26 = (bf16[256,256]{1,0:T(8,128)(2,1)S(1)}, bf16[256,256]{1,0:T(8,128)(2,1)}, u32[]{:S(2)}) copy-start(bf16[256,256]{1,0:T(8,128)(2,1)} %constant.180.clone.refs_11_.refs_10_.refs_2_) | copy-start | bytes 393220
  42.5 60.0 %copy-start.28 = (bf16[256,256]{1,0:T(8,128)(2,1)S(1)}, bf16[256,256]{1,0:T(8,128)(2,1)}, u32[]{:S(2)}) copy-start(bf16[256,256]{1,0:T(8,128)(2,1)} %constant.179.clone.refs_10_.refs_9_.refs_1_) | copy-start | bytes 393220
  101.6 10.0 %copy-start.10 = (f32[2,4,16,1024]{3,2,1,0:T(8,128)}, f32[2,4,16,1024]{3,2,1,0:T(8,128)S(1)}, u32[]{:S(2)}) copy-start(f32[2,4,16,1024]{3,2,1,0:T(8,128)S(1)} %multiply_reduce_fusion.refs_2_.refs_5_) | copy-start | bytes 1572868
  102.4 9.2 %copy-start.30 = (f32[16,16]{1,0:T(8,128)}, f32[16,16]{1,0:T(8,128)S(1)}, u32[]{:S(2)}) copy-start(f32[16,16]{1,0:T(8,128)S(1)} %select_select_fusion.refs_3_.refs_6_) | copy-start | bytes 3076
  102.5 1.0 copy-start.9
  103.5 1.2 copy-start.12
  104.8 1.6 copy-start.25
  111.6 1.3 copy-start.8
  112.9 4.8 %copy-start.33 = (f32[1024]{0:T(1024)S(1)}, f32[1024]{0:T(1024)}, u32[]{:S(2)}) copy-start(f32[1024]{0:T(1024)} %constant.183.clone) | copy-start | bytes 12292
  112.9 32.5 %all-to-all-start = ((f32[16,2,64,256]{3,2,1,0:T(8,128)}), f32[16,2,64,256]{3,2,1,0:T(8,128)}, u32[]{:S(2)}, u32[]{:S(2)}) async-start(f32[16,2,64,256]{3,2,1,0:T(8,128)} %copy-done.8), calls=%async_computation | async-start | bytes 4194304 | tf_op jit(solution)/shard_map/all_to_all | solution.py:891
  117.8 12.9 %copy-start.35 = (f32[3,8,128]{2,1,0:T(8,128)S(1)}, f32[3,8,128]{2,1,0:T(8,128)}, u32[]{:S(2)}) copy-start(f32[3,8,128]{2,1,0:T(8,128)} %get-tuple-element.32) | copy-start | bytes 36868
  145.5 1.0 copy-start.3
  146.5 1.0 copy-start.5
  147.5 0.9 copy-start.14
  148.5 0.9 copy-start.16
  149.4 0.9 copy-start.18
  150.3 0.9 copy-start.20
  156.0 1.3 copy-start.23
  157.3 18.2 %collective-permute-start = (f32[64,1024]{1,0:T(8,128)}, f32[64,1024]{1,0:T(8,128)}, u32[]{:S(2)}, u32[]{:S(2)}) collective-permute-start(f32[64,1024]{1,0:T(8,128)} %get-tuple-element.47), channel_id=1, source_target_pairs={{0,4},{4,0},{1,5},{5,1},{2,6},{6,2},{3,7},{7,3},{8,12},{12,8},{9,1... | collective-permute-start | bytes 786440 | tf_op jit(solution)/shard_map/ppermute | solution.py:909
  175.5 1.0 copy-start.4
  176.6 1.0 copy-start.6
  177.6 0.9 copy-start.15
  178.5 0.9 copy-start.17
  179.4 0.9 copy-start.19
  180.3 0.9 copy-start.21
  181.3 1.6 copy-start.24
  186.8 1.3 copy-start.7
  188.2 32.4 %all-to-all-start.1 = ((f32[16,2,64,256]{3,2,1,0:T(8,128)}), f32[16,2,64,256]{3,2,1,0:T(8,128)}, u32[]{:S(2)}, u32[]{:S(2)}) async-start(f32[16,2,64,256]{3,2,1,0:T(8,128)} %copy-done.7), calls=%async_computation.1 | async-start | bytes 4194304 | tf_op jit(solution)/shard_map/all_to_all | solution.py:931
  192.6 27.9 %copy-start.27 = (bf16[256,256]{1,0:T(8,128)(2,1)S(1)}, bf16[256,256]{1,0:T(8,128)(2,1)}, u32[]{:S(2)}) copy-start(bf16[256,256]{1,0:T(8,128)(2,1)} %constant.180.clone.refs_11_.refs_10_.refs_2_) | copy-start | bytes 393220
  192.6 27.9 %copy-start.29 = (bf16[256,256]{1,0:T(8,128)(2,1)S(1)}, bf16[256,256]{1,0:T(8,128)(2,1)}, u32[]{:S(2)}) copy-start(bf16[256,256]{1,0:T(8,128)(2,1)} %constant.179.clone.refs_10_.refs_9_.refs_1_) | copy-start | bytes 393220
  220.6 1.2 copy-start.11
  228.9 1.3 copy-start.22
  239.1 38.0 %copy-start.34 = (f32[8,128]{1,0:T(8,128)S(1)}, f32[8,128]{1,0:T(8,128)}, u32[]{:S(2)}) copy-start(f32[8,128]{1,0:T(8,128)} %facet_temp.1) | copy-start | bytes 12292

commit v8 on v7

--- a/solution.py
+++ b/solution.py
@@ -899,7 +899,7 @@
         ),
         in_specs=[SMEM] + [VMEM] * 8,
         out_specs=(VMEM, VMEM),
-        compiler_params=SMALL,
+        compiler_params=PARAMS,
         name="gather_modes",
     )(half_id, edges, *y_tables, join_root)
     alpha, temp_own = lax.optimization_barrier((alpha, temp_own))
@@ -914,7 +914,7 @@
         in_specs=[SMEM] + [VMEM] * 9,
         out_specs=VMEM,
         scratch_shapes=[pltpu.VMEM((blocks, 2, own_kx, y_cells), F32)],
-        compiler_params=SMALL,
+        compiler_params=PARAMS,
         name="join",
     )(half_id, modes, alpha, *y_tables, join_root)
     joined, temp_near = lax.optimization_barrier((joined, temp_near))

time: 280 us -> 267 us (0.954)
  local copies, waits for them, and re-layouts: 25.4 us -> 9.74 us
  Pallas kernels: 187 us -> 191 us
    unnamed x73 -> x39, local copies, waits for them, and re-layouts: 24 us -> 8.34 us
  transfers between devices with their start and end apart: 3 -> 3, of which waited for: 2 -> 2; matrix products, arithmetic and copies ran while one was open for 1% -> 1% of each run, Pallas kernels for 16% -> 17%
where the time goes in v8:
time: 267 us; the launch traced here: 266 us
  Pallas kernels  191 us (72%)
  waiting for transfers between devices  24.7 us (9%)
  blocking collectives  17.4 us (7%)
  other arithmetic  12.4 us (5%)
  local copies, waits for them, and re-layouts  9.74 us (4%)
  starting transfers between devices  9.68 us (4%)
    pallas_call x1, Pallas kernels, body(): pl.pallas_call(lambda *refs: forward_kernel(levels, tile, *refs), out_sha...  48.8 us
    pallas_call x1, Pallas kernels, body(): pl.pallas_call(lambda *refs: inverse_kernel(levels, tile, *refs), out_sha...  38 us
    pallas_call x1, Pallas kernels, near_walls(): pl.pallas_call(lambda *refs: stress_kernel(sizes, slots, *refs), out_shap...  19.3 us
    pallas_call x1, Pallas kernels, warm_facets(): pl.pallas_call(lambda *refs: facet_temp_kernel(sizes, slots, *refs), out_...  17.7 us
    pallas_call x1, Pallas kernels, near_walls(): pl.pallas_call(lambda *refs: gather_kernel(w_rows.shape[0] // rows, *refs...  14.9 us
    pallas_call x1, Pallas kernels, body(): pl.pallas_call(theta_kernel, out_shape=jax.ShapeDtypeStruct(temp_rows.sha...  14.5 us
    all_to_all x1, waiting for transfers between devices, body(): lax.all_to_all(joined, ('px', 'py_low'), split_axis=0, concat_axis=0, til...  13.5 us
    pallas_call x1, Pallas kernels, warm_air(): pl.pallas_call(gather_temp_kernel, out_shape=jax.ShapeDtypeStruct(flat, F...  12.9 us
  transfers between devices with their start and end apart: 3, of which 2 were waited for; matrix products, arithmetic and copies ran while one was open for 1% of the time, Pallas kernels for 17%

profile of v8, /device:TPU:0, one launch (start us, length us, event | category | flops | bytes accessed | tf_op | source)
XLA Modules:
  0.0 265.9 jit_solution(12846672135762223507)
XLA Ops:
  0.7 0.1 reshape.396
  0.8 0.8 and_select_fusion.4
  1.5 0.7 compare_select_fusion.2
  2.3 0.7 broadcast_select_fusion.1
  3.0 0.9 add_divide_fusion.3
  3.9 0.7 pad_maximum_fusion
  4.6 0.6 add_convert_fusion.refs_1_
  5.2 0.6 pad_add_fusion.refs_0_.ids_ref
  5.8 14.9 %facet_gather.1 = (f32[8,128]{1,0:T(8,128)}, f32[256,1024]{1,0:T(8,128)}, f32[256,1024]{1,0:T(8,128)}, f32[256,1024]{1,0:T(8,128)}, f32[256,1024]{1,0:T(8,128)}, /*index=5*/f32[256,1024]{1,0:T(8,128)}) custom-call(s32[3,1024]{1,0:T(4,128)} %pad_add_fusion.refs_0_.ids_ref, s32[2]{0:T(128)} %add_convert_fusion.refs_1_, f32[4096,1024]{1,0:T(8,128)} %bitcast.41, ...), custom_call_target="tpu_custom_call" | custom-call | tf_op jit(solution)/shard_map/facet_gather/pallas_call | solution.py:697
  20.7 19.3 %stress_exchange.1 = (f32[3,8,128]{2,1,0:T(8,128)}, f32[4,8,128]{2,1,0:T(8,128)}) custom-call(f32[8,128]{1,0:T(8,128)} %get-tuple-element.31.refs_0_, f32[8,128]{1,0:T(8,128)} %bitcast.52, f32[8,128]{1,0:T(8,128)} %bitcast.58, f32[8,128]{1,0:T(8,128)} %bitcast.54), custom_call_target="tpu_custom_call" | custom-call | tf_op jit(solution)/shard_map/stress_exchange/pallas_call | solution.py:714
  40.0 0.7 slice_bitcast_fusion
  40.7 0.5 fusion
  41.2 1.3 bitcast_subtract_fusion.1.refs_1_
  42.5 0.0 copy-start.8
  42.5 0.0 copy-start.11
  42.5 0.0 copy-start.12
  42.6 48.8 %forward.1 = (f32[16,256,1024]{2,1,0:T(8,128)}, f32[2,256,1024]{2,1,0:T(8,128)}, f32[2,16,1024]{2,1,0:T(8,128)}, f32[4096,1024]{1,0:T(8,128)}) custom-call(s32[3,1024]{1,0:T(4,128)} %pad_add_fusion.refs_0_.ids_ref, f32[1024]{0:T(1024)} %bitcast_subtract_fusion.1.refs_1_, f32[4096,1024]{1,0:T(8,128)} %bitcast.42, f32[16,256,1024]{2,1,0:T(8,128)} %refs_3_.3, ...), custom_call_target="tpu_custom_call" | custom-call | tf_op jit(solution)/shard_map/forward/pallas_call | solution.py:846
  91.4 8.4 %all-gather = f32[8,16,1024]{2,1,0:T(8,128)} all-gather(f32[2,16,1024]{2,1,0:T(8,128)} %get-tuple-element.40), channel_id=2, replica_groups=mesh['px'=4,'py_half'=2,'py_low'=4] {'px'}, dimensions={0}, use_global_device_ids=true | all-gather | bytes 655360 | tf_op jit(solution)/shard_map/all_gather | solution.py:876
  99.8 0.6 gather_fusion
  100.4 1.3 multiply_reduce_fusion.refs_2_.refs_5_
  101.6 0.8 select_select_fusion.refs_3_.refs_6_
  102.5 1.0 copy-done.4
  103.6 1.2 copy-done.7
  104.8 1.6 copy-done.10
  106.4 5.2 %edges.1 = f32[16,2,64,256]{3,2,1,0:T(8,128)S(1)} custom-call(f32[2,256,1024]{2,1,0:T(8,128)S(1)} %copy-done.10, f32[4,2,16,1024]{3,2,1,0:T(8,128)S(1)} %bitcast.40, f32[2,4,16,1024]{3,2,1,0:T(8,128)S(1)} %multiply_reduce_fusion.refs_2_.refs_5_, f32[16,16]{1,0:T(8,128)S(1)} %select_select_fusion.refs_3_.refs_6_, f32[256,1024]{1,0:T(8,128)S(1)} %copy-done, ...), custom_call_target="tpu_custom_call" | custom-call | tf_op jit(solution)/shard_map/edges/pallas_call | solution.py:879
  111.6 0.0 copy-start.3
  111.6 1.3 copy-done.3
  112.9 4.7 %all-to-all-start = ((f32[16,2,64,256]{3,2,1,0:T(8,128)}), f32[16,2,64,256]{3,2,1,0:T(8,128)}, u32[]{:S(2)}, u32[]{:S(2)}) async-start(f32[16,2,64,256]{3,2,1,0:T(8,128)} %copy-done.3), calls=%async_computation | async-start | bytes 4194304 | tf_op jit(solution)/shard_map/all_to_all | solution.py:891
  117.7 0.1 dynamic_slice.3
  117.8 12.9 %temp_gather.1.refs_0_ = f32[8,128]{1,0:T(8,128)} custom-call(s32[3,1024]{1,0:T(4,128)} %pad_add_fusion.refs_0_.ids_ref, bf16[4096,1024]{1,0:T(8,128)(2,1)} %bitcast.43), custom_call_target="tpu_custom_call" | custom-call | bytes 16777216 | tf_op jit(solution)/shard_map/temp_gather/pallas_call | solution.py:730
  130.7 0.7 fusion.7
  131.4 0.5 fusion.1
  132.0 1.3 bitcast_add_fusion.new_ref
  133.2 1.0 subtract_multiply_fusion.refs_8_.refs_9_
  134.2 11.3 %all-to-all-done.refs_1_ = f32[16,2,64,256]{3,2,1,0:T(8,128)} async-done(((f32[16,2,64,256]{3,2,1,0:T(8,128)}), f32[16,2,64,256]{3,2,1,0:T(8,128)}, u32[]{:S(2)}, u32[]{:S(2)}) %all-to-all-start) | async-done | bytes 2097184 | tf_op jit(solution)/shard_map/all_to_all | solution.py:891
  145.5 6.0 %gather_modes.1 = (f32[4,2,64,1024]{3,2,1,0:T(8,128)}, f32[64,1024]{1,0:T(8,128)}) custom-call(s32[1]{0:T(128)} %bitcast.10.refs_0_, f32[16,2,64,256]{3,2,1,0:T(8,128)} %all-to-all-done.refs_1_, bf16[256,256]{1,0:T(8,128)(2,1)} %constant.173.clone.refs_4_.refs_2_.refs_3_.refs_12_, bf16[256,256]{1,0:T(8,128)(2,1)} %constant.174.clone.refs_5_.refs_3_.refs_4_.refs_13_, ...), custom_call_target="tpu_custom_call" | custom-call | tf_op jit(solution)/shard_map/gather_modes/pallas_call | solution.py:894
  151.4 0.5 collective-permute-start
  151.9 17.7 %facet_temp.1 = f32[8,128]{1,0:T(8,128)} custom-call(f32[8,128]{1,0:T(8,128)} %temp_gather.1.refs_0_, f32[8,128]{1,0:T(8,128)} %bitcast.53, f32[8,128]{1,0:T(8,128)} %bitcast.56, f32[8,128]{1,0:T(8,128)} %bitcast.57, f32[8,128]{1,0:T(8,128)} %bitcast.55, f32[4,8,128]{2,1,0:T(8,128)} %get-tuple-element.49.refs_5_), custom_call_target="tpu_custom_call" | custom-call | bytes 16777216 | tf_op jit(solution)/shard_map/facet_temp/pallas_call | solution.py:749
  169.7 6.6 %join.1 = f32[16,2,64,256]{3,2,1,0:T(8,128)} custom-call(s32[1]{0:T(128)} %bitcast.10.refs_0_, f32[4,2,64,1024]{3,2,1,0:T(8,128)} %get-tuple-element.45.refs_1_, f32[64,1024]{1,0:T(8,128)} %collective-permute-done.refs_2_, bf16[256,256]{1,0:T(8,128)(2,1)} %constant.173.clone.refs_4_.refs_2_.refs_3_.refs_12_, ...), custom_call_target="tpu_custom_call" | custom-call | tf_op jit(solution)/shard_map/join/pallas_call | solution.py:911
  176.2 4.4 %all-to-all-start.1 = ((f32[16,2,64,256]{3,2,1,0:T(8,128)}), f32[16,2,64,256]{3,2,1,0:T(8,128)}, u32[]{:S(2)}, u32[]{:S(2)}) async-start(f32[16,2,64,256]{3,2,1,0:T(8,128)} %join.1), calls=%async_computation.1 | async-start | bytes 4194304 | tf_op jit(solution)/shard_map/all_to_all | solution.py:931
  180.7 14.5 %theta.1 = bf16[4096,1024]{1,0:T(8,128)(2,1)} custom-call(s32[3,1024]{1,0:T(4,128)} %pad_add_fusion.refs_0_.ids_ref, f32[1024]{0:T(1024)} %bitcast_add_fusion.new_ref, bf16[4096,1024]{1,0:T(8,128)(2,1)} %bitcast.44), custom_call_target="tpu_custom_call" | custom-call | flops 4194304 | bytes 33554432 | tf_op jit(solution)/shard_map/theta/pallas_call | solution.py:921
  195.2 13.5 %all-to-all-done.1.refs_0_ = f32[16,2,64,256]{3,2,1,0:T(8,128)} async-done(((f32[16,2,64,256]{3,2,1,0:T(8,128)}), f32[16,2,64,256]{3,2,1,0:T(8,128)}, u32[]{:S(2)}, u32[]{:S(2)}) %all-to-all-start.1) | async-done | bytes 2097184 | tf_op jit(solution)/shard_map/all_to_all | solution.py:931
  208.6 1.2 copy-done.6
  209.9 7.1 %spread.1 = (f32[2,256,1024]{2,1,0:T(8,128)S(1)}, f32[2,16,1024]{2,1,0:T(8,128)S(1)}) custom-call(f32[16,2,64,256]{3,2,1,0:T(8,128)} %all-to-all-done.1.refs_0_, bf16[256,256]{1,0:T(8,128)(2,1)S(1)} %copy-done.12, bf16[256,256]{1,0:T(8,128)(2,1)S(1)} %copy-done.11, f32[256,1024]{1,0:T(8,128)S(1)} %copy-done, f32[256,1024]{1,0:T(8,128)S(1)} %copy-done.1, ...), custom_call_target="tpu_custom_call" | custom-call | tf_op jit(solution)/shard_map/spread/pallas_call | solution.py:932
  216.9 1.3 copy-done.9
  218.2 9.0 %all-gather.1 = f32[8,16,1024]{2,1,0:T(8,128)} all-gather(f32[2,16,1024]{2,1,0:T(8,128)S(1)} %get-tuple-element.55), channel_id=3, replica_groups=mesh['px'=4,'py_half'=2,'py_low'=4] {'px'}, dimensions={0}, use_global_device_ids=true | all-gather | bytes 655360 | tf_op jit(solution)/shard_map/all_gather | solution.py:941
  227.2 38.0 %inverse.1 = f32[16,256,1024]{2,1,0:T(8,128)} custom-call(s32[1]{0:T(128)} %bitcast.refs_0_, f32[16,256,1024]{2,1,0:T(8,128)} %get-tuple-element.37.refs_1_, f32[2,256,1024]{2,1,0:T(8,128)} %copy-done.9, f32[4,2,16,1024]{3,2,1,0:T(8,128)} %bitcast.39, f32[4,2,16,1024]{3,2,1,0:T(8,128)} %bitcast.47, f32[2,4,16,1024]{3,2,1,0:T(8,128)} %copy-done.5, ...), custom_call_target="tpu_custom_call" | custom-call | tf_op jit(solution)/shard_map/inverse/pallas_call | solution.py:946
  265.3 0.6 copy.49
  (32 shorter events, 0.1 us)
Async XLA Ops:
  5.8 34.9 %copy-start.15 = (s32[1,1024]{1,0:T(1,128)S(1)}, s32[1,1024]{1,0:T(1,128)}, u32[]{:S(2)}) copy-start(s32[1,1024]{1,0:T(1,128)} %param.42) | copy-start | bytes 12292
  42.5 57.3 %copy-start.14 = (f32[4,4]{1,0:T(4,128)S(1)}, f32[4,4]{1,0:T(4,128)}, u32[]{:S(2)}) copy-start(f32[4,4]{1,0:T(4,128)} %constant.192.clone) | copy-start | bytes 196
  42.5 59.9 %copy-start = (f32[256,1024]{1,0:T(8,128)S(1)}, f32[256,1024]{1,0:T(8,128)}, u32[]{:S(2)}) copy-start(f32[256,1024]{1,0:T(8,128)} %get-tuple-element.33.refs_12_.refs_4_.refs_3_.refs_7_) | copy-start | bytes 3145732
  42.5 59.9 %copy-start.1 = (f32[256,1024]{1,0:T(8,128)S(1)}, f32[256,1024]{1,0:T(8,128)}, u32[]{:S(2)}) copy-start(f32[256,1024]{1,0:T(8,128)} %get-tuple-element.35.refs_14_.refs_6_.refs_4_.refs_8_) | copy-start | bytes 3145732
  42.5 60.0 %copy-start.2 = (f32[256,1024]{1,0:T(8,128)S(1)}, f32[256,1024]{1,0:T(8,128)}, u32[]{:S(2)}) copy-start(f32[256,1024]{1,0:T(8,128)} %get-tuple-element.36.refs_15_.refs_7_.refs_6_.refs_10_) | copy-start | bytes 3145732
  42.5 60.0 %copy-start.8 = (f32[256,128]{1,0:T(8,128)S(1)}, f32[256,128]{1,0:T(8,128)}, u32[]{:S(2)}) copy-start(f32[256,128]{1,0:T(8,128)} %constant.185.clone.refs_16_.refs_8_.refs_7_.refs_11_) | copy-start | bytes 393220
  42.5 60.0 %copy-start.11 = (bf16[256,256]{1,0:T(8,128)(2,1)S(1)}, bf16[256,256]{1,0:T(8,128)(2,1)}, u32[]{:S(2)}) copy-start(bf16[256,256]{1,0:T(8,128)(2,1)} %constant.180.clone.refs_11_.refs_10_.refs_2_) | copy-start | bytes 393220
  42.5 60.0 %copy-start.12 = (bf16[256,256]{1,0:T(8,128)(2,1)S(1)}, bf16[256,256]{1,0:T(8,128)(2,1)}, u32[]{:S(2)}) copy-start(bf16[256,256]{1,0:T(8,128)(2,1)} %constant.179.clone.refs_10_.refs_9_.refs_1_) | copy-start | bytes 393220
  101.6 10.0 %copy-start.5 = (f32[2,4,16,1024]{3,2,1,0:T(8,128)}, f32[2,4,16,1024]{3,2,1,0:T(8,128)S(1)}, u32[]{:S(2)}) copy-start(f32[2,4,16,1024]{3,2,1,0:T(8,128)S(1)} %multiply_reduce_fusion.refs_2_.refs_5_) | copy-start | bytes 1572868
  102.5 9.2 %copy-start.13 = (f32[16,16]{1,0:T(8,128)}, f32[16,16]{1,0:T(8,128)S(1)}, u32[]{:S(2)}) copy-start(f32[16,16]{1,0:T(8,128)S(1)} %select_select_fusion.refs_3_.refs_6_) | copy-start | bytes 3076
  102.5 1.0 copy-start.4
  103.6 1.2 copy-start.7
  104.8 1.6 copy-start.10
  111.6 1.3 copy-start.3
  112.9 4.8 %copy-start.16 = (f32[1024]{0:T(1024)S(1)}, f32[1024]{0:T(1024)}, u32[]{:S(2)}) copy-start(f32[1024]{0:T(1024)} %constant.183.clone) | copy-start | bytes 12292
  112.9 32.5 %all-to-all-start = ((f32[16,2,64,256]{3,2,1,0:T(8,128)}), f32[16,2,64,256]{3,2,1,0:T(8,128)}, u32[]{:S(2)}, u32[]{:S(2)}) async-start(f32[16,2,64,256]{3,2,1,0:T(8,128)} %copy-done.3), calls=%async_computation | async-start | bytes 4194304 | tf_op jit(solution)/shard_map/all_to_all | solution.py:891
  117.8 12.9 %copy-start.18 = (f32[3,8,128]{2,1,0:T(8,128)S(1)}, f32[3,8,128]{2,1,0:T(8,128)}, u32[]{:S(2)}) copy-start(f32[3,8,128]{2,1,0:T(8,128)} %get-tuple-element.32) | copy-start | bytes 36868
  151.4 18.3 %collective-permute-start = (f32[64,1024]{1,0:T(8,128)}, f32[64,1024]{1,0:T(8,128)}, u32[]{:S(2)}, u32[]{:S(2)}) collective-permute-start(f32[64,1024]{1,0:T(8,128)} %get-tuple-element.47), channel_id=1, source_target_pairs={{0,4},{4,0},{1,5},{5,1},{2,6},{6,2},{3,7},{7,3},{8,12},{12,8},{9,1... | collective-permute-start | bytes 786440 | tf_op jit(solution)/shard_map/ppermute | solution.py:909
  176.2 32.4 %all-to-all-start.1 = ((f32[16,2,64,256]{3,2,1,0:T(8,128)}), f32[16,2,64,256]{3,2,1,0:T(8,128)}, u32[]{:S(2)}, u32[]{:S(2)}) async-start(f32[16,2,64,256]{3,2,1,0:T(8,128)} %join.1), calls=%async_computation.1 | async-start | bytes 4194304 | tf_op jit(solution)/shard_map/all_to_all | solution.py:931
  208.6 1.2 copy-start.6
  216.9 1.3 copy-start.9
  227.2 38.1 %copy-start.17 = (f32[8,128]{1,0:T(8,128)S(1)}, f32[8,128]{1,0:T(8,128)}, u32[]{:S(2)}) copy-start(f32[8,128]{1,0:T(8,128)} %facet_temp.1) | copy-start | bytes 12292

commit v9 on v8

--- a/solution.py
+++ b/solution.py
@@ -882,7 +882,7 @@
         in_specs=[VMEM] * 11,
         out_specs=VMEM,
         scratch_shapes=working + [pltpu.VMEM((2, rows, width), F32)],
-        compiler_params=SMALL,
+        compiler_params=PARAMS,
         name="edges",
     )(edges, all_ends, weights, vectors, root, inv, start, top, end, *to_modes)
     w_cell, edges = lax.optimization_barrier((w_cell, edges))

time: 267 us -> 266 us (level)
  Pallas kernels: 191 us -> 195 us
  local copies, waits for them, and re-layouts: 9.74 us -> 6.59 us
    pallas_call x1, Pallas kernels: 5.22 us -> 9.8 us  [body(): pl.pallas_call(lambda *refs: edge_kernel(levels, *refs), out_shape=packed...]
    unnamed x39 -> x37, local copies, waits for them, and re-layouts: 8.34 us -> 5.2 us
where the time goes in v9:
time: 266 us; the launch traced here: 265 us
  Pallas kernels  195 us (73%)
  waiting for transfers between devices  24.5 us (9%)
  blocking collectives  17.4 us (7%)
  other arithmetic  11.3 us (4%)
  starting transfers between devices  9.01 us (3%)
  local copies, waits for them, and re-layouts  6.59 us (2%)
    pallas_call x1, Pallas kernels, body(): pl.pallas_call(lambda *refs: forward_kernel(levels, tile, *refs), out_sha...  48.2 us
    pallas_call x1, Pallas kernels, body(): pl.pallas_call(lambda *refs: inverse_kernel(levels, tile, *refs), out_sha...  38 us
    pallas_call x1, Pallas kernels, near_walls(): pl.pallas_call(lambda *refs: stress_kernel(sizes, slots, *refs), out_shap...  19.3 us
    pallas_call x1, Pallas kernels, warm_facets(): pl.pallas_call(lambda *refs: facet_temp_kernel(sizes, slots, *refs), out_...  17.8 us
    pallas_call x1, Pallas kernels, near_walls(): pl.pallas_call(lambda *refs: gather_kernel(w_rows.shape[0] // rows, *refs...  14.9 us
    pallas_call x1, Pallas kernels, body(): pl.pallas_call(theta_kernel, out_shape=jax.ShapeDtypeStruct(temp_rows.sha...  14.6 us
    all_to_all x1, waiting for transfers between devices, body(): lax.all_to_all(joined, ('px', 'py_low'), split_axis=0, concat_axis=0, til...  13.3 us
    pallas_call x1, Pallas kernels, warm_air(): pl.pallas_call(gather_temp_kernel, out_shape=jax.ShapeDtypeStruct(flat, F...  12.9 us
  transfers between devices with their start and end apart: 3, of which 2 were waited for; matrix products, arithmetic and copies ran while one was open for 1% of the time, Pallas kernels for 17%

profile of v9, /device:TPU:0, one launch (start us, length us, event | category | flops | bytes accessed | tf_op | source)
XLA Modules:
  0.0 264.8 jit_solution(9074891799582116609)
XLA Ops:
  0.7 0.1 reshape.396
  0.8 0.8 and_select_fusion.4
  1.5 0.7 compare_select_fusion.2
  2.3 0.7 broadcast_select_fusion.1
  3.0 0.9 add_divide_fusion.3
  3.9 0.6 add_convert_fusion.refs_1_
  4.5 0.6 pad_add_fusion.refs_0_.ids_ref
  5.1 14.9 %facet_gather.1 = (f32[8,128]{1,0:T(8,128)}, f32[256,1024]{1,0:T(8,128)}, f32[256,1024]{1,0:T(8,128)}, f32[256,1024]{1,0:T(8,128)}, f32[256,1024]{1,0:T(8,128)}, /*index=5*/f32[256,1024]{1,0:T(8,128)}) custom-call(s32[3,1024]{1,0:T(4,128)} %pad_add_fusion.refs_0_.ids_ref, s32[2]{0:T(128)} %add_convert_fusion.refs_1_, f32[4096,1024]{1,0:T(8,128)} %bitcast.39, ...), custom_call_target="tpu_custom_call" | custom-call | tf_op jit(solution)/shard_map/facet_gather/pallas_call | solution.py:697
  20.0 19.3 %stress_exchange.1 = (f32[3,8,128]{2,1,0:T(8,128)}, f32[4,8,128]{2,1,0:T(8,128)}) custom-call(f32[8,128]{1,0:T(8,128)} %get-tuple-element.31.refs_0_, f32[8,128]{1,0:T(8,128)} %bitcast.52, f32[8,128]{1,0:T(8,128)} %bitcast.58, f32[8,128]{1,0:T(8,128)} %bitcast.54), custom_call_target="tpu_custom_call" | custom-call | tf_op jit(solution)/shard_map/stress_exchange/pallas_call | solution.py:714
  39.3 0.7 slice_bitcast_fusion
  40.0 0.5 fusion
  40.5 1.3 bitcast_subtract_fusion.1.refs_1_
  41.8 48.2 %forward.1 = (f32[16,256,1024]{2,1,0:T(8,128)}, f32[2,256,1024]{2,1,0:T(8,128)}, f32[2,16,1024]{2,1,0:T(8,128)}, f32[4096,1024]{1,0:T(8,128)}) custom-call(s32[3,1024]{1,0:T(4,128)} %pad_add_fusion.refs_0_.ids_ref, f32[1024]{0:T(1024)} %bitcast_subtract_fusion.1.refs_1_, f32[4096,1024]{1,0:T(8,128)} %bitcast.40, f32[16,256,1024]{2,1,0:T(8,128)} %refs_3_.3, ...), custom_call_target="tpu_custom_call" | custom-call | tf_op jit(solution)/shard_map/forward/pallas_call | solution.py:846
  90.0 8.4 %all-gather = f32[8,16,1024]{2,1,0:T(8,128)} all-gather(f32[2,16,1024]{2,1,0:T(8,128)} %get-tuple-element.40), channel_id=2, replica_groups=mesh['px'=4,'py_half'=2,'py_low'=4] {'px'}, dimensions={0}, use_global_device_ids=true | all-gather | bytes 655360 | tf_op jit(solution)/shard_map/all_gather | solution.py:876
  98.4 0.6 gather_fusion
  99.0 1.1 multiply_reduce_fusion.refs_2_.refs_5_
  100.0 0.0 copy-done.16
  100.0 0.6 select_select_fusion.refs_3_.refs_6_
  100.6 9.8 %edges.1 = f32[16,2,64,256]{3,2,1,0:T(8,128)} custom-call(f32[2,256,1024]{2,1,0:T(8,128)} %get-tuple-element.39.refs_0_, f32[4,2,16,1024]{3,2,1,0:T(8,128)} %bitcast.45, f32[2,4,16,1024]{3,2,1,0:T(8,128)} %multiply_reduce_fusion.refs_2_.refs_5_, f32[16,16]{1,0:T(8,128)} %select_select_fusion.refs_3_.refs_6_, ...), custom_call_target="tpu_custom_call" | custom-call | tf_op jit(solution)/shard_map/edges/pallas_call | solution.py:879
  110.5 4.0 %all-to-all-start = ((f32[16,2,64,256]{3,2,1,0:T(8,128)}), f32[16,2,64,256]{3,2,1,0:T(8,128)S(1)}, u32[]{:S(2)}, u32[]{:S(2)}) async-start(f32[16,2,64,256]{3,2,1,0:T(8,128)} %edges.1), calls=%async_computation | async-start | bytes 4194304 | tf_op jit(solution)/shard_map/all_to_all | solution.py:891
  114.5 0.1 dynamic_slice.3
  114.6 12.9 %temp_gather.1.refs_0_ = f32[8,128]{1,0:T(8,128)} custom-call(s32[3,1024]{1,0:T(4,128)} %pad_add_fusion.refs_0_.ids_ref, bf16[4096,1024]{1,0:T(8,128)(2,1)} %bitcast.41), custom_call_target="tpu_custom_call" | custom-call | bytes 16777216 | tf_op jit(solution)/shard_map/temp_gather/pallas_call | solution.py:730
  127.5 0.7 fusion.7
  128.2 0.5 fusion.1
  128.8 1.3 bitcast_add_fusion.new_ref
  130.0 1.0 subtract_multiply_fusion.refs_8_.refs_9_
  131.0 11.2 %all-to-all-done.refs_1_ = f32[16,2,64,256]{3,2,1,0:T(8,128)S(1)} async-done(((f32[16,2,64,256]{3,2,1,0:T(8,128)}), f32[16,2,64,256]{3,2,1,0:T(8,128)S(1)}, u32[]{:S(2)}, u32[]{:S(2)}) %all-to-all-start) | async-done | bytes 2097184 | tf_op jit(solution)/shard_map/all_to_all | solution.py:891
  142.2 1.3 copy-done.8
  143.5 6.0 %gather_modes.1 = (f32[4,2,64,1024]{3,2,1,0:T(8,128)}, f32[64,1024]{1,0:T(8,128)}) custom-call(s32[1]{0:T(128)} %bitcast.10.refs_0_, f32[16,2,64,256]{3,2,1,0:T(8,128)} %copy-done.8, bf16[256,256]{1,0:T(8,128)(2,1)} %constant.173.clone.refs_4_.refs_2_.refs_3_.refs_12_, bf16[256,256]{1,0:T(8,128)(2,1)} %constant.174.clone.refs_5_.refs_3_.refs_4_.refs_13_, ...), custom_call_target="tpu_custom_call" | custom-call | tf_op jit(solution)/shard_map/gather_modes/pallas_call | solution.py:894
  149.5 0.5 collective-permute-start
  150.0 17.8 %facet_temp.1 = f32[8,128]{1,0:T(8,128)} custom-call(f32[8,128]{1,0:T(8,128)} %temp_gather.1.refs_0_, f32[8,128]{1,0:T(8,128)} %bitcast.53, f32[8,128]{1,0:T(8,128)} %bitcast.56, f32[8,128]{1,0:T(8,128)} %bitcast.57, f32[8,128]{1,0:T(8,128)} %bitcast.55, f32[4,8,128]{2,1,0:T(8,128)} %get-tuple-element.49.refs_5_), custom_call_target="tpu_custom_call" | custom-call | bytes 16777216 | tf_op jit(solution)/shard_map/facet_temp/pallas_call | solution.py:749
  167.8 0.0 collective-permute-done.refs_2_
  167.8 0.0 copy-start.10
  167.9 0.7 copy-done.10
  168.6 6.5 %join.1 = f32[16,2,64,256]{3,2,1,0:T(8,128)} custom-call(s32[1]{0:T(128)} %bitcast.10.refs_0_, f32[4,2,64,1024]{3,2,1,0:T(8,128)} %get-tuple-element.45.refs_1_, f32[64,1024]{1,0:T(8,128)} %copy-done.10, bf16[256,256]{1,0:T(8,128)(2,1)} %constant.173.clone.refs_4_.refs_2_.refs_3_.refs_12_, bf16[256,256]{1,0:T(8,128)(2,1)} %constant.174.clone.refs_5_.refs_3_.refs_4_.refs_13_, ...), custom_call_target="tpu_custom_call" | custom-call | tf_op jit(solution)/shard_map/join/pallas_call | solution.py:911
  175.1 4.4 %all-to-all-start.1 = ((f32[16,2,64,256]{3,2,1,0:T(8,128)}), f32[16,2,64,256]{3,2,1,0:T(8,128)}, u32[]{:S(2)}, u32[]{:S(2)}) async-start(f32[16,2,64,256]{3,2,1,0:T(8,128)} %join.1), calls=%async_computation.1 | async-start | bytes 4194304 | tf_op jit(solution)/shard_map/all_to_all | solution.py:931
  179.6 0.0 copy-start.4
  179.6 0.0 copy-start.6
  179.6 0.0 copy-start.7
  179.6 14.6 %theta.1 = bf16[4096,1024]{1,0:T(8,128)(2,1)} custom-call(s32[3,1024]{1,0:T(4,128)} %pad_add_fusion.refs_0_.ids_ref, f32[1024]{0:T(1024)} %bitcast_add_fusion.new_ref, bf16[4096,1024]{1,0:T(8,128)(2,1)} %bitcast.42), custom_call_target="tpu_custom_call" | custom-call | flops 4194304 | bytes 33554432 | tf_op jit(solution)/shard_map/theta/pallas_call | solution.py:921
  194.2 13.3 %all-to-all-done.1.refs_0_ = f32[16,2,64,256]{3,2,1,0:T(8,128)} async-done(((f32[16,2,64,256]{3,2,1,0:T(8,128)}), f32[16,2,64,256]{3,2,1,0:T(8,128)}, u32[]{:S(2)}, u32[]{:S(2)}) %all-to-all-start.1) | async-done | bytes 2097184 | tf_op jit(solution)/shard_map/all_to_all | solution.py:931
  207.5 0.0 copy-done.1
  207.5 1.2 copy-done.3
  208.8 7.1 %spread.1 = (f32[2,256,1024]{2,1,0:T(8,128)S(1)}, f32[2,16,1024]{2,1,0:T(8,128)S(1)}) custom-call(f32[16,2,64,256]{3,2,1,0:T(8,128)} %all-to-all-done.1.refs_0_, bf16[256,256]{1,0:T(8,128)(2,1)S(1)} %copy-done.7, bf16[256,256]{1,0:T(8,128)(2,1)S(1)} %copy-done.6, f32[256,1024]{1,0:T(8,128)S(1)} %copy-done, f32[256,1024]{1,0:T(8,128)S(1)} %copy-done.1, ...), custom_call_target="tpu_custom_call" | custom-call | tf_op jit(solution)/shard_map/spread/pallas_call | solution.py:932
  215.8 1.3 copy-done.5
  217.1 9.0 %all-gather.1 = f32[8,16,1024]{2,1,0:T(8,128)} all-gather(f32[2,16,1024]{2,1,0:T(8,128)S(1)} %get-tuple-element.55), channel_id=3, replica_groups=mesh['px'=4,'py_half'=2,'py_low'=4] {'px'}, dimensions={0}, use_global_device_ids=true | all-gather | bytes 655360 | tf_op jit(solution)/shard_map/all_gather | solution.py:941
  226.1 38.0 %inverse.1 = f32[16,256,1024]{2,1,0:T(8,128)} custom-call(s32[1]{0:T(128)} %bitcast.refs_0_, f32[16,256,1024]{2,1,0:T(8,128)} %get-tuple-element.37.refs_1_, f32[2,256,1024]{2,1,0:T(8,128)} %copy-done.5, f32[4,2,16,1024]{3,2,1,0:T(8,128)} %bitcast.46, f32[4,2,16,1024]{3,2,1,0:T(8,128)} %bitcast.47, f32[2,4,16,1024]{3,2,1,0:T(8,128)} %multiply_reduce_fusion.refs_2_.refs_5_, ...), custom_call_target="tpu_custom_call" | custom-call | tf_op jit(solution)/shard_map/inverse/pallas_call | solution.py:946
  264.2 0.6 copy.49
  (30 shorter events, 0.1 us)
Async XLA Ops:
  5.1 34.9 %copy-start.11 = (s32[1,1024]{1,0:T(1,128)S(1)}, s32[1,1024]{1,0:T(1,128)}, u32[]{:S(2)}) copy-start(s32[1,1024]{1,0:T(1,128)} %param.42) | copy-start | bytes 12292
  41.8 56.6 %copy-start.9 = (f32[4,4]{1,0:T(4,128)S(1)}, f32[4,4]{1,0:T(4,128)}, u32[]{:S(2)}) copy-start(f32[4,4]{1,0:T(4,128)} %constant.192.clone) | copy-start | bytes 196
  41.8 58.2 %copy-start.15 = (f32[16,16]{1,0:T(8,128)S(1)}, f32[16,16]{1,0:T(8,128)}, u32[]{:S(2)}) copy-start(f32[16,16]{1,0:T(8,128)} %constant.188.clone) | copy-start | bytes 3076
  41.8 58.2 %copy-start.16 = (f32[16,16]{1,0:T(8,128)S(1)}, f32[16,16]{1,0:T(8,128)}, u32[]{:S(2)}) copy-start(f32[16,16]{1,0:T(8,128)} %constant.187.clone) | copy-start | bytes 3076
  41.8 58.2 %copy-start.17 = (f32[16,16]{1,0:T(8,128)S(1)}, f32[16,16]{1,0:T(8,128)}, u32[]{:S(2)}) copy-start(f32[16,16]{1,0:T(8,128)} %constant.186.clone) | copy-start | bytes 3076
  110.5 4.1 %copy-start.12 = (f32[1024]{0:T(1024)S(1)}, f32[1024]{0:T(1024)}, u32[]{:S(2)}) copy-start(f32[1024]{0:T(1024)} %constant.183.clone) | copy-start | bytes 12292
  110.5 31.8 %all-to-all-start = ((f32[16,2,64,256]{3,2,1,0:T(8,128)}), f32[16,2,64,256]{3,2,1,0:T(8,128)S(1)}, u32[]{:S(2)}, u32[]{:S(2)}) async-start(f32[16,2,64,256]{3,2,1,0:T(8,128)} %edges.1), calls=%async_computation | async-start | bytes 4194304 | tf_op jit(solution)/shard_map/all_to_all | solution.py:891
  114.6 12.9 %copy-start.14 = (f32[3,8,128]{2,1,0:T(8,128)S(1)}, f32[3,8,128]{2,1,0:T(8,128)}, u32[]{:S(2)}) copy-start(f32[3,8,128]{2,1,0:T(8,128)} %get-tuple-element.32) | copy-start | bytes 36868
  142.2 1.3 copy-start.8
  149.5 18.4 %collective-permute-start = (f32[64,1024]{1,0:T(8,128)}, f32[64,1024]{1,0:T(8,128)S(1)}, u32[]{:S(2)}, u32[]{:S(2)}) collective-permute-start(f32[64,1024]{1,0:T(8,128)} %get-tuple-element.47), channel_id=1, source_target_pairs={{0,4},{4,0},{1,5},{5,1},{2,6},{6,2},{3,7},{7,3},{8,12},{12,8},{9,1... | collective-permute-start | bytes 786440 | tf_op jit(solution)/shard_map/ppermute | solution.py:909
  167.8 0.7 copy-start.10
  175.1 32.4 %all-to-all-start.1 = ((f32[16,2,64,256]{3,2,1,0:T(8,128)}), f32[16,2,64,256]{3,2,1,0:T(8,128)}, u32[]{:S(2)}, u32[]{:S(2)}) async-start(f32[16,2,64,256]{3,2,1,0:T(8,128)} %join.1), calls=%async_computation.1 | async-start | bytes 4194304 | tf_op jit(solution)/shard_map/all_to_all | solution.py:931
  179.6 27.9 %copy-start = (f32[256,1024]{1,0:T(8,128)S(1)}, f32[256,1024]{1,0:T(8,128)}, u32[]{:S(2)}) copy-start(f32[256,1024]{1,0:T(8,128)} %get-tuple-element.33.refs_12_.refs_4_.refs_3_.refs_7_) | copy-start | bytes 3145732
  179.6 27.9 %copy-start.1 = (f32[256,1024]{1,0:T(8,128)S(1)}, f32[256,1024]{1,0:T(8,128)}, u32[]{:S(2)}) copy-start(f32[256,1024]{1,0:T(8,128)} %get-tuple-element.35.refs_14_.refs_6_.refs_4_.refs_8_) | copy-start | bytes 3145732
  179.6 27.9 %copy-start.2 = (f32[256,1024]{1,0:T(8,128)S(1)}, f32[256,1024]{1,0:T(8,128)}, u32[]{:S(2)}) copy-start(f32[256,1024]{1,0:T(8,128)} %get-tuple-element.36.refs_15_.refs_7_.refs_6_.refs_10_) | copy-start | bytes 3145732
  179.6 27.9 %copy-start.4 = (f32[256,128]{1,0:T(8,128)S(1)}, f32[256,128]{1,0:T(8,128)}, u32[]{:S(2)}) copy-start(f32[256,128]{1,0:T(8,128)} %constant.185.clone.refs_16_.refs_8_.refs_7_.refs_11_) | copy-start | bytes 393220
  179.6 27.9 %copy-start.6 = (bf16[256,256]{1,0:T(8,128)(2,1)S(1)}, bf16[256,256]{1,0:T(8,128)(2,1)}, u32[]{:S(2)}) copy-start(bf16[256,256]{1,0:T(8,128)(2,1)} %constant.180.clone.refs_11_.refs_10_.refs_2_) | copy-start | bytes 393220
  179.6 27.9 %copy-start.7 = (bf16[256,256]{1,0:T(8,128)(2,1)S(1)}, bf16[256,256]{1,0:T(8,128)(2,1)}, u32[]{:S(2)}) copy-start(bf16[256,256]{1,0:T(8,128)(2,1)} %constant.179.clone.refs_10_.refs_9_.refs_1_) | copy-start | bytes 393220
  207.5 1.2 copy-start.3
  215.8 1.3 copy-start.5
  226.1 38.1 %copy-start.13 = (f32[8,128]{1,0:T(8,128)S(1)}, f32[8,128]{1,0:T(8,128)}, u32[]{:S(2)}) copy-start(f32[8,128]{1,0:T(8,128)} %facet_temp.1) | copy-start | bytes 12292
